TPU v7x, 32 devices: a whole 2x2x4 slice. The times are simulated.
32 devices in a mesh: group: 2 (over x), tile: 16 (over z, y, core).
Axes of the slice: x: 2, y: 2, z: 4, core: 2. Of those that a mesh axis runs over, the one named last changes fastest.
Arguments:
- object_field: float32 [4, 2, 2048, 2048], P('group', None, 'tile'), parts along dimension 0, may hold values from -6 to 6
- probe: float32 [2, 256, 256], replicated, may hold values from -6 to 6
- measured: bfloat16 [64, 256, 256], P(('group', 'tile')), parts along dimension 0, may hold values from 0.099609375 to 3
- frame_table: int32 [64, 3], P(('group', 'tile')), parts along dimension 0, may hold values from 0 to 1792, as said below
- frame_count: int32 [32], P(('group', 'tile')), parts along dimension 0, may hold values from 0 to 2, as said below
Outputs:
- updated_object: float32 [4, 2, 2048, 2048], P('group', None, 'tile'), parts along dimension 0
- phase_map: float32 [4, 2048, 2048], P('group', 'tile'), parts along dimension 0
There are 2 independent parts, one for each index of `group`. A program takes and returns all parts, laid end to end along the dimension named above; an argument that names none is the same for every part. Nothing has to cross between parts.
Inputs may be any that keep to these rules, and one draw needn't show every extreme that they name: `frame_table`: per slot: the row offset is below 128, and the frame's rows d * 128 + offset to that plus 256 - 1 and columns lie inside the projection; the angle is below 2. Only the first frame_count[d] slots of device d are live. `frame_count`: exactly 2 on some device in every draw; zero on every device d with d * 128 > 1792.
All inputs are finite; a program needn't handle non-finite values.
Results may differ from a plain program's by a relative error of at most 0.0009.
Values may be sent and summed in bfloat16 or wider, within the bound.
A program may use at most 192 MiB of HBM per device.

v0:
```python
import functools
import math

import numpy as np
import jax
import jax.numpy as jnp
from jax import lax
from jax.experimental import pallas as pl
from jax.experimental.pallas import tpu as pltpu
from jax.sharding import PartitionSpec as P

magnitude_floor = 0.5
soften_term = 0.5
screen_term = 0.0001
epsilon_term = 1e-06
f32 = jnp.float32
bf16 = jnp.bfloat16
LANES = 128
GROUP = 8
TILE = 256
VMEM_BYTES = 30 * 1024 * 1024
MESH = pl.DeviceIdType.MESH
vmem = pl.BlockSpec(memory_space=pltpu.VMEM)
smem = pl.BlockSpec(memory_space=pltpu.SMEM)
hbm = pl.BlockSpec(memory_space=pltpu.HBM)


def cost(micros):
    return pl.CostEstimate(
        flops=0, bytes_accessed=int(micros * 3_000_000), transcendentals=0
    )


def params(**more):
    return pltpu.CompilerParams(vmem_limit_bytes=VMEM_BYTES, **more)


def exchange_kernel(moves, keep, work, arrays, inputs, *refs):
    sources, given = refs[:arrays], refs[arrays : arrays + inputs]
    outs = refs[arrays + inputs : 2 * arrays + inputs]
    made = refs[2 * arrays + inputs : -2]
    send_sems, recv_sems = refs[-2:]
    count = lax.axis_size("tile")
    me = lax.axis_index("tile")
    barrier = pltpu.get_barrier_semaphore()
    met = jnp.zeros((), jnp.int32)
    for by in sorted({sign * by for *_, by in moves for sign in (1, -1)}):
        there = (me + by >= 0) & (me + by < count)

        @pl.when(there)
        def _():
            pl.semaphore_signal(
                barrier, inc=1, device_id={"tile": me + by}, device_id_type=MESH
            )

        met = met + jnp.where(there, 1, 0)
    pl.semaphore_wait(barrier, met)
    copies = []
    for index, (array, first, last, by) in enumerate(moves):
        copy = pltpu.make_async_remote_copy(
            src_ref=sources[array].at[first],
            dst_ref=outs[array].at[last],
            send_sem=send_sems.at[index],
            recv_sem=recv_sems.at[index],
            device_id={"tile": me + by},
            device_id_type=MESH,
        )
        sends = (me + by >= 0) & (me + by < count)
        takes = (me - by >= 0) & (me - by < count)
        copies.append((copy, sends, takes, outs[array], last))
        pl.when(sends)(copy.start)
    if work is not None:
        work(*given, *made)
    for array, first, last in keep:
        outs[array][last] = sources[array][first]
    for copy, sends, takes, out, last in copies:

        @pl.when(jnp.logical_not(takes))
        def _():
            out[last] = jnp.zeros(out.shape[1:], out.dtype)

    for copy, sends, takes, out, last in copies:
        pl.when(takes)(copy.wait_recv)
        pl.when(sends)(copy.wait_send)


def exchanged(sources, slots, moves, keep, number, name, work=None, given=(), made=()):
    return pl.pallas_call(
        functools.partial(exchange_kernel, moves, keep, work, len(sources), len(given)),
        out_shape=[
            jax.ShapeDtypeStruct((slot,) + source.shape[1:], source.dtype)
            for slot, source in zip(slots, sources)
        ]
        + list(made),
        in_specs=[vmem] * (len(sources) + len(given)),
        out_specs=[vmem] * (len(sources) + len(made)),
        scratch_shapes=[pltpu.SemaphoreType.DMA((len(moves),))] * 2,
        compiler_params=params(collective_id=number, has_side_effects=True),
        cost_estimate=cost(4),
        name=name,
    )(*sources, *given)


def join_kernel(ends, powers, extra, out, heard, told, up_sems, in_sems, down_sems, back_sems):
    count = lax.axis_size("tile")
    me = lax.axis_index("tile")
    blocks, lines = ends.shape[0], ends.shape[1]
    angles = lines // 2
    stride = count // blocks
    mine = me // stride
    joins = lax.rem(me, stride) == 0
    barrier = pltpu.get_barrier_semaphore()

    def greet(by, _):
        pl.semaphore_signal(
            barrier, inc=1, device_id={"tile": lax.rem(me + by, count)}, device_id_type=MESH
        )
        return 0

    lax.fori_loop(1, count, greet, 0)
    pl.semaphore_wait(barrier, count - 1)

    def up(by):
        block = lax.rem(mine + by, blocks)
        return pltpu.make_async_remote_copy(
            src_ref=ends.at[block],
            dst_ref=heard.at[me],
            send_sem=up_sems.at[block],
            recv_sem=in_sems.at[me],
            device_id={"tile": block * stride},
            device_id_type=MESH,
        )

    def came(other):
        return pltpu.make_async_remote_copy(
            src_ref=ends.at[0],
            dst_ref=heard.at[other],
            send_sem=up_sems.at[0],
            recv_sem=in_sems.at[other],
            device_id={"tile": other},
            device_id_type=MESH,
        )

    def down(other):
        return pltpu.make_async_remote_copy(
            src_ref=told.at[other],
            dst_ref=out.at[mine],
            send_sem=down_sems.at[other],
            recv_sem=back_sems.at[mine],
            device_id={"tile": other},
            device_id_type=MESH,
        )

    def answered(block):
        return pltpu.make_async_remote_copy(
            src_ref=told.at[0],
            dst_ref=out.at[block],
            send_sem=down_sems.at[0],
            recv_sem=back_sems.at[block],
            device_id={"tile": block * stride},
            device_id_type=MESH,
        )

    def each(limit, step):
        def run(index, _):
            step(index)
            return 0

        lax.fori_loop(0, limit, run, 0)

    for by in range(blocks):
        pl.when(lax.rem(mine + by, blocks) * stride != me)(lambda: up(by).start())

    @pl.when(joins)
    def _():
        heard[me] = ends[mine]
        for by in range(1, count):
            came(lax.rem(me + by, count)).wait_recv()
        step = powers[mine, 1:2]
        whole = powers[mine, count : count + 1]
        closing = extra[mine, 1:2]
        gain = extra[mine, 0:1]
        wall = heard[count - 1, angles:]
        floor = heard[0, :angles]
        for strip in range(1, count):
            floor = floor * step + heard[strip, :angles]
            wall = wall * step + heard[count - 1 - strip, angles:]
        enter = (wall + whole * floor) * closing
        leave = (floor + whole * wall) * closing
        for strip in range(count):
            told[strip, :angles] = enter * gain
            enter = enter * step + heard[strip, :angles]
            back = count - 1 - strip
            told[back, angles:] = leave * gain
            leave = leave * step + heard[back, angles:]
        for by in range(1, count):
            down(lax.rem(me + by, count)).start()
        out[mine] = told[me]

    for by in range(blocks):
        block = lax.rem(mine + by, blocks)
        pl.when(block * stride != me)(lambda: answered(block).wait_recv())
        pl.when(block * stride != me)(lambda: up(by).wait_send())

    @pl.when(joins)
    def _():
        for by in range(1, count):
            down(lax.rem(me + by, count)).wait_send()


def fourier_tables(side):
    indices = np.arange(side)
    products = indices[:, None] * indices[None, :] % side
    phases = products.astype(np.float64) * (-2.0 * math.pi / side)
    scale = 1.0 / math.sqrt(side)
    return (
        jnp.asarray(np.cos(phases) * scale, f32).astype(bf16),
        jnp.asarray(np.sin(phases) * scale, f32).astype(bf16),
    )


def cosine_factors(grid_side):
    half = grid_side // 2
    step = 32
    out = []
    for odd in (0, 1):
        freqs = 2 * np.arange(half) + odd
        scale = np.where(freqs == 0, math.sqrt(1.0 / grid_side), math.sqrt(2.0 / grid_side))
        coarse = (2 * step * np.arange(half // step)[:, None] * freqs[None, :]) % (4 * grid_side)
        fine = ((2 * np.arange(step)[:, None] + 1) * freqs[None, :]) % (4 * grid_side)
        unit = math.pi / (2 * grid_side)
        out.append(
            np.stack(
                [
                    np.cos(coarse * unit) * scale,
                    np.sin(coarse * unit) * scale,
                    np.cos(fine * unit),
                    np.sin(fine * unit),
                ]
            )
        )
    return jnp.asarray(np.stack(out), f32)


def decay_tables(grid_side, strip_rows):
    half = grid_side // 2
    freqs = np.concatenate([2 * np.arange(half), 2 * np.arange(half) + 1]).astype(np.float64)
    shift = screen_term + 2.0 - 2.0 * np.cos(freqs * math.pi / grid_side)
    rate = 2.0 * np.arcsinh(np.sqrt(shift) / 2.0)
    gain = 1.0 / (2.0 * np.sinh(rate))
    rows = np.arange(GROUP)[:, None]
    down = [np.where(rows >= s, np.exp(-s * rate), 0.0) for s in (1, 2, 4)]
    up = [np.where(rows < GROUP - s, np.exp(-s * rate), 0.0) for s in (1, 2, 4)]
    down.append(np.exp(-(rows + 1) * rate))
    up.append(np.exp(-(GROUP - rows) * rate))
    local = np.stack(down + up)
    strips = grid_side // strip_rows
    powers = np.exp(-strip_rows * np.arange(strips + 1)[:, None] * rate)
    extra = np.stack(
        [gain, 1.0 / (1.0 - np.exp(-2.0 * grid_side * rate)), np.exp(-GROUP * rate)]
        + [rate * 0.0] * 5
    )
    return local.astype(np.float32), powers.astype(np.float32), extra.astype(np.float32)


def table_kernel(factors, even_hi, even_lo, odd_hi, odd_lo):
    step = factors.shape[2]
    blocks = even_hi.shape[0] // step
    for part, (high, low) in enumerate(((even_hi, even_lo), (odd_hi, odd_lo))):
        fine_cos = factors[part, 2]
        fine_sin = factors[part, 3]
        for block in range(blocks):
            value = (
                factors[part, 0, block : block + 1] * fine_cos
                - factors[part, 1, block : block + 1] * fine_sin
            )
            rounded = value.astype(bf16)
            high[block * step : (block + 1) * step] = rounded
            low[block * step : (block + 1) * step] = (value - rounded.astype(f32)).astype(bf16)


def window_start(column, width, span):
    return jnp.minimum(column // LANES, (width - span) // LANES) * LANES


def cut_kernel(tables, field, out, buffer, sems):
    count, cap = out.shape[0], out.shape[1]
    width = field.shape[3]
    side = out.shape[-1]
    span = side + LANES
    jobs = [(j, s) for j in range(count) for s in range(cap)]

    def fetch(index):
        j, s = jobs[index]
        start = pl.multiple_of(window_start(tables[j, s, 1], width, span), LANES)
        return pltpu.make_async_copy(
            field.at[tables[j, s, 2], :, :, pl.ds(start, span)], buffer.at[index], sems.at[index]
        )

    for index in range(len(jobs)):
        fetch(index).start()
    for index, (j, s) in enumerate(jobs):
        fetch(index).wait()
        column = tables[j, s, 1]
        shift = column - window_start(column, width, span)
        for part in range(2):
            turned = pltpu.roll(buffer[index, part], lax.rem(span - shift, span), 1)
            out[j, s, part] = turned[:, :side].astype(bf16)


def frame_kernel(
    tables, probe, moved, cos_ref, sin_ref, arrived, own_out, away_out, window
):
    pieces = [arrived.at[j] for j in range(arrived.shape[0])]
    measured = moved.at[0]
    cap, side = measured.shape[0], measured.shape[1]
    strip = pieces[0].shape[2]
    reach = len(pieces) - 1
    middle = reach // 2
    total = (reach + 1) * strip
    cos_part, sin_part = cos_ref[...], sin_ref[...]
    stacked = jnp.concatenate([cos_part, sin_part], 0)
    joined = jnp.concatenate([cos_part, sin_part], 1)
    probe_re, probe_im = probe[0], probe[1]
    peak = jnp.max(probe_re * probe_re + probe_im * probe_im) + epsilon_term

    def left(re, im, sign):
        products = jnp.dot(
            stacked, jnp.concatenate([re, im], 1), preferred_element_type=f32
        )
        cc, ci = products[:side, :side], products[:side, side:]
        sc, si = products[side:, :side], products[side:, side:]
        return (cc - si, ci + sc) if sign > 0 else (cc + si, ci - sc)

    def right(re, im, sign):
        products = jnp.dot(
            jnp.concatenate([re, im], 0), joined, preferred_element_type=f32
        )
        rc, rs = products[:side, :side], products[:side, side:]
        ic, js = products[side:, :side], products[side:, side:]
        return (rc - js, rs + ic) if sign > 0 else (rc + js, ic - rs)

    for s in range(cap):
        offset = tables[middle, s, 0]
        patch = []
        for part in range(2):
            for j in range(reach + 1):
                window[j * strip : (j + 1) * strip] = pieces[j][s, part].astype(f32)
            turned = pltpu.roll(window[...], lax.rem(total - offset, total), 0)
            patch.append(turned[:side])
        wave_re = (probe_re * patch[0] - probe_im * patch[1]).astype(bf16)
        wave_im = (probe_re * patch[1] + probe_im * patch[0]).astype(bf16)
        half_re, half_im = left(wave_re, wave_im, 1)
        spec_re, spec_im = right(half_re.astype(bf16), half_im.astype(bf16), 1)
        amplitude = jnp.sqrt(spec_re * spec_re + spec_im * spec_im)
        factor = measured[s].astype(f32) / jnp.maximum(amplitude, magnitude_floor) - 1.0
        back_re, back_im = left(
            (spec_re * factor).astype(bf16), (spec_im * factor).astype(bf16), -1
        )
        corr_re, corr_im = right(back_re.astype(bf16), back_im.astype(bf16), -1)
        live = s < tables[middle, cap, 0]
        updates = (
            (probe_re * corr_re + probe_im * corr_im) / peak,
            (probe_re * corr_im - probe_im * corr_re) / peak,
        )
        for part in range(2):
            window[...] = jnp.zeros_like(window)
            window[:side] = jnp.where(live, updates[part], 0.0)
            turned = pltpu.roll(window[...], offset, 0)
            for j in range(reach + 1):
                piece = turned[j * strip : (j + 1) * strip]
                if j == middle:
                    own_out[s, part] = piece
                else:
                    away_out[j, s, part] = piece.astype(bf16)


def place_kernel(tables, field, own, away_ref, updated, out, edges, sem):
    pieces = [away_ref.at[j] for j in range(away_ref.shape[0])]
    pieces[(len(pieces) - 1) // 2] = own
    width = field.shape[3]
    cap, side = own.shape[0], own.shape[3]
    span = side + LANES
    out[...] = field[...]
    pad = jnp.zeros((own.shape[2], LANES), f32)
    for j, source in enumerate(pieces):
        for s in range(cap):
            column = tables[j, s, 1]
            start = pl.multiple_of(window_start(column, width, span), LANES)
            shift = column - start
            angle = tables[j, s, 2]
            for part in range(2):
                value = jnp.concatenate([source[s, part].astype(f32), pad], 1)
                turned = pltpu.roll(value, shift, 1)
                out[angle, part, :, pl.ds(start, span)] = (
                    out[angle, part, :, pl.ds(start, span)] + turned
                )
    strip = field.shape[2]
    for angle in range(field.shape[0]):
        for part in range(2):
            edges[0, angle, part] = out[angle, part, :1]
            edges[1, angle, part] = out[angle, part, strip - 1 :]
    copy = pltpu.make_async_copy(out, updated, sem)
    copy.start()
    copy.wait()


def mirror(value):
    side = value.shape[1]
    rows = lax.broadcasted_iota(jnp.int32, (side, side), 0)
    columns = lax.broadcasted_iota(jnp.int32, (side, side), 1)
    swap = jnp.where(rows + columns == side - 1, 1.0, 0.0).astype(bf16)
    total = None
    for _ in range(3):
        piece = value.astype(bf16)
        value = value - piece.astype(f32)
        term = jnp.dot(piece, swap, preferred_element_type=f32)
        total = term if total is None else total + term
    return total


def split_store(value, high, low, columns):
    rounded = value.astype(bf16)
    high[:, columns] = rounded
    low[:, columns] = (value - rounded.astype(f32)).astype(bf16)


def bond(a_re, a_im, b_re, b_im):
    cross = a_re * b_im - a_im * b_re
    power = a_re * a_re + a_im * a_im + b_re * b_re + b_im * b_im + soften_term
    return 2.0 * cross / power


def forward_kernel(
    field, halo, even_hi, even_lo, odd_hi, odd_lo, local, extra,
    out, ends, source, xeh, xel, xoh, xol,
):
    angles, _, strip, width = field.shape
    half = width // 2
    block = GROUP * 2
    columns = lax.broadcasted_iota(jnp.int32, (block, width), 1)
    for angle in range(angles):
        for first in range(0, strip, block):
            here, up, down, left = [], [], [], []
            for part in range(2):
                body = field[angle, part, first : first + block]
                before = (
                    halo[0, angle, part]
                    if first == 0
                    else field[angle, part, first - 1 : first]
                )
                after = (
                    halo[1, angle, part]
                    if first + block == strip
                    else field[angle, part, first + block : first + block + 1]
                )
                here.append(body)
                up.append(jnp.concatenate([before, body[:-1]], 0))
                down.append(jnp.concatenate([body[1:], after], 0))
                left.append(jnp.where(columns == 0, 0.0, pltpu.roll(body, 1, 1)))
            row_up = bond(*up, *here)
            row_down = bond(*here, *down)
            col_left = bond(*left, *here)
            col_right = jnp.where(
                columns == width - 1, 0.0, pltpu.roll(col_left, width - 1, 1)
            )
            source[angle * strip + first : angle * strip + first + block] = -(
                row_down - row_up + col_right - col_left
            )
    for first in range(0, half, TILE):
        near = source[:, first : first + TILE]
        far = mirror(source[:, width - first - TILE : width - first])
        where = slice(first, first + TILE)
        split_store(near + far, xeh, xel, where)
        split_store(near - far, xoh, xol, where)
    for base, high, low, table_hi, table_lo in (
        (0, xeh, xel, even_hi, even_lo),
        (half, xoh, xol, odd_hi, odd_lo),
    ):
        for first in range(0, half, TILE):
            where = slice(first, first + TILE)
            source[:, base + first : base + first + TILE] = (
                jnp.dot(high[...], table_hi[:, where], preferred_element_type=f32)
                + jnp.dot(low[...], table_hi[:, where], preferred_element_type=f32)
                + jnp.dot(high[...], table_lo[:, where], preferred_element_type=f32)
            )
    groups = strip // GROUP

    def scan(chunk, _):
        where = pl.ds(pl.multiple_of(chunk * LANES, LANES), LANES)
        gain = extra[0:1, where]
        for angle in range(angles):
            value = source[angle * strip : (angle + 1) * strip, where]
            value = value.reshape(groups, GROUP, LANES)
            fall, rise = value, value
            for index, by in enumerate((1, 2, 4)):
                fall = fall + local[index, :, where][None] * pltpu.roll(fall, by, 1)
                rise = rise + local[4 + index, :, where][None] * pltpu.roll(rise, GROUP - by, 1)
            falls, carry = [], None
            for group in range(groups):
                item = fall[group]
                if carry is not None:
                    item = item + local[3, :, where] * carry
                carry = item[GROUP - 1 :]
                falls.append(item)
            ends[chunk, angle : angle + 1] = carry
            rises, carry = [None] * groups, None
            for group in reversed(range(groups)):
                item = rise[group]
                if carry is not None:
                    item = item + local[7, :, where] * carry
                carry = item[:1]
                rises[group] = item
            ends[chunk, angles + angle : angles + angle + 1] = carry
            for group in range(groups):
                out[angle, group * GROUP : (group + 1) * GROUP, where] = gain * (
                    falls[group] + rises[group] - value[group]
                )
        return 0

    lax.fori_loop(0, width // LANES, scan, 0)


def inverse_kernel(
    value, incoming, even_hi, even_lo, odd_hi, odd_lo, local, extra, out, xh, xl
):
    angles, strip, width = value.shape
    half = width // 2
    groups = strip // GROUP

    def enter(chunk, _):
        where = pl.ds(pl.multiple_of(chunk * LANES, LANES), LANES)
        for angle in range(angles):
            fall = incoming[chunk, angle : angle + 1]
            rise = incoming[chunk, angles + angle : angles + angle + 1]
            step = extra[2:3, where]
            falls, rises = [], []
            for group in range(groups):
                falls.append(fall)
                rises.append(rise)
                fall = fall * step
                rise = rise * step
            for pair in range(0, groups, 2):
                rows = []
                for group in (pair, pair + 1):
                    rows.append(
                        value[angle, group * GROUP : (group + 1) * GROUP, where]
                        + local[3, :, where] * falls[group]
                        + local[7, :, where] * rises[groups - 1 - group]
                    )
                item = jnp.concatenate(rows, 0)
                rounded = item.astype(bf16)
                start = angle * strip + pair * GROUP
                xh[start : start + 2 * GROUP, where] = rounded
                xl[start : start + 2 * GROUP, where] = (item - rounded.astype(f32)).astype(bf16)
        return 0

    lax.fori_loop(0, width // LANES, enter, 0)
    last = (((1,), (1,)), ((), ()))
    for first in range(0, half, TILE):
        where = slice(first, first + TILE)
        parts = []
        for base, table_hi, table_lo in ((0, even_hi, even_lo), (half, odd_hi, odd_lo)):
            high = xh[:, base : base + half]
            low = xl[:, base : base + half]
            parts.append(
                lax.dot_general(high, table_hi[where], last, preferred_element_type=f32)
                + lax.dot_general(low, table_hi[where], last, preferred_element_type=f32)
                + lax.dot_general(high, table_lo[where], last, preferred_element_type=f32)
            )
        near = parts[0] + parts[1]
        far = mirror(parts[0] - parts[1])
        for angle in range(angles):
            rows = slice(angle * strip, (angle + 1) * strip)
            out[angle, :, where] = near[rows]
            out[angle, :, width - first - TILE : width - first] = far[rows]


def body(object_field, probe, measured, frame_table, frame_count):
    angles, _, strip, width = object_field.shape
    side = probe.shape[1]
    cap = measured.shape[0]
    half = width // 2
    reach = side // strip
    rows = angles * strip
    strips = lax.axis_size("tile")
    blocks = width // LANES
    shape = jax.ShapeDtypeStruct

    middle = reach // 2
    others = [j for j in range(reach + 1) if j != middle]
    record = jnp.concatenate(
        [frame_table, jnp.pad(frame_count[:, None], ((0, 0), (0, 2)))]
    )
    moves = [(0, 0, j, j) for j in range(1, reach + 1)]
    keep = [(0, 0, 0)]
    if middle:
        moves.append((1, 0, 0, middle))
    else:
        keep.append((1, 0, 0))
    tables, moved = exchanged(
        [record[None], measured[None]], [reach + 1, 1], moves, keep, 0, "tell"
    )
    cuts = pl.pallas_call(
        cut_kernel,
        out_shape=shape((reach + 1, cap, 2, strip, side), bf16),
        in_specs=[smem, hbm],
        out_specs=vmem,
        scratch_shapes=[
            pltpu.VMEM(((reach + 1) * cap, 2, strip, side + LANES), f32),
            pltpu.SemaphoreType.DMA(((reach + 1) * cap,)),
        ],
        compiler_params=pltpu.CompilerParams(vmem_limit_bytes=2 * VMEM_BYTES),
        cost_estimate=cost(2),
        name="cut",
    )(tables, object_field)
    (arrived,) = exchanged(
        [cuts], [reach + 1], [(0, j, j, middle - j) for j in others], [(0, middle, middle)], 1, "fetch"
    )

    factors = cosine_factors(width)
    local, powers, extra = decay_tables(width, strip)

    def by_block(table):
        return jnp.asarray(table.reshape(-1, blocks, LANES).transpose(1, 0, 2))

    cos_part, sin_part = fourier_tables(side)

    own, away = pl.pallas_call(
        frame_kernel,
        out_shape=[
            shape((cap, 2, strip, side), f32),
            shape((reach + 1, cap, 2, strip, side), bf16),
        ],
        in_specs=[smem] + [vmem] * 5,
        out_specs=[vmem, vmem],
        scratch_shapes=[pltpu.VMEM(((reach + 1) * strip, side), f32)],
        compiler_params=params(),
        cost_estimate=cost(4),
        name="frames",
    )(tables, probe, moved, cos_part, sin_part, arrived)
    (landed,) = exchanged(
        [away], [reach + 1], [(0, j, j, j - middle) for j in others], [], 2, "give"
    )

    updated, held, edges = pl.pallas_call(
        place_kernel,
        out_shape=[shape(object_field.shape, f32)] * 2 + [shape((2, angles, 2, 1, width), f32)],
        in_specs=[smem, vmem, vmem, vmem],
        out_specs=[hbm, vmem, vmem],
        scratch_shapes=[pltpu.SemaphoreType.DMA],
        compiler_params=params(),
        cost_estimate=cost(3),
        name="place",
    )(tables, object_field, own, landed)
    halo, *half_tables = exchanged(
        [edges], [2], [(0, 1, 0, 1), (0, 0, 1, -1)], [], 3, "edges",
        table_kernel, [factors], [shape((half, half), bf16)] * 4,
    )

    solved, ends = pl.pallas_call(
        forward_kernel,
        out_shape=[shape((angles, strip, width), f32), shape((blocks, 2 * angles, LANES), f32)],
        in_specs=[vmem] * 8,
        out_specs=[vmem, vmem],
        scratch_shapes=[pltpu.VMEM((rows, width), f32)] + [pltpu.VMEM((rows, half), bf16)] * 4,
        compiler_params=params(),
        cost_estimate=cost(9),
        name="forward",
    )(held, halo, *half_tables, local, extra)
    incoming = pl.pallas_call(
        join_kernel,
        out_shape=shape(ends.shape, f32),
        in_specs=[vmem] * 3,
        out_specs=vmem,
        scratch_shapes=[
            pltpu.VMEM((strips, 2 * angles, LANES), f32),
            pltpu.VMEM((strips, 2 * angles, LANES), f32),
            pltpu.SemaphoreType.DMA((blocks,)),
            pltpu.SemaphoreType.DMA((strips,)),
            pltpu.SemaphoreType.DMA((strips,)),
            pltpu.SemaphoreType.DMA((blocks,)),
        ],
        compiler_params=params(collective_id=4, has_side_effects=True),
        cost_estimate=cost(10),
        name="join",
    )(ends, by_block(powers), by_block(extra))
    phase_map = pl.pallas_call(
        inverse_kernel,
        out_shape=shape((angles, strip, width), f32),
        in_specs=[vmem] * 8,
        out_specs=vmem,
        scratch_shapes=[
            pltpu.VMEM((rows, width), bf16),
            pltpu.VMEM((rows, width), bf16),
        ],
        compiler_params=params(),
        cost_estimate=cost(6),
        name="inverse",
    )(solved, incoming, *half_tables, local, extra)
    return (updated, phase_map)


def solution(mesh):
    return jax.shard_map(
        body,
        mesh=mesh,
        in_specs=(
            P("group", None, "tile", None),
            P(),
            P(("group", "tile"), None, None),
            P(("group", "tile"), None),
            P(("group", "tile")),
        ),
        out_specs=(P("group", None, "tile", None), P("group", "tile", None)),
        check_vma=False,
    )
```

profile of v0, /device:TPU:0, one launch (start us, length us, event | category | flops | bytes accessed | tf_op | source)
XLA Modules:
  0.0 73.8 jit_solution(7959951034225477662)
XLA Ops:
  1.3 0.7 fusion.refs_0_
  2.0 0.0 copy-start.6
  2.0 0.9 %copy-done.6 = bf16[2,256,256]{2,1,0:T(8,128)(2,1)S(1)} copy-done((bf16[2,256,256]{2,1,0:T(8,128)(2,1)S(1)}, bf16[2,256,256]{2,1,0:T(8,128)(2,1)}, u32[]{:S(2)}) %copy-start.6) | copy-done | bytes 262168
  2.9 4.4 %tell.1 = (s32[3,3,3]{2,1,0:T(4,128)S(1)}, bf16[1,2,256,256]{3,2,1,0:T(8,128)(2,1)S(1)}) custom-call(s32[1,3,3]{2,1,0:T(4,128)S(1)} %fusion.refs_0_, bf16[1,2,256,256]{3,2,1,0:T(8,128)(2,1)S(1)} %bitcast.5), custom_call_target="tpu_custom_call" | custom-call | bytes 12000000 | tf_op jit(solution)/shard_map/tell/pallas_call | solution.py:88
  7.3 0.0 copy-start.11
  7.3 0.6 copy-done.11
  7.9 4.2 %cut.1.refs_0_ = bf16[3,2,2,128,256]{4,3,2,1,0:T(8,128)(2,1)} custom-call(s32[3,3,3]{2,1,0:T(4,128)} %copy-done.11, f32[2,2,128,2048]{3,2,1,0:T(8,128)} %field.3), custom_call_target="tpu_custom_call" | custom-call | bytes 6000000 | tf_op jit(solution)/shard_map/cut/pallas_call | solution.py:604
  12.1 0.0 copy-start.1
  12.1 1.1 %copy-done.1 = bf16[3,2,2,128,256]{4,3,2,1,0:T(8,128)(2,1)S(1)} copy-done((bf16[3,2,2,128,256]{4,3,2,1,0:T(8,128)(2,1)S(1)}, bf16[3,2,2,128,256]{4,3,2,1,0:T(8,128)(2,1)}, u32[]{:S(2)}) %copy-start.1) | copy-done | bytes 786456
  13.2 5.3 %fetch.1.arrived = bf16[3,2,2,128,256]{4,3,2,1,0:T(8,128)(2,1)S(1)} custom-call(bf16[3,2,2,128,256]{4,3,2,1,0:T(8,128)(2,1)S(1)} %copy-done.1), custom_call_target="tpu_custom_call" | custom-call | bytes 12000000 | tf_op jit(solution)/shard_map/fetch/pallas_call | solution.py:88
  18.5 0.0 copy-done.4
  18.5 0.0 copy-done.8
  18.5 0.0 copy-done.9
  18.6 0.0 copy-done.12
  18.6 4.3 %frames.1 = (f32[2,2,128,256]{3,2,1,0:T(8,128)S(1)}, bf16[3,2,2,128,256]{4,3,2,1,0:T(8,128)(2,1)S(1)}) custom-call(s32[3,3,3]{2,1,0:T(4,128)S(1)} %copy-done.12, f32[2,256,256]{2,1,0:T(8,128)S(1)} %copy-done.4, bf16[1,2,256,256]{3,2,1,0:T(8,128)(2,1)S(1)} %get-tuple-element.17.moved, bf16[256,256]{1,0:T(8,128)(2,1)S(1)} %copy-done.9, ...), custom_call_target="tpu_custom_call" | custom-call | bytes 12000000 | tf_op jit(solution)/shard_map/frames/pallas_call | solution.py:629
  22.8 8.7 %give.1.away_ref = bf16[3,2,2,128,256]{4,3,2,1,0:T(8,128)(2,1)S(1)} custom-call(bf16[3,2,2,128,256]{4,3,2,1,0:T(8,128)(2,1)S(1)} %get-tuple-element.19.refs_0_), custom_call_target="tpu_custom_call" | custom-call | bytes 12000000 | tf_op jit(solution)/shard_map/give/pallas_call | solution.py:88
  31.5 0.0 copy-done
  31.5 0.0 copy-start.3
  31.6 0.0 copy-start.2
  31.6 0.0 copy-start.5
  31.6 3.4 %place.1 = (f32[2,2,128,2048]{3,2,1,0:T(8,128)}, f32[2,2,128,2048]{3,2,1,0:T(8,128)S(1)}, f32[2,2,2,1,2048]{4,3,2,1,0:T(1,128)S(1)}) custom-call(s32[3,3,3]{2,1,0:T(4,128)S(1)} %copy-done.12, f32[2,2,128,2048]{3,2,1,0:T(8,128)S(1)} %copy-done, f32[2,2,128,256]{3,2,1,0:T(8,128)S(1)} %get-tuple-element.18.own, bf16[3,2,2,128,256]{4,3,2,1,0:T(8,128)(2,1)S(1)} %give.1.away_ref), custom_call_target="tpu_custom_call" | custom-call | bytes 9000000 | tf_op jit(solution)/shard_map/place/pallas_call | solution.py:646
  35.0 0.0 copy-done.3
  35.0 8.4 %edges.1 = (f32[2,2,2,1,2048]{4,3,2,1,0:T(1,128)S(1)}, bf16[1024,1024]{1,0:T(8,128)(2,1)S(1)}, bf16[1024,1024]{1,0:T(8,128)(2,1)S(1)}, bf16[1024,1024]{1,0:T(8,128)(2,1)S(1)}, bf16[1024,1024]{1,0:T(8,128)(2,1)S(1)}) custom-call(f32[2,2,2,1,2048]{4,3,2,1,0:T(1,128)S(1)} %get-tuple-element.22.refs_0_, f32[2,4,32,1024]{3,2,1,0:T(8,128)S(1)} %copy-done.3), custom_call_target="tpu_custom_call" | custom-call | bytes 12000000 | tf_op jit(solution)/shard_map/edges/pallas_call | solution.py:88
  43.4 0.0 copy-done.2
  43.4 0.0 copy-done.5
  43.4 0.0 copy-start.7
  43.4 0.0 copy-start.10
  43.4 9.8 %forward.1 = (f32[2,128,2048]{2,1,0:T(8,128)S(1)}, f32[16,4,128]{2,1,0:T(4,128)S(1)}) custom-call(f32[2,2,128,2048]{3,2,1,0:T(8,128)S(1)} %get-tuple-element.21.field, f32[2,2,2,1,2048]{4,3,2,1,0:T(1,128)S(1)} %get-tuple-element.23.halo, bf16[1024,1024]{1,0:T(8,128)(2,1)S(1)} %get-tuple-element.24.even_hi, bf16[1024,1024]{1,0:T(8,128)(2,1)S(1)} %get-tuple-element.25.even_lo, ...), custom_call_target="tpu_custom_call" | custom-call | bytes 27000000 | tf_op jit(solution)/shard_map/forward/pallas_call | solution.py:661
  53.3 0.0 copy-done.7
  53.3 0.0 copy-done.10
  53.3 13.7 %join.1.incoming = f32[16,4,128]{2,1,0:T(4,128)S(1)} custom-call(f32[16,4,128]{2,1,0:T(4,128)S(1)} %get-tuple-element.29.ends, f32[16,17,128]{2,1,0:T(8,128)S(1)} %copy-done.7, f32[16,8,128]{2,1,0:T(8,128)S(1)} %copy-done.10), custom_call_target="tpu_custom_call" | custom-call | bytes 30000000 | tf_op jit(solution)/shard_map/join/pallas_call | solution.py:671
  67.0 6.8 %inverse.1 = f32[2,128,2048]{2,1,0:T(8,128)} custom-call(f32[2,128,2048]{2,1,0:T(8,128)S(1)} %get-tuple-element.28.value, f32[16,4,128]{2,1,0:T(4,128)S(1)} %join.1.incoming, bf16[1024,1024]{1,0:T(8,128)(2,1)S(1)} %get-tuple-element.24.even_hi, bf16[1024,1024]{1,0:T(8,128)(2,1)S(1)} %get-tuple-element.25.even_lo, ...), custom_call_target="tpu_custom_call" | custom-call | bytes 18000000 | tf_op jit(solution)/shard_map/inverse/pallas_call | solution.py:688
  (5 shorter events, 0.0 us)
Async XLA Ops:
  2.0 0.9 %copy-start.6 = (bf16[2,256,256]{2,1,0:T(8,128)(2,1)S(1)}, bf16[2,256,256]{2,1,0:T(8,128)(2,1)}, u32[]{:S(2)}) copy-start(bf16[2,256,256]{2,1,0:T(8,128)(2,1)} %param.14) | copy-start | bytes 786436
  7.3 0.6 copy-start.11
  7.9 10.7 %copy-start.4 = (f32[2,256,256]{2,1,0:T(8,128)S(1)}, f32[2,256,256]{2,1,0:T(8,128)}, u32[]{:S(2)}) copy-start(f32[2,256,256]{2,1,0:T(8,128)} %probe.1) | copy-start | bytes 1572868
  7.9 10.7 %copy-start.8 = (bf16[256,256]{1,0:T(8,128)(2,1)S(1)}, bf16[256,256]{1,0:T(8,128)(2,1)}, u32[]{:S(2)}) copy-start(bf16[256,256]{1,0:T(8,128)(2,1)} %constant.29.sin_ref) | copy-start | bytes 393220
  7.9 10.7 %copy-start.9 = (bf16[256,256]{1,0:T(8,128)(2,1)S(1)}, bf16[256,256]{1,0:T(8,128)(2,1)}, u32[]{:S(2)}) copy-start(bf16[256,256]{1,0:T(8,128)(2,1)} %constant.28.cos_ref) | copy-start | bytes 393220
  7.9 10.7 %copy-start.12 = (s32[3,3,3]{2,1,0:T(4,128)S(1)}, s32[3,3,3]{2,1,0:T(4,128)}, u32[]{:S(2)}) copy-start(s32[3,3,3]{2,1,0:T(4,128)} %copy-done.11) | copy-start | bytes 328
  12.1 1.1 %copy-start.1 = (bf16[3,2,2,128,256]{4,3,2,1,0:T(8,128)(2,1)S(1)}, bf16[3,2,2,128,256]{4,3,2,1,0:T(8,128)(2,1)}, u32[]{:S(2)}) copy-start(bf16[3,2,2,128,256]{4,3,2,1,0:T(8,128)(2,1)} %cut.1.refs_0_) | copy-start | bytes 2359300
  13.2 18.3 %copy-start = (f32[2,2,128,2048]{3,2,1,0:T(8,128)S(1)}, f32[2,2,128,2048]{3,2,1,0:T(8,128)}, u32[]{:S(2)}) copy-start(f32[2,2,128,2048]{3,2,1,0:T(8,128)} %field.3) | copy-start | bytes 12582916
  31.5 3.5 %copy-start.3 = (f32[2,4,32,1024]{3,2,1,0:T(8,128)S(1)}, f32[2,4,32,1024]{3,2,1,0:T(8,128)}, u32[]{:S(2)}) copy-start(f32[2,4,32,1024]{3,2,1,0:T(8,128)} %constant.16.clone.refs_1_) | copy-start | bytes 3145732
  31.6 11.8 %copy-start.2 = (f32[8,8,2048]{2,1,0:T(8,128)S(1)}, f32[8,8,2048]{2,1,0:T(8,128)}, u32[]{:S(2)}) copy-start(f32[8,8,2048]{2,1,0:T(8,128)} %constant.19.clone.local) | copy-start | bytes 1572868
  31.6 11.8 %copy-start.5 = (f32[8,2048]{1,0:T(8,128)S(1)}, f32[8,2048]{1,0:T(8,128)}, u32[]{:S(2)}) copy-start(f32[8,2048]{1,0:T(8,128)} %constant.20.clone.extra) | copy-start | bytes 196612
  43.4 9.9 %copy-start.7 = (f32[16,17,128]{2,1,0:T(8,128)S(1)}, f32[16,17,128]{2,1,0:T(8,128)}, u32[]{:S(2)}) copy-start(f32[16,17,128]{2,1,0:T(8,128)} %constant.21.clone.powers) | copy-start | bytes 417796
  43.4 9.9 %copy-start.10 = (f32[16,8,128]{2,1,0:T(8,128)S(1)}, f32[16,8,128]{2,1,0:T(8,128)}, u32[]{:S(2)}) copy-start(f32[16,8,128]{2,1,0:T(8,128)} %constant.22.clone.extra) | copy-start | bytes 196612
where the time goes:
time: 74.1 us; the launch traced here: 73.8 us
  Pallas kernels  68.9 us (93%)
  local copies, waits for them, and re-layouts  2.72 us (4%)
  between operations  1.49 us (2%)
    pallas_call x4, Pallas kernels, exchanged(): pl.pallas_call(functools.partial(exchange_kernel, moves, keep, work, len(...  26.7 us
    pallas_call x1, Pallas kernels, body(): pl.pallas_call(join_kernel, out_shape=shape(ends.shape, f32), in_specs=[v...  13.7 us
    pallas_call x1, Pallas kernels, body(): pl.pallas_call(forward_kernel, out_shape=[shape((angles, strip, width), f...  9.82 us
    pallas_call x1, Pallas kernels, body(): pl.pallas_call(inverse_kernel, out_shape=shape((angles, strip, width), f3...  6.83 us
    pallas_call x1, Pallas kernels, body(): pl.pallas_call(frame_kernel, out_shape=[shape((cap, 2, strip, side), f32)...  4.27 us
    pallas_call x1, Pallas kernels, body(): pl.pallas_call(cut_kernel, out_shape=shape((reach + 1, cap, 2, strip, sid...  4.2 us
    pallas_call x1, Pallas kernels, body(): pl.pallas_call(place_kernel, out_shape=[shape(object_field.shape, f32)] *...  3.42 us
    unnamed x26, local copies, waits for them, and re-layouts  2.72 us

commit v1 on v0

--- a/solution.py
+++ b/solution.py
@@ -33,72 +33,6 @@
 
 def params(**more):
     return pltpu.CompilerParams(vmem_limit_bytes=VMEM_BYTES, **more)
-
-
-def exchange_kernel(moves, keep, work, arrays, inputs, *refs):
-    sources, given = refs[:arrays], refs[arrays : arrays + inputs]
-    outs = refs[arrays + inputs : 2 * arrays + inputs]
-    made = refs[2 * arrays + inputs : -2]
-    send_sems, recv_sems = refs[-2:]
-    count = lax.axis_size("tile")
-    me = lax.axis_index("tile")
-    barrier = pltpu.get_barrier_semaphore()
-    met = jnp.zeros((), jnp.int32)
-    for by in sorted({sign * by for *_, by in moves for sign in (1, -1)}):
-        there = (me + by >= 0) & (me + by < count)
-
-        @pl.when(there)
-        def _():
-            pl.semaphore_signal(
-                barrier, inc=1, device_id={"tile": me + by}, device_id_type=MESH
-            )
-
-        met = met + jnp.where(there, 1, 0)
-    pl.semaphore_wait(barrier, met)
-    copies = []
-    for index, (array, first, last, by) in enumerate(moves):
-        copy = pltpu.make_async_remote_copy(
-            src_ref=sources[array].at[first],
-            dst_ref=outs[array].at[last],
-            send_sem=send_sems.at[index],
-            recv_sem=recv_sems.at[index],
-            device_id={"tile": me + by},
-            device_id_type=MESH,
-        )
-        sends = (me + by >= 0) & (me + by < count)
-        takes = (me - by >= 0) & (me - by < count)
-        copies.append((copy, sends, takes, outs[array], last))
-        pl.when(sends)(copy.start)
-    if work is not None:
-        work(*given, *made)
-    for array, first, last in keep:
-        outs[array][last] = sources[array][first]
-    for copy, sends, takes, out, last in copies:
-
-        @pl.when(jnp.logical_not(takes))
-        def _():
-            out[last] = jnp.zeros(out.shape[1:], out.dtype)
-
-    for copy, sends, takes, out, last in copies:
-        pl.when(takes)(copy.wait_recv)
-        pl.when(sends)(copy.wait_send)
-
-
-def exchanged(sources, slots, moves, keep, number, name, work=None, given=(), made=()):
-    return pl.pallas_call(
-        functools.partial(exchange_kernel, moves, keep, work, len(sources), len(given)),
-        out_shape=[
-            jax.ShapeDtypeStruct((slot,) + source.shape[1:], source.dtype)
-            for slot, source in zip(slots, sources)
-        ]
-        + list(made),
-        in_specs=[vmem] * (len(sources) + len(given)),
-        out_specs=[vmem] * (len(sources) + len(made)),
-        scratch_shapes=[pltpu.SemaphoreType.DMA((len(moves),))] * 2,
-        compiler_params=params(collective_id=number, has_side_effects=True),
-        cost_estimate=cost(4),
-        name=name,
-    )(*sources, *given)
 
 
 def join_kernel(ends, powers, extra, out, heard, told, up_sems, in_sems, down_sems, back_sems):
@@ -263,61 +197,177 @@
     return local.astype(np.float32), powers.astype(np.float32), extra.astype(np.float32)
 
 
-def table_kernel(factors, even_hi, even_lo, odd_hi, odd_lo):
+def table_rows(factors, part, high, low):
     step = factors.shape[2]
-    blocks = even_hi.shape[0] // step
-    for part, (high, low) in enumerate(((even_hi, even_lo), (odd_hi, odd_lo))):
-        fine_cos = factors[part, 2]
-        fine_sin = factors[part, 3]
-        for block in range(blocks):
-            value = (
-                factors[part, 0, block : block + 1] * fine_cos
-                - factors[part, 1, block : block + 1] * fine_sin
-            )
-            rounded = value.astype(bf16)
-            high[block * step : (block + 1) * step] = rounded
-            low[block * step : (block + 1) * step] = (value - rounded.astype(f32)).astype(bf16)
+
+    def run(block, _):
+        rows = pl.ds(pl.multiple_of(block * step, step), step)
+        value = (
+            factors[part, 0, pl.ds(block, 1)] * factors[part, 2]
+            - factors[part, 1, pl.ds(block, 1)] * factors[part, 3]
+        )
+        rounded = value.astype(bf16)
+        high[rows] = rounded
+        low[rows] = (value - rounded.astype(f32)).astype(bf16)
+        return 0
+
+    lax.fori_loop(0, high.shape[0] // step, run, 0)
 
 
 def window_start(column, width, span):
     return jnp.minimum(column // LANES, (width - span) // LANES) * LANES
 
 
-def cut_kernel(tables, field, out, buffer, sems):
-    count, cap = out.shape[0], out.shape[1]
-    width = field.shape[3]
-    side = out.shape[-1]
+def update_kernel(
+    frame_table, frame_count, field, probe_in, measured, cos_in, sin_in, factors_in,
+    held, halo, even_hi, even_lo, odd_hi, odd_lo,
+    tables, counts, probe, cos_ref, sin_ref, factors, moved, cuts, arrived, away, landed,
+    own, placed, window, edges,
+    load_sems, tell_sems, count_sems, moved_sems, fetch_sems, give_sems, edge_sems,
+):
+    count = lax.axis_size("tile")
+    me = lax.axis_index("tile")
+    angles, _, strip, width = field.shape
+    cap, side = measured.shape[0], measured.shape[1]
     span = side + LANES
-    jobs = [(j, s) for j in range(count) for s in range(cap)]
-
-    def fetch(index):
-        j, s = jobs[index]
-        start = pl.multiple_of(window_start(tables[j, s, 1], width, span), LANES)
-        return pltpu.make_async_copy(
-            field.at[tables[j, s, 2], :, :, pl.ds(start, span)], buffer.at[index], sems.at[index]
-        )
-
-    for index in range(len(jobs)):
-        fetch(index).start()
-    for index, (j, s) in enumerate(jobs):
-        fetch(index).wait()
-        column = tables[j, s, 1]
-        shift = column - window_start(column, width, span)
-        for part in range(2):
-            turned = pltpu.roll(buffer[index, part], lax.rem(span - shift, span), 1)
-            out[j, s, part] = turned[:, :side].astype(bf16)
-
-
-def frame_kernel(
-    tables, probe, moved, cos_ref, sin_ref, arrived, own_out, away_out, window
-):
-    pieces = [arrived.at[j] for j in range(arrived.shape[0])]
-    measured = moved.at[0]
-    cap, side = measured.shape[0], measured.shape[1]
-    strip = pieces[0].shape[2]
-    reach = len(pieces) - 1
+    lanes = span // LANES
+    blocks = width // LANES
+    reach = tables.shape[0] - 1
     middle = reach // 2
     total = (reach + 1) * strip
+    others = [j for j in range(reach + 1) if j != middle]
+
+    def inside(place):
+        return (place >= 0) & (place < count)
+
+    def load(index, source, target):
+        return pltpu.make_async_copy(source, target, load_sems.at[index])
+
+    loads = [
+        load(0, frame_table, tables.at[0]),
+        load(1, factors_in, factors),
+        load(2, probe_in, probe),
+        load(3, cos_in, cos_ref),
+        load(4, sin_in, sin_ref),
+    ]
+    strips = [
+        load(5 + block, field.at[:, :, :, block * LANES : (block + 1) * LANES], held.at[:, :, block])
+        for block in range(blocks)
+    ]
+    for item in loads[:2] + strips + loads[2:]:
+        item.start()
+    loads[0].wait()
+
+    def send(source, target, sems, index, by):
+        copy = pltpu.make_async_remote_copy(
+            src_ref=source,
+            dst_ref=target,
+            send_sem=sems.at[0, index],
+            recv_sem=sems.at[1, index],
+            device_id={"tile": me + by},
+            device_id_type=MESH,
+        )
+        return copy, inside(me + by), inside(me - by)
+
+    barrier = pltpu.get_barrier_semaphore()
+    met = jnp.zeros((), jnp.int32)
+    for by in [sign * by for by in range(1, reach + 1) for sign in (1, -1)]:
+
+        @pl.when(inside(me + by))
+        def _():
+            pl.semaphore_signal(
+                barrier, inc=1, device_id={"tile": me + by}, device_id_type=MESH
+            )
+
+        met = met + jnp.where(inside(me + by), 1, 0)
+    pl.semaphore_wait(barrier, met)
+
+    tells = [
+        send(tables.at[0], tables.at[j], tell_sems, j, j) for j in range(1, reach + 1)
+    ]
+    tells.append(send(frame_count, counts, count_sems, 0, middle))
+    moves = [
+        send(measured.at[s], moved.at[s], moved_sems, s, middle) for s in range(cap)
+    ]
+    fetches = [
+        [send(cuts.at[j, s], arrived.at[j, s], fetch_sems, s * (reach + 1) + j, middle - j) for j in others]
+        for s in range(cap)
+    ]
+    gives = [
+        [send(away.at[j, s], landed.at[j, s], give_sems, s * (reach + 1) + j, j - middle) for j in others]
+        for s in range(cap)
+    ]
+    borders = [
+        send(edges.at[1], halo.at[0], edge_sems, 0, 1),
+        send(edges.at[0], halo.at[1], edge_sems, 1, -1),
+    ]
+    started = []
+
+    def start(items):
+        for copy, sends, takes in items:
+            pl.when(sends)(copy.start)
+            started.append((copy, sends))
+
+    def arrive(items):
+        for copy, sends, takes in items:
+            pl.when(takes)(copy.wait_recv)
+
+    def blank(items, wipe):
+        for index, (copy, sends, takes) in enumerate(items):
+
+            @pl.when(jnp.logical_not(takes))
+            def _():
+                wipe(index)
+
+    def wipe_table(index):
+        if index == reach:
+            counts[0] = 0
+        else:
+            for s in range(cap):
+                for item in range(3):
+                    tables[index + 1, s, item] = 0
+
+    def wipe(ref, *first):
+        ref[first] = jnp.zeros(ref.shape[len(first):], ref.dtype)
+
+    start(tells)
+    start(moves)
+    blank(tells, wipe_table)
+    blank(moves, lambda s: wipe(moved, s))
+    for s in range(cap):
+        blank(fetches[s], lambda index: wipe(arrived, others[index], s))
+        blank(gives[s], lambda index: wipe(landed, others[index], s))
+    blank(borders, lambda index: wipe(halo, index))
+    for j in range(reach + 1):
+        for s in range(cap):
+            for part in range(2):
+                placed[j, s, part, 0] = jnp.zeros((strip, LANES), f32)
+    loads[1].wait()
+    table_rows(factors, 0, even_hi, even_lo)
+    for item in strips:
+        item.wait()
+    arrive(tells)
+
+    def first_block(j, s):
+        return jnp.minimum(tables[j, s, 1] // LANES, blocks - lanes)
+
+    for s in range(cap):
+        for j in others + [middle]:
+            block = first_block(j, s)
+            shift = tables[j, s, 1] - block * LANES
+            angle = tables[j, s, 2]
+            for part in range(2):
+                piece = jnp.concatenate(
+                    [held[angle, part, block + lane] for lane in range(lanes)], 1
+                )
+                turned = pltpu.roll(piece, lax.rem(span - shift, span), 1)
+                target = arrived if j == middle else cuts
+                target[j, s, part] = turned[:, :side].astype(bf16)
+        start(fetches[s])
+
+    table_rows(factors, 1, odd_hi, odd_lo)
+    for item in loads[2:5]:
+        item.wait()
     cos_part, sin_part = cos_ref[...], sin_ref[...]
     stacked = jnp.concatenate([cos_part, sin_part], 0)
     joined = jnp.concatenate([cos_part, sin_part], 1)
@@ -341,11 +391,12 @@
         return (rc - js, rs + ic) if sign > 0 else (rc + js, ic - rs)
 
     for s in range(cap):
+        arrive(fetches[s])
         offset = tables[middle, s, 0]
         patch = []
         for part in range(2):
             for j in range(reach + 1):
-                window[j * strip : (j + 1) * strip] = pieces[j][s, part].astype(f32)
+                window[j * strip : (j + 1) * strip] = arrived[j, s, part].astype(f32)
             turned = pltpu.roll(window[...], lax.rem(total - offset, total), 0)
             patch.append(turned[:side])
         wave_re = (probe_re * patch[0] - probe_im * patch[1]).astype(bf16)
@@ -353,56 +404,83 @@
         half_re, half_im = left(wave_re, wave_im, 1)
         spec_re, spec_im = right(half_re.astype(bf16), half_im.astype(bf16), 1)
         amplitude = jnp.sqrt(spec_re * spec_re + spec_im * spec_im)
-        factor = measured[s].astype(f32) / jnp.maximum(amplitude, magnitude_floor) - 1.0
+        if s == 0:
+            arrive(moves)
+        factor = moved[s].astype(f32) / jnp.maximum(amplitude, magnitude_floor) - 1.0
         back_re, back_im = left(
             (spec_re * factor).astype(bf16), (spec_im * factor).astype(bf16), -1
         )
         corr_re, corr_im = right(back_re.astype(bf16), back_im.astype(bf16), -1)
-        live = s < tables[middle, cap, 0]
+        live = s < counts[0]
         updates = (
             (probe_re * corr_re + probe_im * corr_im) / peak,
             (probe_re * corr_im - probe_im * corr_re) / peak,
         )
         for part in range(2):
-            window[...] = jnp.zeros_like(window)
             window[:side] = jnp.where(live, updates[part], 0.0)
+            window[side:] = jnp.zeros((total - side, side), f32)
             turned = pltpu.roll(window[...], offset, 0)
             for j in range(reach + 1):
                 piece = turned[j * strip : (j + 1) * strip]
                 if j == middle:
-                    own_out[s, part] = piece
+                    own[s, part] = piece
                 else:
-                    away_out[j, s, part] = piece.astype(bf16)
-
-
-def place_kernel(tables, field, own, away_ref, updated, out, edges, sem):
-    pieces = [away_ref.at[j] for j in range(away_ref.shape[0])]
-    pieces[(len(pieces) - 1) // 2] = own
-    width = field.shape[3]
-    cap, side = own.shape[0], own.shape[3]
-    span = side + LANES
-    out[...] = field[...]
-    pad = jnp.zeros((own.shape[2], LANES), f32)
-    for j, source in enumerate(pieces):
-        for s in range(cap):
-            column = tables[j, s, 1]
-            start = pl.multiple_of(window_start(column, width, span), LANES)
-            shift = column - start
-            angle = tables[j, s, 2]
-            for part in range(2):
-                value = jnp.concatenate([source[s, part].astype(f32), pad], 1)
-                turned = pltpu.roll(value, shift, 1)
-                out[angle, part, :, pl.ds(start, span)] = (
-                    out[angle, part, :, pl.ds(start, span)] + turned
-                )
-    strip = field.shape[2]
-    for angle in range(field.shape[0]):
+                    away[j, s, part] = piece.astype(bf16)
+        start(gives[s])
+
+    pad = jnp.zeros((strip, LANES), f32)
+
+    def shifted(source, j, s):
+        shift = tables[j, s, 1] - first_block(j, s) * LANES
         for part in range(2):
-            edges[0, angle, part] = out[angle, part, :1]
-            edges[1, angle, part] = out[angle, part, strip - 1 :]
-    copy = pltpu.make_async_copy(out, updated, sem)
-    copy.start()
-    copy.wait()
+            value = jnp.concatenate([source[part].astype(f32), pad], 1)
+            turned = pltpu.roll(value, shift, 1)
+            for lane in range(lanes):
+                placed[j, s, part, lane + 1] = turned[:, lane * LANES : (lane + 1) * LANES]
+
+    def add(items, rows):
+        def chunk(block, _):
+            for angle in range(angles):
+                found = []
+                for j, s in items:
+                    near = block - first_block(j, s)
+                    hit = (tables[j, s, 2] == angle) & (near >= 0) & (near < lanes)
+                    found.append(jnp.where(hit, near + 1, 0))
+                for part in range(2):
+                    for row in rows:
+                        value = held[angle, part, block, row]
+                        for (j, s), index in zip(items, found):
+                            value = value + placed[j, s, part, index, row]
+                        held[angle, part, block, row] = value
+            return 0
+
+        lax.fori_loop(0, blocks, chunk, 0)
+
+    for s in range(cap):
+        shifted(own.at[s], middle, s)
+    early = [(middle, s) for s in range(cap)]
+    for s in range(cap - 1):
+        arrive(gives[s])
+        for j in others:
+            shifted(landed.at[j, s], j, s)
+        early += [(j, s) for j in others]
+    add(early, [slice(0, strip)])
+    arrive(gives[cap - 1])
+    for j in others:
+        shifted(landed.at[j, cap - 1], j, cap - 1)
+    late = [(j, cap - 1) for j in others]
+    add(late, [slice(0, GROUP), slice(strip - GROUP, strip)])
+    for angle in range(angles):
+        for part in range(2):
+            for block in range(blocks):
+                where = slice(block * LANES, (block + 1) * LANES)
+                edges[0, angle, part, :, where] = held[angle, part, block, :1]
+                edges[1, angle, part, :, where] = held[angle, part, block, strip - 1 :]
+    start(borders)
+    add(late, [slice(GROUP, strip - GROUP)])
+    arrive(borders)
+    for copy, sends in started:
+        pl.when(sends)(copy.wait_send)
 
 
 def mirror(value):
@@ -433,9 +511,25 @@
 
 def forward_kernel(
     field, halo, even_hi, even_lo, odd_hi, odd_lo, local, extra,
-    out, ends, source, xeh, xel, xoh, xol,
+    updated, out, ends, source, xeh, xel, xoh, xol, sems,
 ):
-    angles, _, strip, width = field.shape
+    angles, _, strip, width = updated.shape
+    copies = [
+        pltpu.make_async_copy(
+            field.at[:, :, block],
+            updated.at[:, :, :, block * LANES : (block + 1) * LANES],
+            sems.at[block],
+        )
+        for block in range(width // LANES)
+    ]
+    for copy in copies:
+        copy.start()
+
+    def rows_of(angle, part, rows):
+        return jnp.concatenate(
+            [field[angle, part, block, rows] for block in range(width // LANES)], 1
+        )
+
     half = width // 2
     block = GROUP * 2
     columns = lax.broadcasted_iota(jnp.int32, (block, width), 1)
@@ -443,16 +537,16 @@
         for first in range(0, strip, block):
             here, up, down, left = [], [], [], []
             for part in range(2):
-                body = field[angle, part, first : first + block]
+                body = rows_of(angle, part, slice(first, first + block))
                 before = (
                     halo[0, angle, part]
                     if first == 0
-                    else field[angle, part, first - 1 : first]
+                    else rows_of(angle, part, slice(first - 1, first))
                 )
                 after = (
                     halo[1, angle, part]
                     if first + block == strip
-                    else field[angle, part, first + block : first + block + 1]
+                    else rows_of(angle, part, slice(first + block, first + block + 1))
                 )
                 here.append(body)
                 up.append(jnp.concatenate([before, body[:-1]], 0))
@@ -519,6 +613,8 @@
         return 0
 
     lax.fori_loop(0, width // LANES, scan, 0)
+    for copy in copies:
+        copy.wait()
 
 
 def inverse_kernel(
@@ -587,83 +683,64 @@
     blocks = width // LANES
     shape = jax.ShapeDtypeStruct
 
-    middle = reach // 2
-    others = [j for j in range(reach + 1) if j != middle]
-    record = jnp.concatenate(
-        [frame_table, jnp.pad(frame_count[:, None], ((0, 0), (0, 2)))]
-    )
-    moves = [(0, 0, j, j) for j in range(1, reach + 1)]
-    keep = [(0, 0, 0)]
-    if middle:
-        moves.append((1, 0, 0, middle))
-    else:
-        keep.append((1, 0, 0))
-    tables, moved = exchanged(
-        [record[None], measured[None]], [reach + 1, 1], moves, keep, 0, "tell"
-    )
-    cuts = pl.pallas_call(
-        cut_kernel,
-        out_shape=shape((reach + 1, cap, 2, strip, side), bf16),
-        in_specs=[smem, hbm],
-        out_specs=vmem,
-        scratch_shapes=[
-            pltpu.VMEM(((reach + 1) * cap, 2, strip, side + LANES), f32),
-            pltpu.SemaphoreType.DMA(((reach + 1) * cap,)),
-        ],
-        compiler_params=pltpu.CompilerParams(vmem_limit_bytes=2 * VMEM_BYTES),
-        cost_estimate=cost(2),
-        name="cut",
-    )(tables, object_field)
-    (arrived,) = exchanged(
-        [cuts], [reach + 1], [(0, j, j, middle - j) for j in others], [(0, middle, middle)], 1, "fetch"
-    )
-
-    factors = cosine_factors(width)
+    pieces = (reach + 1) * cap
     local, powers, extra = decay_tables(width, strip)
 
     def by_block(table):
         return jnp.asarray(table.reshape(-1, blocks, LANES).transpose(1, 0, 2))
 
-    cos_part, sin_part = fourier_tables(side)
-
-    own, away = pl.pallas_call(
-        frame_kernel,
+    factors = cosine_factors(width)
+    table = (reach + 1, cap, 2, strip, side)
+    held, halo, *half_tables = pl.pallas_call(
+        update_kernel,
         out_shape=[
-            shape((cap, 2, strip, side), f32),
-            shape((reach + 1, cap, 2, strip, side), bf16),
+            shape((angles, 2, blocks, strip, LANES), f32),
+            shape((2, angles, 2, 1, width), f32),
+        ]
+        + [shape((half, half), bf16)] * 4,
+        in_specs=[smem] * 2 + [hbm] * 6,
+        out_specs=[vmem] * 6,
+        scratch_shapes=[
+            pltpu.SMEM((reach + 1, cap, 3), jnp.int32),
+            pltpu.SMEM((1,), jnp.int32),
+            pltpu.VMEM(probe.shape, f32),
+            pltpu.VMEM((side, side), bf16),
+            pltpu.VMEM((side, side), bf16),
+            pltpu.VMEM(factors.shape, f32),
+            pltpu.VMEM(measured.shape, bf16),
+            pltpu.VMEM(table, bf16),
+            pltpu.VMEM(table, bf16),
+            pltpu.VMEM(table, bf16),
+            pltpu.VMEM(table, bf16),
+            pltpu.VMEM((cap, 2, strip, side), f32),
+            pltpu.VMEM((reach + 1, cap, 2, side // LANES + 2, strip, LANES), f32),
+            pltpu.VMEM(((reach + 1) * strip, side), f32),
+            pltpu.VMEM((2, angles, 2, 1, width), f32),
+            pltpu.SemaphoreType.DMA((5 + blocks,)),
+            pltpu.SemaphoreType.DMA((2, reach + 1)),
+            pltpu.SemaphoreType.DMA((2, 1)),
+            pltpu.SemaphoreType.DMA((2, cap)),
+            pltpu.SemaphoreType.DMA((2, pieces)),
+            pltpu.SemaphoreType.DMA((2, pieces)),
+            pltpu.SemaphoreType.DMA((2, 2)),
         ],
-        in_specs=[smem] + [vmem] * 5,
-        out_specs=[vmem, vmem],
-        scratch_shapes=[pltpu.VMEM(((reach + 1) * strip, side), f32)],
-        compiler_params=params(),
-        cost_estimate=cost(4),
-        name="frames",
-    )(tables, probe, moved, cos_part, sin_part, arrived)
-    (landed,) = exchanged(
-        [away], [reach + 1], [(0, j, j, j - middle) for j in others], [], 2, "give"
-    )
-
-    updated, held, edges = pl.pallas_call(
-        place_kernel,
-        out_shape=[shape(object_field.shape, f32)] * 2 + [shape((2, angles, 2, 1, width), f32)],
-        in_specs=[smem, vmem, vmem, vmem],
+        compiler_params=params(collective_id=0, has_side_effects=True),
+        cost_estimate=cost(20),
+        name="update",
+    )(frame_table, frame_count, object_field, probe, measured, *fourier_tables(side), factors)
+
+    updated, solved, ends = pl.pallas_call(
+        forward_kernel,
+        out_shape=[
+            shape(object_field.shape, f32),
+            shape((angles, strip, width), f32),
+            shape((blocks, 2 * angles, LANES), f32),
+        ],
+        in_specs=[vmem] * 8,
         out_specs=[hbm, vmem, vmem],
-        scratch_shapes=[pltpu.SemaphoreType.DMA],
-        compiler_params=params(),
-        cost_estimate=cost(3),
-        name="place",
-    )(tables, object_field, own, landed)
-    halo, *half_tables = exchanged(
-        [edges], [2], [(0, 1, 0, 1), (0, 0, 1, -1)], [], 3, "edges",
-        table_kernel, [factors], [shape((half, half), bf16)] * 4,
-    )
-
-    solved, ends = pl.pallas_call(
-        forward_kernel,
-        out_shape=[shape((angles, strip, width), f32), shape((blocks, 2 * angles, LANES), f32)],
-        in_specs=[vmem] * 8,
-        out_specs=[vmem, vmem],
-        scratch_shapes=[pltpu.VMEM((rows, width), f32)] + [pltpu.VMEM((rows, half), bf16)] * 4,
+        scratch_shapes=[pltpu.VMEM((rows, width), f32)]
+        + [pltpu.VMEM((rows, half), bf16)] * 4
+        + [pltpu.SemaphoreType.DMA((blocks,))],
         compiler_params=params(),
         cost_estimate=cost(9),
         name="forward",

time: 74.1 us -> 64.6 us (0.87)
  Pallas kernels: 68.9 us -> 55 us
  local copies, waits for them, and re-layouts: 2.72 us -> 7.9 us
    pallas_call x8 -> x2, Pallas kernels: 48.4 us -> 33.1 us  [the longest x1 23.1 us: body(): pl.pallas_call(update_kernel, out_shape=[shape((angles, 2, blocks, strip,...]
    unnamed x26 -> x22, local copies, waits for them, and re-layouts: 2.72 us -> 7.9 us
    pallas_call x1, Pallas kernels: 13.7 us -> 15.1 us  [body(): pl.pallas_call(join_kernel, out_shape=shape(ends.shape, f32), in_specs=[v...]
where the time goes in v1:
time: 64.6 us; the launch traced here: 64.3 us
  Pallas kernels  55 us (85%)
  local copies, waits for them, and re-layouts  7.9 us (12%)
  between operations  1.36 us (2%)
    pallas_call x1, Pallas kernels, body(): pl.pallas_call(update_kernel, out_shape=[shape((angles, 2, blocks, strip,...  23.1 us
    pallas_call x1, Pallas kernels, body(): pl.pallas_call(join_kernel, out_shape=shape(ends.shape, f32), in_specs=[v...  15.1 us
    pallas_call x1, Pallas kernels, body(): pl.pallas_call(forward_kernel, out_shape=[shape(object_field.shape, f32),...  10 us
    unnamed x22, local copies, waits for them, and re-layouts  7.9 us
    pallas_call x1, Pallas kernels, body(): pl.pallas_call(inverse_kernel, out_shape=shape((angles, strip, width), f3...  6.85 us

profile of v1, /device:TPU:0, one launch (start us, length us, event | category | flops | bytes accessed | tf_op | source)
XLA Modules:
  0.0 64.3 jit_solution(4482713349126817932)
XLA Ops:
  1.3 0.0 copy-start
  1.3 2.2 %copy-done = f32[2,2,128,2048]{3,2,1,0:T(8,128)S(1)} copy-done((f32[2,2,128,2048]{3,2,1,0:T(8,128)S(1)}, f32[2,2,128,2048]{3,2,1,0:T(8,128)}, u32[]{:S(2)}) %copy-start) | copy-done | bytes 4194328
  3.5 0.0 copy-start.2
  3.5 1.2 %copy-done.2 = f32[2,4,32,1024]{3,2,1,0:T(8,128)S(1)} copy-done((f32[2,4,32,1024]{3,2,1,0:T(8,128)S(1)}, f32[2,4,32,1024]{3,2,1,0:T(8,128)}, u32[]{:S(2)}) %copy-start.2) | copy-done | bytes 1048600
  4.7 0.0 copy-start.3
  4.7 1.0 %copy-done.3 = f32[2,256,256]{2,1,0:T(8,128)S(1)} copy-done((f32[2,256,256]{2,1,0:T(8,128)S(1)}, f32[2,256,256]{2,1,0:T(8,128)}, u32[]{:S(2)}) %copy-start.3) | copy-done | bytes 524312
  5.7 0.0 copy-start.5
  5.7 0.9 %copy-done.5 = bf16[2,256,256]{2,1,0:T(8,128)(2,1)S(1)} copy-done((bf16[2,256,256]{2,1,0:T(8,128)(2,1)S(1)}, bf16[2,256,256]{2,1,0:T(8,128)(2,1)}, u32[]{:S(2)}) %copy-start.5) | copy-done | bytes 262168
  6.7 0.0 copy-start.7
  6.7 0.9 %copy-done.7 = bf16[256,256]{1,0:T(8,128)(2,1)S(1)} copy-done((bf16[256,256]{1,0:T(8,128)(2,1)S(1)}, bf16[256,256]{1,0:T(8,128)(2,1)}, u32[]{:S(2)}) %copy-start.7) | copy-done | bytes 131096
  7.6 0.0 copy-start.8
  7.6 0.9 %copy-done.8 = bf16[256,256]{1,0:T(8,128)(2,1)S(1)} copy-done((bf16[256,256]{1,0:T(8,128)(2,1)S(1)}, bf16[256,256]{1,0:T(8,128)(2,1)}, u32[]{:S(2)}) %copy-start.8) | copy-done | bytes 131096
  8.5 0.0 copy-start.10
  8.5 0.7 %copy-done.10 = s32[2,3]{1,0:T(2,128)S(1)} copy-done((s32[2,3]{1,0:T(2,128)S(1)}, s32[2,3]{1,0:T(2,128)}, u32[]{:S(2)}) %copy-start.10) | copy-done | bytes 48
  9.2 0.0 copy-start.1
  9.2 0.0 copy-start.4
  9.2 23.1 %update.1 = (f32[2,2,16,128,128]{4,3,2,1,0:T(8,128)S(1)}, f32[2,2,2,1,2048]{4,3,2,1,0:T(1,128)S(1)}, bf16[1024,1024]{1,0:T(8,128)(2,1)S(1)}, bf16[1024,1024]{1,0...) custom-call(s32[2,3]{1,0:T(2,128)S(1)} %copy-done.10, s32[1]{0:T(128)S(6)} %copy.14.frame_count, ...), custom_call_target="tpu_custom_call" | custom-call | bytes 60000000 | tf_op jit(solution)/shard_map/update/pallas_call | solution.py:694
  32.3 0.0 copy-done.1
  32.3 0.0 copy-done.4
  32.3 0.0 copy-start.6
  32.3 0.0 copy-start.9
  32.3 10.0 %forward.1 = (f32[2,2,128,2048]{3,2,1,0:T(8,128)}, f32[2,128,2048]{2,1,0:T(8,128)S(1)}, f32[16,4,128]{2,1,0:T(4,128)S(1)}) custom-call(f32[2,2,16,128,128]{4,3,2,1,0:T(8,128)S(1)} %get-tuple-element.11.field, f32[2,2,2,1,2048]{4,3,2,1,0:T(1,128)S(1)} %get-tuple-element.12.halo, bf16[1024,1024]{1,0:T(8,128)(2,1)S(1)} %get-tuple-element.13.even_hi, ...), custom_call_target="tpu_custom_call" | custom-call | bytes 27000000 | tf_op jit(solution)/shard_map/forward/pallas_call | solution.py:732
  42.4 0.0 copy-done.6
  42.4 0.0 copy-done.9
  42.4 15.1 %join.1.incoming = f32[16,4,128]{2,1,0:T(4,128)S(1)} custom-call(f32[16,4,128]{2,1,0:T(4,128)S(1)} %get-tuple-element.19.ends, f32[16,17,128]{2,1,0:T(8,128)S(1)} %copy-done.6, f32[16,8,128]{2,1,0:T(8,128)S(1)} %copy-done.9), custom_call_target="tpu_custom_call" | custom-call | bytes 30000000 | tf_op jit(solution)/shard_map/join/pallas_call | solution.py:748
  57.5 6.8 %inverse.1 = f32[2,128,2048]{2,1,0:T(8,128)} custom-call(f32[2,128,2048]{2,1,0:T(8,128)S(1)} %get-tuple-element.18.value, f32[16,4,128]{2,1,0:T(4,128)S(1)} %join.1.incoming, bf16[1024,1024]{1,0:T(8,128)(2,1)S(1)} %get-tuple-element.13.even_hi, bf16[1024,1024]{1,0:T(8,128)(2,1)S(1)} %get-tuple-element.14.even_lo, ...), custom_call_target="tpu_custom_call" | custom-call | bytes 18000000 | tf_op jit(solution)/shard_map/inverse/pallas_call | solution.py:765
Async XLA Ops:
  1.3 2.2 %copy-start = (f32[2,2,128,2048]{3,2,1,0:T(8,128)S(1)}, f32[2,2,128,2048]{3,2,1,0:T(8,128)}, u32[]{:S(2)}) copy-start(f32[2,2,128,2048]{3,2,1,0:T(8,128)} %field.1) | copy-start | bytes 12582916
  3.5 1.2 %copy-start.2 = (f32[2,4,32,1024]{3,2,1,0:T(8,128)S(1)}, f32[2,4,32,1024]{3,2,1,0:T(8,128)}, u32[]{:S(2)}) copy-start(f32[2,4,32,1024]{3,2,1,0:T(8,128)} %constant.14.clone.factors_in) | copy-start | bytes 3145732
  4.7 1.0 %copy-start.3 = (f32[2,256,256]{2,1,0:T(8,128)S(1)}, f32[2,256,256]{2,1,0:T(8,128)}, u32[]{:S(2)}) copy-start(f32[2,256,256]{2,1,0:T(8,128)} %probe_in.1) | copy-start | bytes 1572868
  5.7 0.9 %copy-start.5 = (bf16[2,256,256]{2,1,0:T(8,128)(2,1)S(1)}, bf16[2,256,256]{2,1,0:T(8,128)(2,1)}, u32[]{:S(2)}) copy-start(bf16[2,256,256]{2,1,0:T(8,128)(2,1)} %measured.1) | copy-start | bytes 786436
  6.7 0.9 %copy-start.7 = (bf16[256,256]{1,0:T(8,128)(2,1)S(1)}, bf16[256,256]{1,0:T(8,128)(2,1)}, u32[]{:S(2)}) copy-start(bf16[256,256]{1,0:T(8,128)(2,1)} %constant.25.sin_in) | copy-start | bytes 393220
  7.6 0.9 %copy-start.8 = (bf16[256,256]{1,0:T(8,128)(2,1)S(1)}, bf16[256,256]{1,0:T(8,128)(2,1)}, u32[]{:S(2)}) copy-start(bf16[256,256]{1,0:T(8,128)(2,1)} %constant.24.cos_in) | copy-start | bytes 393220
  8.5 0.7 %copy-start.10 = (s32[2,3]{1,0:T(2,128)S(1)}, s32[2,3]{1,0:T(2,128)}, u32[]{:S(2)}) copy-start(s32[2,3]{1,0:T(2,128)} %frame_table.1) | copy-start | bytes 76
  9.2 23.1 %copy-start.1 = (f32[8,8,2048]{2,1,0:T(8,128)S(1)}, f32[8,8,2048]{2,1,0:T(8,128)}, u32[]{:S(2)}) copy-start(f32[8,8,2048]{2,1,0:T(8,128)} %constant.17.clone.local) | copy-start | bytes 1572868
  9.2 23.1 %copy-start.4 = (f32[8,2048]{1,0:T(8,128)S(1)}, f32[8,2048]{1,0:T(8,128)}, u32[]{:S(2)}) copy-start(f32[8,2048]{1,0:T(8,128)} %constant.18.clone.extra) | copy-start | bytes 196612
  32.3 10.1 %copy-start.6 = (f32[16,17,128]{2,1,0:T(8,128)S(1)}, f32[16,17,128]{2,1,0:T(8,128)}, u32[]{:S(2)}) copy-start(f32[16,17,128]{2,1,0:T(8,128)} %constant.19.clone.powers) | copy-start | bytes 417796
  32.3 10.0 %copy-start.9 = (f32[16,8,128]{2,1,0:T(8,128)S(1)}, f32[16,8,128]{2,1,0:T(8,128)}, u32[]{:S(2)}) copy-start(f32[16,8,128]{2,1,0:T(8,128)} %constant.20.clone.extra) | copy-start | bytes 196612

commit v2 on v1

--- a/solution.py
+++ b/solution.py
@@ -219,7 +219,7 @@
 
 
 def update_kernel(
-    frame_table, frame_count, field, probe_in, measured, cos_in, sin_in, factors_in,
+    frame_count, frame_table, field, probe_in, measured, cos_in, sin_in, factors_in,
     held, halo, even_hi, even_lo, odd_hi, odd_lo,
     tables, counts, probe, cos_ref, sin_ref, factors, moved, cuts, arrived, away, landed,
     own, placed, window, edges,
@@ -254,9 +254,8 @@
         load(5 + block, field.at[:, :, :, block * LANES : (block + 1) * LANES], held.at[:, :, block])
         for block in range(blocks)
     ]
-    for item in loads[:2] + strips + loads[2:]:
+    for item in loads[:2] + strips + loads[2:5]:
         item.start()
-    loads[0].wait()
 
     def send(source, target, sems, index, by):
         copy = pltpu.make_async_remote_copy(
@@ -330,6 +329,7 @@
     def wipe(ref, *first):
         ref[first] = jnp.zeros(ref.shape[len(first):], ref.dtype)
 
+    loads[0].wait()
     start(tells)
     start(moves)
     blank(tells, wipe_table)
@@ -698,7 +698,7 @@
             shape((2, angles, 2, 1, width), f32),
         ]
         + [shape((half, half), bf16)] * 4,
-        in_specs=[smem] * 2 + [hbm] * 6,
+        in_specs=[smem] + [hbm] * 7,
         out_specs=[vmem] * 6,
         scratch_shapes=[
             pltpu.SMEM((reach + 1, cap, 3), jnp.int32),
@@ -727,7 +727,20 @@
         compiler_params=params(collective_id=0, has_side_effects=True),
         cost_estimate=cost(20),
         name="update",
-    )(frame_table, frame_count, object_field, probe, measured, *fourier_tables(side), factors)
+    )(
+        frame_count,
+        *[
+            pltpu.with_memory_space_constraint(item, pltpu.HBM)
+            for item in (
+                frame_table,
+                object_field,
+                probe,
+                measured,
+                *fourier_tables(side),
+                factors,
+            )
+        ],
+    )
 
     updated, solved, ends = pl.pallas_call(
         forward_kernel,

time: 64.6 us -> 55.1 us (0.85)
  local copies, waits for them, and re-layouts: 7.9 us -> 0.03 us
  Pallas kernels: 55 us -> 53.5 us
    unnamed x22 -> x8, local copies, waits for them, and re-layouts: 7.9 us -> 0.03 us
    pallas_call x1, Pallas kernels: 23.1 us -> 21.9 us  [body(): pl.pallas_call(update_kernel, out_shape=[shape((angles, 2, blocks, strip,...]
where the time goes in v2:
time: 55.1 us; the launch traced here: 54.9 us
  Pallas kernels  53.5 us (97%)
  between operations  1.36 us (2%)
    pallas_call x1, Pallas kernels, body(): pl.pallas_call(update_kernel, out_shape=[shape((angles, 2, blocks, strip,...  21.9 us
    pallas_call x1, Pallas kernels, body(): pl.pallas_call(join_kernel, out_shape=shape(ends.shape, f32), in_specs=[v...  15.1 us
    pallas_call x1, Pallas kernels, body(): pl.pallas_call(forward_kernel, out_shape=[shape(object_field.shape, f32),...  9.76 us
    pallas_call x1, Pallas kernels, body(): pl.pallas_call(inverse_kernel, out_shape=shape((angles, strip, width), f3...  6.83 us

profile of v2, /device:TPU:0, one launch (start us, length us, event | category | flops | bytes accessed | tf_op | source)
XLA Modules:
  0.0 54.9 jit_solution(13985406118897242608)
XLA Ops:
  1.3 0.0 copy-start
  1.3 0.0 copy-start.1
  1.3 21.9 %update.1 = (f32[2,2,16,128,128]{4,3,2,1,0:T(8,128)S(1)}, f32[2,2,2,1,2048]{4,3,2,1,0:T(1,128)S(1)}, bf16[1024,1024]{1,0:T(8,128)(2,1)S(1)}, bf16[1024,1024]{1,0...) custom-call(s32[1]{0:T(128)S(6)} %copy.14.frame_count, s32[2,3]{1,0:T(2,128)} %frame_table.1, ...), custom_call_target="tpu_custom_call" | custom-call | bytes 60000000 | tf_op jit(solution)/shard_map/update/pallas_call | solution.py:694
  23.2 0.0 copy-done
  23.2 0.0 copy-done.1
  23.2 0.0 copy-start.2
  23.2 0.0 copy-start.3
  23.2 9.8 %forward.1 = (f32[2,2,128,2048]{3,2,1,0:T(8,128)}, f32[2,128,2048]{2,1,0:T(8,128)S(1)}, f32[16,4,128]{2,1,0:T(4,128)S(1)}) custom-call(f32[2,2,16,128,128]{4,3,2,1,0:T(8,128)S(1)} %get-tuple-element.11.field, f32[2,2,2,1,2048]{4,3,2,1,0:T(1,128)S(1)} %get-tuple-element.12.halo, bf16[1024,1024]{1,0:T(8,128)(2,1)S(1)} %get-tuple-element.13.even_hi, ...), custom_call_target="tpu_custom_call" | custom-call | bytes 27000000 | tf_op jit(solution)/shard_map/forward/pallas_call | solution.py:745
  33.0 0.0 copy-done.2
  33.0 0.0 copy-done.3
  33.0 15.1 %join.1.incoming = f32[16,4,128]{2,1,0:T(4,128)S(1)} custom-call(f32[16,4,128]{2,1,0:T(4,128)S(1)} %get-tuple-element.19.ends, f32[16,17,128]{2,1,0:T(8,128)S(1)} %copy-done.2, f32[16,8,128]{2,1,0:T(8,128)S(1)} %copy-done.3), custom_call_target="tpu_custom_call" | custom-call | bytes 30000000 | tf_op jit(solution)/shard_map/join/pallas_call | solution.py:761
  48.1 6.8 %inverse.1 = f32[2,128,2048]{2,1,0:T(8,128)} custom-call(f32[2,128,2048]{2,1,0:T(8,128)S(1)} %get-tuple-element.18.value, f32[16,4,128]{2,1,0:T(4,128)S(1)} %join.1.incoming, bf16[1024,1024]{1,0:T(8,128)(2,1)S(1)} %get-tuple-element.13.even_hi, bf16[1024,1024]{1,0:T(8,128)(2,1)S(1)} %get-tuple-element.14.even_lo, ...), custom_call_target="tpu_custom_call" | custom-call | bytes 18000000 | tf_op jit(solution)/shard_map/inverse/pallas_call | solution.py:778
Async XLA Ops:
  1.3 21.9 %copy-start = (f32[8,8,2048]{2,1,0:T(8,128)S(1)}, f32[8,8,2048]{2,1,0:T(8,128)}, u32[]{:S(2)}) copy-start(f32[8,8,2048]{2,1,0:T(8,128)} %constant.17.clone.local) | copy-start | bytes 1572868
  1.3 21.9 %copy-start.1 = (f32[8,2048]{1,0:T(8,128)S(1)}, f32[8,2048]{1,0:T(8,128)}, u32[]{:S(2)}) copy-start(f32[8,2048]{1,0:T(8,128)} %constant.18.clone.extra) | copy-start | bytes 196612
  23.2 9.8 %copy-start.2 = (f32[16,17,128]{2,1,0:T(8,128)S(1)}, f32[16,17,128]{2,1,0:T(8,128)}, u32[]{:S(2)}) copy-start(f32[16,17,128]{2,1,0:T(8,128)} %constant.19.clone.powers) | copy-start | bytes 417796
  23.2 9.8 %copy-start.3 = (f32[16,8,128]{2,1,0:T(8,128)S(1)}, f32[16,8,128]{2,1,0:T(8,128)}, u32[]{:S(2)}) copy-start(f32[16,8,128]{2,1,0:T(8,128)} %constant.20.clone.extra) | copy-start | bytes 196612

commit v3 on v2

--- a/solution.py
+++ b/solution.py
@@ -181,20 +181,16 @@
     freqs = np.concatenate([2 * np.arange(half), 2 * np.arange(half) + 1]).astype(np.float64)
     shift = screen_term + 2.0 - 2.0 * np.cos(freqs * math.pi / grid_side)
     rate = 2.0 * np.arcsinh(np.sqrt(shift) / 2.0)
-    gain = 1.0 / (2.0 * np.sinh(rate))
-    rows = np.arange(GROUP)[:, None]
-    down = [np.where(rows >= s, np.exp(-s * rate), 0.0) for s in (1, 2, 4)]
-    up = [np.where(rows < GROUP - s, np.exp(-s * rate), 0.0) for s in (1, 2, 4)]
-    down.append(np.exp(-(rows + 1) * rate))
-    up.append(np.exp(-(GROUP - rows) * rate))
-    local = np.stack(down + up)
+    gain = 2.0 / (2.0 * np.sinh(rate))
+    groups = strip_rows // GROUP
+    segments = np.exp(-groups * np.arange(GROUP)[:, None] * rate)
+    steps = np.exp(-(np.arange(groups)[:, None] + 1) * rate)
+    jumps = np.exp(-groups * np.array([[1], [2], [4]]) * rate)
+    decays = np.concatenate([segments, segments[::-1], gain[None], jumps, steps])
     strips = grid_side // strip_rows
     powers = np.exp(-strip_rows * np.arange(strips + 1)[:, None] * rate)
-    extra = np.stack(
-        [gain, 1.0 / (1.0 - np.exp(-2.0 * grid_side * rate)), np.exp(-GROUP * rate)]
-        + [rate * 0.0] * 5
-    )
-    return local.astype(np.float32), powers.astype(np.float32), extra.astype(np.float32)
+    extra = np.stack([gain, 1.0 / (1.0 - np.exp(-2.0 * grid_side * rate))])
+    return decays.astype(np.float32), powers.astype(np.float32), extra.astype(np.float32)
 
 
 def table_rows(factors, part, high, low):
@@ -488,13 +484,11 @@
     rows = lax.broadcasted_iota(jnp.int32, (side, side), 0)
     columns = lax.broadcasted_iota(jnp.int32, (side, side), 1)
     swap = jnp.where(rows + columns == side - 1, 1.0, 0.0).astype(bf16)
-    total = None
-    for _ in range(3):
-        piece = value.astype(bf16)
-        value = value - piece.astype(f32)
-        term = jnp.dot(piece, swap, preferred_element_type=f32)
-        total = term if total is None else total + term
-    return total
+    high = value.astype(bf16)
+    low = (value - high.astype(f32)).astype(bf16)
+    return jnp.dot(high, swap, preferred_element_type=f32) + jnp.dot(
+        low, swap, preferred_element_type=f32
+    )
 
 
 def split_store(value, high, low, columns):
@@ -503,146 +497,217 @@
     low[:, columns] = (value - rounded.astype(f32)).astype(bf16)
 
 
-def bond(a_re, a_im, b_re, b_im):
-    cross = a_re * b_im - a_im * b_re
-    power = a_re * a_re + a_im * a_im + b_re * b_re + b_im * b_im + soften_term
-    return 2.0 * cross / power
+def power_of(re, im):
+    return re * re + im * im + 0.5 * soften_term
+
+
+def half_bond(first, second):
+    cross = first[0] * second[1] - first[1] * second[0]
+    return cross / (first[2] + second[2])
 
 
 def forward_kernel(
-    field, halo, even_hi, even_lo, odd_hi, odd_lo, local, extra,
-    updated, out, ends, source, xeh, xel, xoh, xol, sems,
+    field, halo, even_hi, even_lo, odd_hi, odd_lo, decays,
+    updated, out, carries, ends, source, xeh, xel, xoh, xol, coefs, power, drops, shifts, bonds, partial, afters, sems,
 ):
-    angles, _, strip, width = updated.shape
+    angles, _, blocks, strip, _ = field.shape
+    width = blocks * LANES
+    groups = strip // GROUP
     copies = [
         pltpu.make_async_copy(
             field.at[:, :, block],
             updated.at[:, :, :, block * LANES : (block + 1) * LANES],
             sems.at[block],
         )
-        for block in range(width // LANES)
+        for block in range(blocks)
     ]
     for copy in copies:
         copy.start()
-
-    def rows_of(angle, part, rows):
-        return jnp.concatenate(
-            [field[angle, part, block, rows] for block in range(width // LANES)], 1
-        )
+    lane = lax.broadcasted_iota(jnp.int32, (GROUP, LANES), 1)
+    segment = lax.broadcasted_iota(jnp.int32, (GROUP, LANES), 0)
+
+    for angle in range(angles):
+
+        def rows_of(group):
+            return slice(group * GROUP, (group + 1) * GROUP)
+
+        def prepare(block, slot):
+            for group in range(groups):
+                pair = [field[angle, part, block, rows_of(group)] for part in range(2)]
+                power[slot, rows_of(group)] = power_of(*pair)
+                for part, value in enumerate(pair):
+                    shifts[slot, part, group] = pltpu.roll(value, 1, 1)
+
+        def combine(block, slot):
+            where = pl.ds(pl.multiple_of(block * LANES, LANES), LANES)
+
+            def beyond(upper):
+                edge, by, border = (0, 1, 0) if upper else (GROUP - 1, GROUP - 1, 1)
+                pair = [
+                    jnp.where(
+                        segment == edge,
+                        halo[border, angle, part, :, where],
+                        pltpu.roll(field[angle, part, block, rows_of(0 if upper else groups - 1)], by, 0),
+                    )
+                    for part in range(2)
+                ]
+                return pair + [power_of(*pair)]
+
+            for group in range(groups):
+                here = [field[angle, part, block, rows_of(group)] for part in range(2)]
+                here.append(power[slot, rows_of(group)])
+                if group == 0:
+                    drops[GROUP - 1 : 2 * GROUP - 1] = half_bond(beyond(True), here)
+                if group == groups - 1:
+                    below = beyond(False)
+                else:
+                    lower = slice(group * GROUP + 1, (group + 1) * GROUP + 1)
+                    below = [field[angle, part, block, lower] for part in range(2)]
+                    below.append(power[slot, lower])
+                down = half_bond(here, below)
+                first = (group + 1) * GROUP
+                drops[first : first + GROUP] = down
+                up = drops[first - 1 : first - 1 + GROUP]
+                left = [
+                    jnp.where(lane == 0, shifts[1 - slot, part, group], shifts[slot, part, group])
+                    for part in range(2)
+                ]
+                bond = half_bond(left + [power_of(*left)], here)
+                bonds[slot, group] = bond
+                partial[slot, group] = up - down + bond
+
+        def finish(block, slot):
+            behind = pl.ds(pl.multiple_of(jnp.maximum(block - 1, 0) * LANES, LANES), LANES)
+            for group in range(groups):
+                after = pltpu.roll(bonds[slot, group], LANES - 1, 1)
+                first = angle * strip + group * GROUP
+                source[first : first + GROUP, behind] = partial[1 - slot, group] - jnp.where(
+                    lane == LANES - 1, after, afters[group]
+                )
+                afters[group] = after
+
+        def step(pair, _):
+            block = 2 * pair
+            finish(block - 1, 1)
+            combine(block, 0)
+            prepare(block + 1, 1)
+            finish(block, 0)
+            combine(block + 1, 1)
+            prepare(jnp.minimum(block + 2, blocks - 1), 0)
+            return 0
+
+        for group in range(groups):
+            for part in range(2):
+                shifts[1, part, group] = jnp.zeros((GROUP, LANES), f32)
+        prepare(0, 0)
+        lax.fori_loop(0, blocks // 2, step, 0)
+        finish(blocks - 1, 1)
+        for group in range(groups):
+            first = angle * strip + group * GROUP
+            source[first : first + GROUP, width - LANES :] = partial[1, group] - jnp.where(
+                lane == LANES - 1, 0.0, afters[group]
+            )
 
     half = width // 2
-    block = GROUP * 2
-    columns = lax.broadcasted_iota(jnp.int32, (block, width), 1)
-    for angle in range(angles):
-        for first in range(0, strip, block):
-            here, up, down, left = [], [], [], []
-            for part in range(2):
-                body = rows_of(angle, part, slice(first, first + block))
-                before = (
-                    halo[0, angle, part]
-                    if first == 0
-                    else rows_of(angle, part, slice(first - 1, first))
-                )
-                after = (
-                    halo[1, angle, part]
-                    if first + block == strip
-                    else rows_of(angle, part, slice(first + block, first + block + 1))
-                )
-                here.append(body)
-                up.append(jnp.concatenate([before, body[:-1]], 0))
-                down.append(jnp.concatenate([body[1:], after], 0))
-                left.append(jnp.where(columns == 0, 0.0, pltpu.roll(body, 1, 1)))
-            row_up = bond(*up, *here)
-            row_down = bond(*here, *down)
-            col_left = bond(*left, *here)
-            col_right = jnp.where(
-                columns == width - 1, 0.0, pltpu.roll(col_left, width - 1, 1)
-            )
-            source[angle * strip + first : angle * strip + first + block] = -(
-                row_down - row_up + col_right - col_left
-            )
-    for first in range(0, half, TILE):
-        near = source[:, first : first + TILE]
-        far = mirror(source[:, width - first - TILE : width - first])
-        where = slice(first, first + TILE)
+
+    def tile(index):
+        return pl.ds(pl.multiple_of(index * TILE, TILE), TILE)
+
+    def fold(index, _):
+        where = tile(index)
+        near = source[:, where]
+        far = mirror(source[:, tile(width // TILE - 1 - index)])
         split_store(near + far, xeh, xel, where)
         split_store(near - far, xoh, xol, where)
+        return 0
+
+    lax.fori_loop(0, half // TILE, fold, 0)
     for base, high, low, table_hi, table_lo in (
         (0, xeh, xel, even_hi, even_lo),
         (half, xoh, xol, odd_hi, odd_lo),
     ):
-        for first in range(0, half, TILE):
-            where = slice(first, first + TILE)
-            source[:, base + first : base + first + TILE] = (
+
+        def transform(index, _):
+            where = tile(index)
+            value = (
                 jnp.dot(high[...], table_hi[:, where], preferred_element_type=f32)
                 + jnp.dot(low[...], table_hi[:, where], preferred_element_type=f32)
                 + jnp.dot(high[...], table_lo[:, where], preferred_element_type=f32)
             )
-    groups = strip // GROUP
+            for column in range(TILE // LANES):
+                block = (base + index * TILE) // LANES + column
+                coefs[block] = value[:, column * LANES : (column + 1) * LANES]
+            return 0
+
+        lax.fori_loop(0, half // TILE, transform, 0)
 
     def scan(chunk, _):
         where = pl.ds(pl.multiple_of(chunk * LANES, LANES), LANES)
-        gain = extra[0:1, where]
+        gain = decays[2 * GROUP : 2 * GROUP + 1, where]
+        step = decays[2 * GROUP + 4 : 2 * GROUP + 5, where]
         for angle in range(angles):
-            value = source[angle * strip : (angle + 1) * strip, where]
-            value = value.reshape(groups, GROUP, LANES)
-            fall, rise = value, value
+            values = [
+                coefs[chunk, pl.ds(angle * strip + group, GROUP, stride=groups)]
+                for group in range(groups)
+            ]
+            fall, falls = values[0], [values[0]]
+            for group in range(1, groups):
+                fall = values[group] + step * fall
+                falls.append(fall)
+            rise = values[-1]
+            for group in reversed(range(groups)):
+                total = falls[group]
+                if group < groups - 1:
+                    later = step * rise
+                    total = total + later
+                    rise = values[group] + later
+                out[angle, group * GROUP : (group + 1) * GROUP, where] = gain * total
             for index, by in enumerate((1, 2, 4)):
-                fall = fall + local[index, :, where][None] * pltpu.roll(fall, by, 1)
-                rise = rise + local[4 + index, :, where][None] * pltpu.roll(rise, GROUP - by, 1)
-            falls, carry = [], None
-            for group in range(groups):
-                item = fall[group]
-                if carry is not None:
-                    item = item + local[3, :, where] * carry
-                carry = item[GROUP - 1 :]
-                falls.append(item)
-            ends[chunk, angle : angle + 1] = carry
-            rises, carry = [None] * groups, None
-            for group in reversed(range(groups)):
-                item = rise[group]
-                if carry is not None:
-                    item = item + local[7, :, where] * carry
-                carry = item[:1]
-                rises[group] = item
-            ends[chunk, angles + angle : angles + angle + 1] = carry
-            for group in range(groups):
-                out[angle, group * GROUP : (group + 1) * GROUP, where] = gain * (
-                    falls[group] + rises[group] - value[group]
-                )
+                jump = decays[2 * GROUP + 1 + index : 2 * GROUP + 2 + index, where]
+                fall = fall + jnp.where(segment >= by, pltpu.roll(fall, by, 0), 0.0) * jump
+                rise = rise + jnp.where(segment < GROUP - by, pltpu.roll(rise, GROUP - by, 0), 0.0) * jump
+            ends[chunk, angle : angle + 1] = fall[GROUP - 1 :]
+            ends[chunk, angles + angle : angles + angle + 1] = rise[:1]
+            carries[chunk, angle] = gain * jnp.where(segment >= 1, pltpu.roll(fall, 1, 0), 0.0)
+            carries[chunk, angles + angle] = gain * jnp.where(
+                segment < GROUP - 1, pltpu.roll(rise, GROUP - 1, 0), 0.0
+            )
         return 0
 
-    lax.fori_loop(0, width // LANES, scan, 0)
+    lax.fori_loop(0, blocks, scan, 0, unroll=2)
     for copy in copies:
         copy.wait()
 
 
 def inverse_kernel(
-    value, incoming, even_hi, even_lo, odd_hi, odd_lo, local, extra, out, xh, xl
+    value, carries, incoming, even_hi, even_lo, odd_hi, odd_lo, decays, out, xh, xl, parted, sems
 ):
     angles, strip, width = value.shape
     half = width // 2
     groups = strip // GROUP
+    blocks = width // LANES
 
     def enter(chunk, _):
         where = pl.ds(pl.multiple_of(chunk * LANES, LANES), LANES)
         for angle in range(angles):
-            fall = incoming[chunk, angle : angle + 1]
-            rise = incoming[chunk, angles + angle : angles + angle + 1]
-            step = extra[2:3, where]
-            falls, rises = [], []
-            for group in range(groups):
-                falls.append(fall)
-                rises.append(rise)
-                fall = fall * step
-                rise = rise * step
+            fall = (
+                carries[chunk, angle]
+                + decays[:GROUP, where] * incoming[chunk, angle : angle + 1]
+            )
+            rise = (
+                carries[chunk, angles + angle]
+                + decays[GROUP : 2 * GROUP, where]
+                * incoming[chunk, angles + angle : angles + angle + 1]
+            )
             for pair in range(0, groups, 2):
                 rows = []
                 for group in (pair, pair + 1):
+                    ahead = 2 * GROUP + 4 + group
+                    behind = 2 * GROUP + 4 + groups - 1 - group
                     rows.append(
                         value[angle, group * GROUP : (group + 1) * GROUP, where]
-                        + local[3, :, where] * falls[group]
-                        + local[7, :, where] * rises[groups - 1 - group]
+                        + decays[ahead : ahead + 1, where] * fall
+                        + decays[behind : behind + 1, where] * rise
                     )
                 item = jnp.concatenate(rows, 0)
                 rounded = item.astype(bf16)
@@ -651,8 +716,9 @@
                 xl[start : start + 2 * GROUP, where] = (item - rounded.astype(f32)).astype(bf16)
         return 0
 
-    lax.fori_loop(0, width // LANES, enter, 0)
+    lax.fori_loop(0, blocks, enter, 0)
     last = (((1,), (1,)), ((), ()))
+    copies = []
     for first in range(0, half, TILE):
         where = slice(first, first + TILE)
         parts = []
@@ -666,10 +732,24 @@
             )
         near = parts[0] + parts[1]
         far = mirror(parts[0] - parts[1])
-        for angle in range(angles):
-            rows = slice(angle * strip, (angle + 1) * strip)
-            out[angle, :, where] = near[rows]
-            out[angle, :, width - first - TILE : width - first] = far[rows]
+        for item, start in ((near, first), (far, width - first - TILE)):
+            for column in range(0, TILE, LANES):
+                block = (start + column) // LANES
+                for angle in range(angles):
+                    for group in range(groups):
+                        row = angle * strip + group * GROUP
+                        parted[angle, block, pl.ds(group, GROUP, stride=groups)] = item[
+                            row : row + GROUP, column : column + LANES
+                        ]
+                copy = pltpu.make_async_copy(
+                    parted.at[:, block],
+                    out.at[:, :, block * LANES : (block + 1) * LANES],
+                    sems.at[block],
+                )
+                copy.start()
+                copies.append(copy)
+    for copy in copies:
+        copy.wait()
 
 
 def body(object_field, probe, measured, frame_table, frame_count):
@@ -684,7 +764,7 @@
     shape = jax.ShapeDtypeStruct
 
     pieces = (reach + 1) * cap
-    local, powers, extra = decay_tables(width, strip)
+    decays, powers, extra = decay_tables(width, strip)
 
     def by_block(table):
         return jnp.asarray(table.reshape(-1, blocks, LANES).transpose(1, 0, 2))
@@ -742,22 +822,32 @@
         ],
     )
 
-    updated, solved, ends = pl.pallas_call(
+    updated, solved, carries, ends = pl.pallas_call(
         forward_kernel,
         out_shape=[
             shape(object_field.shape, f32),
             shape((angles, strip, width), f32),
+            shape((blocks, 2 * angles, GROUP, LANES), f32),
             shape((blocks, 2 * angles, LANES), f32),
         ],
-        in_specs=[vmem] * 8,
-        out_specs=[hbm, vmem, vmem],
+        in_specs=[vmem] * 7,
+        out_specs=[hbm, vmem, vmem, vmem],
         scratch_shapes=[pltpu.VMEM((rows, width), f32)]
         + [pltpu.VMEM((rows, half), bf16)] * 4
+        + [
+            pltpu.VMEM((blocks, rows, LANES), f32),
+            pltpu.VMEM((2, strip, LANES), f32),
+            pltpu.VMEM((strip + GROUP, LANES), f32),
+            pltpu.VMEM((2, 2, strip // GROUP, GROUP, LANES), f32),
+            pltpu.VMEM((2, strip // GROUP, GROUP, LANES), f32),
+            pltpu.VMEM((2, strip // GROUP, GROUP, LANES), f32),
+            pltpu.VMEM((strip // GROUP, GROUP, LANES), f32),
+        ]
         + [pltpu.SemaphoreType.DMA((blocks,))],
         compiler_params=params(),
         cost_estimate=cost(9),
         name="forward",
-    )(held, halo, *half_tables, local, extra)
+    )(held, halo, *half_tables, decays)
     incoming = pl.pallas_call(
         join_kernel,
         out_shape=shape(ends.shape, f32),
@@ -779,15 +869,17 @@
         inverse_kernel,
         out_shape=shape((angles, strip, width), f32),
         in_specs=[vmem] * 8,
-        out_specs=vmem,
+        out_specs=hbm,
         scratch_shapes=[
             pltpu.VMEM((rows, width), bf16),
             pltpu.VMEM((rows, width), bf16),
+            pltpu.VMEM((angles, blocks, strip, LANES), f32),
+            pltpu.SemaphoreType.DMA((blocks,)),
         ],
         compiler_params=params(),
         cost_estimate=cost(6),
         name="inverse",
-    )(solved, incoming, *half_tables, local, extra)
+    )(solved, carries, incoming, *half_tables, decays)
     return (updated, phase_map)
 
 

time: 55.1 us -> 55.3 us (level)
    pallas_call x1, Pallas kernels: 9.76 us -> 10.4 us  [body(): pl.pallas_call(forward_kernel, out_shape=[shape(object_field.shape, f32),...]
where the time goes in v3:
time: 55.3 us; the launch traced here: 55.2 us
  Pallas kernels  53.8 us (97%)
  between operations  1.35 us (2%)
    pallas_call x1, Pallas kernels, body(): pl.pallas_call(update_kernel, out_shape=[shape((angles, 2, blocks, strip,...  21.7 us
    pallas_call x1, Pallas kernels, body(): pl.pallas_call(join_kernel, out_shape=shape(ends.shape, f32), in_specs=[v...  15.1 us
    pallas_call x1, Pallas kernels, body(): pl.pallas_call(forward_kernel, out_shape=[shape(object_field.shape, f32),...  10.4 us
    pallas_call x1, Pallas kernels, body(): pl.pallas_call(inverse_kernel, out_shape=shape((angles, strip, width), f3...  6.61 us

profile of v3, /device:TPU:0, one launch (start us, length us, event | category | flops | bytes accessed | tf_op | source)
XLA Modules:
  0.0 55.2 jit_solution(16712571693139660351)
XLA Ops:
  1.3 0.0 copy-start
  1.3 21.7 %update.1 = (f32[2,2,16,128,128]{4,3,2,1,0:T(8,128)S(1)}, f32[2,2,2,1,2048]{4,3,2,1,0:T(1,128)S(1)}, bf16[1024,1024]{1,0:T(8,128)(2,1)S(1)}, bf16[1024,1024]{1,0...) custom-call(s32[1]{0:T(128)S(6)} %copy.13.frame_count, s32[2,3]{1,0:T(2,128)} %frame_table.1, ...), custom_call_target="tpu_custom_call" | custom-call | bytes 60000000 | tf_op jit(solution)/shard_map/update/pallas_call | solution.py:774
  23.0 0.0 copy-done
  23.0 0.0 copy-start.1
  23.0 0.0 copy-start.2
  23.0 10.4 %forward.1 = (f32[2,2,128,2048]{3,2,1,0:T(8,128)}, f32[2,128,2048]{2,1,0:T(8,128)S(1)}, f32[16,4,8,128]{3,2,1,0:T(8,128)S(1)}, f32[16,4,128]{2,1,0:T(4,128)S(1)}) custom-call(f32[2,2,16,128,128]{4,3,2,1,0:T(8,128)S(1)} %get-tuple-element.12.field, f32[2,2,2,1,2048]{4,3,2,1,0:T(1,128)S(1)} %get-tuple-element.13.halo, ...), custom_call_target="tpu_custom_call" | custom-call | bytes 27000000 | tf_op jit(solution)/shard_map/forward/pallas_call | solution.py:825
  33.5 0.0 copy-done.1
  33.5 0.0 copy-done.2
  33.5 15.1 %join.1.incoming = f32[16,4,128]{2,1,0:T(4,128)S(1)} custom-call(f32[16,4,128]{2,1,0:T(4,128)S(1)} %get-tuple-element.21.ends, f32[16,17,128]{2,1,0:T(8,128)S(1)} %copy-done.1, f32[16,2,128]{2,1,0:T(2,128)S(1)} %copy-done.2), custom_call_target="tpu_custom_call" | custom-call | bytes 30000000 | tf_op jit(solution)/shard_map/join/pallas_call | solution.py:851
  48.6 6.6 %inverse.1 = f32[2,128,2048]{2,1,0:T(8,128)} custom-call(f32[2,128,2048]{2,1,0:T(8,128)S(1)} %get-tuple-element.19.value, f32[16,4,8,128]{3,2,1,0:T(8,128)S(1)} %get-tuple-element.20.carries, f32[16,4,128]{2,1,0:T(4,128)S(1)} %join.1.incoming, bf16[1024,1024]{1,0:T(8,128)(2,1)S(1)} %get-tuple-element.14.even_hi, ...), custom_call_target="tpu_custom_call" | custom-call | bytes 18000000 | tf_op jit(solution)/shard_map/inverse/pallas_call | solution.py:868
Async XLA Ops:
  1.3 21.7 %copy-start = (f32[36,2048]{1,0:T(8,128)S(1)}, f32[36,2048]{1,0:T(8,128)}, u32[]{:S(2)}) copy-start(f32[36,2048]{1,0:T(8,128)} %constant.15.clone.decays) | copy-start | bytes 884740
  23.0 10.5 %copy-start.1 = (f32[16,17,128]{2,1,0:T(8,128)S(1)}, f32[16,17,128]{2,1,0:T(8,128)}, u32[]{:S(2)}) copy-start(f32[16,17,128]{2,1,0:T(8,128)} %constant.16.clone.powers) | copy-start | bytes 417796
  23.0 10.5 %copy-start.2 = (f32[16,2,128]{2,1,0:T(2,128)S(1)}, f32[16,2,128]{2,1,0:T(2,128)}, u32[]{:S(2)}) copy-start(f32[16,2,128]{2,1,0:T(2,128)} %constant.17.clone.extra) | copy-start | bytes 49156

commit v4 on v3

--- a/solution.py
+++ b/solution.py
@@ -33,113 +33,6 @@
 
 def params(**more):
     return pltpu.CompilerParams(vmem_limit_bytes=VMEM_BYTES, **more)
-
-
-def join_kernel(ends, powers, extra, out, heard, told, up_sems, in_sems, down_sems, back_sems):
-    count = lax.axis_size("tile")
-    me = lax.axis_index("tile")
-    blocks, lines = ends.shape[0], ends.shape[1]
-    angles = lines // 2
-    stride = count // blocks
-    mine = me // stride
-    joins = lax.rem(me, stride) == 0
-    barrier = pltpu.get_barrier_semaphore()
-
-    def greet(by, _):
-        pl.semaphore_signal(
-            barrier, inc=1, device_id={"tile": lax.rem(me + by, count)}, device_id_type=MESH
-        )
-        return 0
-
-    lax.fori_loop(1, count, greet, 0)
-    pl.semaphore_wait(barrier, count - 1)
-
-    def up(by):
-        block = lax.rem(mine + by, blocks)
-        return pltpu.make_async_remote_copy(
-            src_ref=ends.at[block],
-            dst_ref=heard.at[me],
-            send_sem=up_sems.at[block],
-            recv_sem=in_sems.at[me],
-            device_id={"tile": block * stride},
-            device_id_type=MESH,
-        )
-
-    def came(other):
-        return pltpu.make_async_remote_copy(
-            src_ref=ends.at[0],
-            dst_ref=heard.at[other],
-            send_sem=up_sems.at[0],
-            recv_sem=in_sems.at[other],
-            device_id={"tile": other},
-            device_id_type=MESH,
-        )
-
-    def down(other):
-        return pltpu.make_async_remote_copy(
-            src_ref=told.at[other],
-            dst_ref=out.at[mine],
-            send_sem=down_sems.at[other],
-            recv_sem=back_sems.at[mine],
-            device_id={"tile": other},
-            device_id_type=MESH,
-        )
-
-    def answered(block):
-        return pltpu.make_async_remote_copy(
-            src_ref=told.at[0],
-            dst_ref=out.at[block],
-            send_sem=down_sems.at[0],
-            recv_sem=back_sems.at[block],
-            device_id={"tile": block * stride},
-            device_id_type=MESH,
-        )
-
-    def each(limit, step):
-        def run(index, _):
-            step(index)
-            return 0
-
-        lax.fori_loop(0, limit, run, 0)
-
-    for by in range(blocks):
-        pl.when(lax.rem(mine + by, blocks) * stride != me)(lambda: up(by).start())
-
-    @pl.when(joins)
-    def _():
-        heard[me] = ends[mine]
-        for by in range(1, count):
-            came(lax.rem(me + by, count)).wait_recv()
-        step = powers[mine, 1:2]
-        whole = powers[mine, count : count + 1]
-        closing = extra[mine, 1:2]
-        gain = extra[mine, 0:1]
-        wall = heard[count - 1, angles:]
-        floor = heard[0, :angles]
-        for strip in range(1, count):
-            floor = floor * step + heard[strip, :angles]
-            wall = wall * step + heard[count - 1 - strip, angles:]
-        enter = (wall + whole * floor) * closing
-        leave = (floor + whole * wall) * closing
-        for strip in range(count):
-            told[strip, :angles] = enter * gain
-            enter = enter * step + heard[strip, :angles]
-            back = count - 1 - strip
-            told[back, angles:] = leave * gain
-            leave = leave * step + heard[back, angles:]
-        for by in range(1, count):
-            down(lax.rem(me + by, count)).start()
-        out[mine] = told[me]
-
-    for by in range(blocks):
-        block = lax.rem(mine + by, blocks)
-        pl.when(block * stride != me)(lambda: answered(block).wait_recv())
-        pl.when(block * stride != me)(lambda: up(by).wait_send())
-
-    @pl.when(joins)
-    def _():
-        for by in range(1, count):
-            down(lax.rem(me + by, count)).wait_send()
 
 
 def fourier_tables(side):
@@ -176,7 +69,7 @@
     return jnp.asarray(np.stack(out), f32)
 
 
-def decay_tables(grid_side, strip_rows):
+def decay_tables(grid_side, strip_rows, plane):
     half = grid_side // 2
     freqs = np.concatenate([2 * np.arange(half), 2 * np.arange(half) + 1]).astype(np.float64)
     shift = screen_term + 2.0 - 2.0 * np.cos(freqs * math.pi / grid_side)
@@ -187,10 +80,10 @@
     steps = np.exp(-(np.arange(groups)[:, None] + 1) * rate)
     jumps = np.exp(-groups * np.array([[1], [2], [4]]) * rate)
     decays = np.concatenate([segments, segments[::-1], gain[None], jumps, steps])
-    strips = grid_side // strip_rows
-    powers = np.exp(-strip_rows * np.arange(strips + 1)[:, None] * rate)
-    extra = np.stack([gain, 1.0 / (1.0 - np.exp(-2.0 * grid_side * rate))])
-    return decays.astype(np.float32), powers.astype(np.float32), extra.astype(np.float32)
+    spans = strip_rows * np.array([[1], [plane], [grid_side // strip_rows]])
+    closing = 1.0 / (1.0 - np.exp(-2.0 * grid_side * rate))
+    joins = np.concatenate([np.exp(-spans * rate), closing[None], gain[None]])
+    return decays.astype(np.float32), joins.astype(np.float32)
 
 
 def table_rows(factors, part, high, low):
@@ -507,22 +400,107 @@
 
 
 def forward_kernel(
-    field, halo, even_hi, even_lo, odd_hi, odd_lo, decays,
-    updated, out, carries, ends, source, xeh, xel, xoh, xol, coefs, power, drops, shifts, bonds, partial, afters, sems,
+    field, halo, even_hi, even_lo, odd_hi, odd_lo, decays, joins,
+    solved, carried, incoming, evens,
+    source, xeh, xel, xoh, xol, coefs, power, drops, shifts, bonds, partial, afters,
+    out, carries, ends, heard, sums, totals, told,
+    up_sems, in_sems, over_sems, across_sems, down_sems, back_sems,
 ):
     angles, _, blocks, strip, _ = field.shape
     width = blocks * LANES
     groups = strip // GROUP
-    copies = [
-        pltpu.make_async_copy(
-            field.at[:, :, block],
-            updated.at[:, :, :, block * LANES : (block + 1) * LANES],
-            sems.at[block],
-        )
-        for block in range(blocks)
-    ]
-    for copy in copies:
-        copy.start()
+    plane, share = ends.shape[1], ends.shape[2]
+    planes = totals.shape[1]
+    me = lax.axis_index("tile")
+    floor_at, seat = me // plane, lax.rem(me, plane)
+    beside = [lax.rem(seat + by, plane) for by in range(1, plane)]
+    beyond_planes = [lax.rem(floor_at + by, planes) for by in range(1, planes)]
+    barrier = pltpu.get_barrier_semaphore()
+    for peer in [floor_at * plane + other for other in beside] + [
+        other * plane + seat for other in beyond_planes
+    ]:
+        pl.semaphore_signal(barrier, inc=1, device_id={"tile": peer}, device_id_type=MESH)
+
+    def hop(source_ref, target_ref, send_sem, recv_sem, peer):
+        return pltpu.make_async_remote_copy(
+            src_ref=source_ref,
+            dst_ref=target_ref,
+            send_sem=send_sem,
+            recv_sem=recv_sem,
+            device_id={"tile": peer},
+            device_id_type=MESH,
+        )
+
+    def up(part, other, slot):
+        return hop(
+            ends.at[part, other], heard.at[part, slot], up_sems.at[part, other],
+            in_sems.at[part, slot], floor_at * plane + other,
+        )
+
+    def over(part, other, slot):
+        return hop(
+            sums.at[part], totals.at[part, slot], over_sems.at[part, other],
+            across_sems.at[part, slot], other * plane + seat,
+        )
+
+    def down(part, other, slot):
+        return hop(
+            told.at[part, other], incoming.at[part, slot], down_sems.at[part, other],
+            back_sems.at[part, slot], floor_at * plane + other,
+        )
+
+    def gather(part):
+        for other in beside:
+            up(part, other, seat).start()
+        heard[part, seat] = ends[part, seat]
+
+    def spread(part):
+        for other in beside:
+            up(part, other, other).wait_recv()
+        step = joins[part, seat, 0][:, None]
+        fall = heard[part, 0, :, :angles]
+        rise = heard[part, plane - 1, :, angles:]
+        for item in range(1, plane):
+            fall = fall * step + heard[part, item, :, :angles]
+            rise = rise * step + heard[part, plane - 1 - item, :, angles:]
+        sums[part, :, :angles] = fall
+        sums[part, :, angles:] = rise
+        for other in beyond_planes:
+            over(part, other, floor_at).start()
+        totals[part, floor_at] = sums[part]
+
+    def answer(part):
+        for other in beyond_planes:
+            over(part, other, other).wait_recv()
+        step, leap, whole, closing, gain = [joins[part, seat, item][:, None] for item in range(5)]
+        bottom = totals[part, 0, :, :angles]
+        top = totals[part, planes - 1, :, angles:]
+        for item in range(1, planes):
+            bottom = bottom * leap + totals[part, item, :, :angles]
+            top = top * leap + totals[part, planes - 1 - item, :, angles:]
+        fall = (top + whole * bottom) * closing
+        rise = (bottom + whole * top) * closing
+        fall_here, rise_here = fall, rise
+        for item in range(planes):
+            fall_here = jnp.where(floor_at == item, fall, fall_here)
+            fall = fall * leap + totals[part, item, :, :angles]
+            back = planes - 1 - item
+            rise_here = jnp.where(floor_at == back, rise, rise_here)
+            rise = rise * leap + totals[part, back, :, angles:]
+        for item in range(plane):
+            told[part, item, :, :angles] = fall_here * gain
+            fall_here = fall_here * step + heard[part, item, :, :angles]
+            back = plane - 1 - item
+            told[part, back, :, angles:] = rise_here * gain
+            rise_here = rise_here * step + heard[part, back, :, angles:]
+        for other in beside:
+            down(part, other, seat).start()
+        incoming[part, seat] = told[part, seat]
+
+    def learn(part):
+        for other in beside:
+            down(part, other, other).wait_recv()
+
     lane = lax.broadcasted_iota(jnp.int32, (GROUP, LANES), 1)
     segment = lax.broadcasted_iota(jnp.int32, (GROUP, LANES), 0)
 
@@ -611,93 +589,124 @@
     half = width // 2
 
     def tile(index):
-        return pl.ds(pl.multiple_of(index * TILE, TILE), TILE)
-
-    def fold(index, _):
+        return slice(index * TILE, (index + 1) * TILE)
+
+    def fold(index):
         where = tile(index)
         near = source[:, where]
         far = mirror(source[:, tile(width // TILE - 1 - index)])
         split_store(near + far, xeh, xel, where)
         split_store(near - far, xoh, xol, where)
-        return 0
-
-    lax.fori_loop(0, half // TILE, fold, 0)
-    for base, high, low, table_hi, table_lo in (
-        (0, xeh, xel, even_hi, even_lo),
-        (half, xoh, xol, odd_hi, odd_lo),
-    ):
-
-        def transform(index, _):
-            where = tile(index)
-            value = (
-                jnp.dot(high[...], table_hi[:, where], preferred_element_type=f32)
-                + jnp.dot(low[...], table_hi[:, where], preferred_element_type=f32)
-                + jnp.dot(high[...], table_lo[:, where], preferred_element_type=f32)
-            )
-            for column in range(TILE // LANES):
-                block = (base + index * TILE) // LANES + column
-                coefs[block] = value[:, column * LANES : (column + 1) * LANES]
+
+    for index in range(half // TILE):
+        fold(index)
+    def transform(part, index):
+        high, low, table_hi, table_lo = (
+            (xeh, xel, even_hi, even_lo),
+            (xoh, xol, odd_hi, odd_lo),
+        )[part]
+        where = tile(index)
+        value = (
+            jnp.dot(high[...], table_hi[:, where], preferred_element_type=f32)
+            + jnp.dot(low[...], table_hi[:, where], preferred_element_type=f32)
+            + jnp.dot(high[...], table_lo[:, where], preferred_element_type=f32)
+        )
+        for column in range(TILE // LANES):
+            block = index * TILE // LANES + column
+            coefs[part, block] = value[:, column * LANES : (column + 1) * LANES]
+
+    def scan(part):
+        result, carry_ref = ((out, carries), (solved, carried))[part]
+
+        def run(chunk, _):
+            where = pl.ds(pl.multiple_of(chunk * LANES, LANES), LANES)
+            table = pl.ds(pl.multiple_of(part * half + chunk * LANES, LANES), LANES)
+            owner, place = chunk // share, lax.rem(chunk, share)
+            gain = decays[2 * GROUP : 2 * GROUP + 1, table]
+            step = decays[2 * GROUP + 4 : 2 * GROUP + 5, table]
+            for angle in range(angles):
+                values = [
+                    coefs[part, chunk, pl.ds(angle * strip + group, GROUP, stride=groups)]
+                    for group in range(groups)
+                ]
+                fall, falls = values[0], [values[0]]
+                for group in range(1, groups):
+                    fall = values[group] + step * fall
+                    falls.append(fall)
+                rise = values[-1]
+                for group in reversed(range(groups)):
+                    total = falls[group]
+                    if group < groups - 1:
+                        later = step * rise
+                        total = total + later
+                        rise = values[group] + later
+                    result[angle, group * GROUP : (group + 1) * GROUP, where] = gain * total
+                for index, by in enumerate((1, 2, 4)):
+                    jump = decays[2 * GROUP + 1 + index : 2 * GROUP + 2 + index, table]
+                    fall = fall + jnp.where(segment >= by, pltpu.roll(fall, by, 0), 0.0) * jump
+                    rise = (
+                        rise
+                        + jnp.where(segment < GROUP - by, pltpu.roll(rise, GROUP - by, 0), 0.0)
+                        * jump
+                    )
+                ends[part, owner, place, angle : angle + 1] = fall[GROUP - 1 :]
+                ends[part, owner, place, angles + angle : angles + angle + 1] = rise[:1]
+                carry_ref[chunk, angle] = gain * jnp.where(
+                    segment >= 1, pltpu.roll(fall, 1, 0), 0.0
+                )
+                carry_ref[chunk, angles + angle] = gain * jnp.where(
+                    segment < GROUP - 1, pltpu.roll(rise, GROUP - 1, 0), 0.0
+                )
             return 0
 
-        lax.fori_loop(0, half // TILE, transform, 0)
-
-    def scan(chunk, _):
+        lax.fori_loop(0, blocks // 2, run, 0, unroll=2)
+
+    tiles = half // TILE
+    for index in range(tiles):
+        transform(0, index)
+    scan(0)
+    pl.semaphore_wait(barrier, plane + planes - 2)
+    gather(0)
+    for index in range(tiles):
+        transform(1, index)
+    spread(0)
+    scan(1)
+    gather(1)
+    spread(1)
+    answer(0)
+    learn(0)
+    enter(0, out, carries, incoming, decays, xeh, xel)
+    for index in range(tiles):
+        if index == 1 or tiles == 1:
+            answer(1)
+        evens[:, tile(index)] = restored(xeh, xel, even_hi, even_lo, tile(index))
+    learn(1)
+    for part in range(2):
+        for other in beside:
+            up(part, other, seat).wait_send()
+            down(part, other, seat).wait_send()
+        for other in beyond_planes:
+            over(part, other, floor_at).wait_send()
+
+
+def enter(part, value, carries, incoming, decays, high, low):
+    angles, strip, half = value.shape
+    groups = strip // GROUP
+    share = incoming.shape[2]
+
+    def run(chunk, _):
         where = pl.ds(pl.multiple_of(chunk * LANES, LANES), LANES)
-        gain = decays[2 * GROUP : 2 * GROUP + 1, where]
-        step = decays[2 * GROUP + 4 : 2 * GROUP + 5, where]
-        for angle in range(angles):
-            values = [
-                coefs[chunk, pl.ds(angle * strip + group, GROUP, stride=groups)]
-                for group in range(groups)
-            ]
-            fall, falls = values[0], [values[0]]
-            for group in range(1, groups):
-                fall = values[group] + step * fall
-                falls.append(fall)
-            rise = values[-1]
-            for group in reversed(range(groups)):
-                total = falls[group]
-                if group < groups - 1:
-                    later = step * rise
-                    total = total + later
-                    rise = values[group] + later
-                out[angle, group * GROUP : (group + 1) * GROUP, where] = gain * total
-            for index, by in enumerate((1, 2, 4)):
-                jump = decays[2 * GROUP + 1 + index : 2 * GROUP + 2 + index, where]
-                fall = fall + jnp.where(segment >= by, pltpu.roll(fall, by, 0), 0.0) * jump
-                rise = rise + jnp.where(segment < GROUP - by, pltpu.roll(rise, GROUP - by, 0), 0.0) * jump
-            ends[chunk, angle : angle + 1] = fall[GROUP - 1 :]
-            ends[chunk, angles + angle : angles + angle + 1] = rise[:1]
-            carries[chunk, angle] = gain * jnp.where(segment >= 1, pltpu.roll(fall, 1, 0), 0.0)
-            carries[chunk, angles + angle] = gain * jnp.where(
-                segment < GROUP - 1, pltpu.roll(rise, GROUP - 1, 0), 0.0
-            )
-        return 0
-
-    lax.fori_loop(0, blocks, scan, 0, unroll=2)
-    for copy in copies:
-        copy.wait()
-
-
-def inverse_kernel(
-    value, carries, incoming, even_hi, even_lo, odd_hi, odd_lo, decays, out, xh, xl, parted, sems
-):
-    angles, strip, width = value.shape
-    half = width // 2
-    groups = strip // GROUP
-    blocks = width // LANES
-
-    def enter(chunk, _):
-        where = pl.ds(pl.multiple_of(chunk * LANES, LANES), LANES)
+        table = pl.ds(pl.multiple_of(part * half + chunk * LANES, LANES), LANES)
+        owner, place = chunk // share, lax.rem(chunk, share)
         for angle in range(angles):
             fall = (
                 carries[chunk, angle]
-                + decays[:GROUP, where] * incoming[chunk, angle : angle + 1]
+                + decays[:GROUP, table] * incoming[part, owner, place, angle : angle + 1]
             )
             rise = (
                 carries[chunk, angles + angle]
-                + decays[GROUP : 2 * GROUP, where]
-                * incoming[chunk, angles + angle : angles + angle + 1]
+                + decays[GROUP : 2 * GROUP, table]
+                * incoming[part, owner, place, angles + angle : angles + angle + 1]
             )
             for pair in range(0, groups, 2):
                 rows = []
@@ -706,32 +715,52 @@
                     behind = 2 * GROUP + 4 + groups - 1 - group
                     rows.append(
                         value[angle, group * GROUP : (group + 1) * GROUP, where]
-                        + decays[ahead : ahead + 1, where] * fall
-                        + decays[behind : behind + 1, where] * rise
+                        + decays[ahead : ahead + 1, table] * fall
+                        + decays[behind : behind + 1, table] * rise
                     )
                 item = jnp.concatenate(rows, 0)
                 rounded = item.astype(bf16)
                 start = angle * strip + pair * GROUP
-                xh[start : start + 2 * GROUP, where] = rounded
-                xl[start : start + 2 * GROUP, where] = (item - rounded.astype(f32)).astype(bf16)
+                high[start : start + 2 * GROUP, where] = rounded
+                low[start : start + 2 * GROUP, where] = (item - rounded.astype(f32)).astype(bf16)
         return 0
 
-    lax.fori_loop(0, blocks, enter, 0)
+    lax.fori_loop(0, half // LANES, run, 0)
+
+
+def restored(high, low, table_hi, table_lo, where):
     last = (((1,), (1,)), ((), ()))
+    return (
+        lax.dot_general(high[...], table_hi[where], last, preferred_element_type=f32)
+        + lax.dot_general(low[...], table_hi[where], last, preferred_element_type=f32)
+        + lax.dot_general(high[...], table_lo[where], last, preferred_element_type=f32)
+    )
+
+
+def inverse_kernel(
+    field, value, carries, incoming, evens, odd_hi, odd_lo, decays,
+    updated, out, xh, xl, parted, sems, field_sems,
+):
+    angles, strip, half = value.shape
+    width = 2 * half
+    groups = strip // GROUP
+    blocks = width // LANES
     copies = []
+    for block in range(blocks):
+        copy = pltpu.make_async_copy(
+            field.at[:, :, block],
+            updated.at[:, :, :, block * LANES : (block + 1) * LANES],
+            field_sems.at[block],
+        )
+        copy.start()
+        copies.append(copy)
+    enter(1, value, carries, incoming, decays, xh, xl)
     for first in range(0, half, TILE):
         where = slice(first, first + TILE)
-        parts = []
-        for base, table_hi, table_lo in ((0, even_hi, even_lo), (half, odd_hi, odd_lo)):
-            high = xh[:, base : base + half]
-            low = xl[:, base : base + half]
-            parts.append(
-                lax.dot_general(high, table_hi[where], last, preferred_element_type=f32)
-                + lax.dot_general(low, table_hi[where], last, preferred_element_type=f32)
-                + lax.dot_general(high, table_lo[where], last, preferred_element_type=f32)
-            )
-        near = parts[0] + parts[1]
-        far = mirror(parts[0] - parts[1])
+        even = evens[:, where]
+        odd = restored(xh, xl, odd_hi, odd_lo, where)
+        near = even + odd
+        far = mirror(even - odd)
         for item, start in ((near, first), (far, width - first - TILE)):
             for column in range(0, TILE, LANES):
                 block = (start + column) // LANES
@@ -764,10 +793,10 @@
     shape = jax.ShapeDtypeStruct
 
     pieces = (reach + 1) * cap
-    decays, powers, extra = decay_tables(width, strip)
-
-    def by_block(table):
-        return jnp.asarray(table.reshape(-1, blocks, LANES).transpose(1, 0, 2))
+    plane = 2 ** (int(math.log2(strips)) // 2)
+    share = blocks // (2 * plane)
+    decays, joins = decay_tables(width, strip, plane)
+    joins = jnp.asarray(joins.reshape(-1, 2, plane, share, LANES).transpose(1, 2, 0, 3, 4))
 
     factors = cosine_factors(width)
     table = (reach + 1, cap, 2, strip, side)
@@ -822,64 +851,62 @@
         ],
     )
 
-    updated, solved, carries, ends = pl.pallas_call(
+    planes = strips // plane
+    lines = (share, 2 * angles, LANES)
+    solved, carried, incoming, evens = pl.pallas_call(
         forward_kernel,
         out_shape=[
-            shape(object_field.shape, f32),
-            shape((angles, strip, width), f32),
-            shape((blocks, 2 * angles, GROUP, LANES), f32),
-            shape((blocks, 2 * angles, LANES), f32),
+            shape((angles, strip, half), f32),
+            shape((blocks // 2, 2 * angles, GROUP, LANES), f32),
+            shape((2, plane) + lines, f32),
+            shape((rows, half), f32),
         ],
-        in_specs=[vmem] * 7,
-        out_specs=[hbm, vmem, vmem, vmem],
+        in_specs=[vmem] * 8,
+        out_specs=[vmem] * 4,
         scratch_shapes=[pltpu.VMEM((rows, width), f32)]
         + [pltpu.VMEM((rows, half), bf16)] * 4
         + [
-            pltpu.VMEM((blocks, rows, LANES), f32),
+            pltpu.VMEM((2, blocks // 2, rows, LANES), f32),
             pltpu.VMEM((2, strip, LANES), f32),
             pltpu.VMEM((strip + GROUP, LANES), f32),
             pltpu.VMEM((2, 2, strip // GROUP, GROUP, LANES), f32),
             pltpu.VMEM((2, strip // GROUP, GROUP, LANES), f32),
             pltpu.VMEM((2, strip // GROUP, GROUP, LANES), f32),
             pltpu.VMEM((strip // GROUP, GROUP, LANES), f32),
-        ]
-        + [pltpu.SemaphoreType.DMA((blocks,))],
-        compiler_params=params(),
-        cost_estimate=cost(9),
+            pltpu.VMEM((angles, strip, half), f32),
+            pltpu.VMEM((blocks // 2, 2 * angles, GROUP, LANES), f32),
+            pltpu.VMEM((2, plane) + lines, f32),
+            pltpu.VMEM((2, plane) + lines, f32),
+            pltpu.VMEM((2,) + lines, f32),
+            pltpu.VMEM((2, planes) + lines, f32),
+            pltpu.VMEM((2, plane) + lines, f32),
+            pltpu.SemaphoreType.DMA((2, plane)),
+            pltpu.SemaphoreType.DMA((2, plane)),
+            pltpu.SemaphoreType.DMA((2, planes)),
+            pltpu.SemaphoreType.DMA((2, planes)),
+            pltpu.SemaphoreType.DMA((2, plane)),
+            pltpu.SemaphoreType.DMA((2, plane)),
+        ],
+        compiler_params=params(collective_id=1, has_side_effects=True),
+        cost_estimate=cost(15),
         name="forward",
-    )(held, halo, *half_tables, decays)
-    incoming = pl.pallas_call(
-        join_kernel,
-        out_shape=shape(ends.shape, f32),
-        in_specs=[vmem] * 3,
-        out_specs=vmem,
+    )(held, halo, *half_tables, decays, joins)
+    updated, phase_map = pl.pallas_call(
+        inverse_kernel,
+        out_shape=[shape(object_field.shape, f32), shape((angles, strip, width), f32)],
+        in_specs=[vmem] * 8,
+        out_specs=[hbm, hbm],
         scratch_shapes=[
-            pltpu.VMEM((strips, 2 * angles, LANES), f32),
-            pltpu.VMEM((strips, 2 * angles, LANES), f32),
+            pltpu.VMEM((rows, half), bf16),
+            pltpu.VMEM((rows, half), bf16),
+            pltpu.VMEM((angles, blocks, strip, LANES), f32),
             pltpu.SemaphoreType.DMA((blocks,)),
-            pltpu.SemaphoreType.DMA((strips,)),
-            pltpu.SemaphoreType.DMA((strips,)),
-            pltpu.SemaphoreType.DMA((blocks,)),
-        ],
-        compiler_params=params(collective_id=4, has_side_effects=True),
-        cost_estimate=cost(10),
-        name="join",
-    )(ends, by_block(powers), by_block(extra))
-    phase_map = pl.pallas_call(
-        inverse_kernel,
-        out_shape=shape((angles, strip, width), f32),
-        in_specs=[vmem] * 8,
-        out_specs=hbm,
-        scratch_shapes=[
-            pltpu.VMEM((rows, width), bf16),
-            pltpu.VMEM((rows, width), bf16),
-            pltpu.VMEM((angles, blocks, strip, LANES), f32),
             pltpu.SemaphoreType.DMA((blocks,)),
         ],
         compiler_params=params(),
         cost_estimate=cost(6),
         name="inverse",
-    )(solved, carries, incoming, *half_tables, decays)
+    )(held, solved, carried, incoming, evens, *half_tables[2:], decays)
     return (updated, phase_map)
 
 

time: 55.3 us -> 53.6 us (0.969)
  Pallas kernels: 53.8 us -> 51.9 us
    pallas_call x3 -> x2, Pallas kernels: 32.1 us -> 30 us  [the longest x1 23.6 us: body(): pl.pallas_call(forward_kernel, out_shape=[shape((angles, strip, half), f3...]
where the time goes in v4:
time: 53.6 us; the launch traced here: 53.4 us
  Pallas kernels  51.9 us (97%)
  between operations  1.49 us (3%)
    pallas_call x1, Pallas kernels, body(): pl.pallas_call(forward_kernel, out_shape=[shape((angles, strip, half), f3...  23.6 us
    pallas_call x1, Pallas kernels, body(): pl.pallas_call(update_kernel, out_shape=[shape((angles, 2, blocks, strip,...  21.9 us
    pallas_call x1, Pallas kernels, body(): pl.pallas_call(inverse_kernel, out_shape=[shape(object_field.shape, f32),...  6.44 us

profile of v4, /device:TPU:0, one launch (start us, length us, event | category | flops | bytes accessed | tf_op | source)
XLA Modules:
  0.0 53.4 jit_solution(10979462316534105055)
XLA Ops:
  1.3 0.0 copy-start
  1.3 0.0 copy-start.1
  1.3 21.9 %update.1 = (f32[2,2,16,128,128]{4,3,2,1,0:T(8,128)S(1)}, f32[2,2,2,1,2048]{4,3,2,1,0:T(1,128)S(1)}, bf16[1024,1024]{1,0:T(8,128)(2,1)S(1)}, bf16[1024,1024]{1,0...) custom-call(s32[1]{0:T(128)S(6)} %copy.12.frame_count, s32[2,3]{1,0:T(2,128)} %frame_table.1, ...), custom_call_target="tpu_custom_call" | custom-call | bytes 60000000 | tf_op jit(solution)/shard_map/update/pallas_call | solution.py:803
  23.2 0.0 copy-done
  23.2 0.0 copy-done.1
  23.2 23.6 %forward.1 = (f32[2,128,1024]{2,1,0:T(8,128)S(1)}, f32[8,4,8,128]{3,2,1,0:T(8,128)S(1)}, f32[2,4,2,4,128]{4,3,2,1,0:T(4,128)S(1)}, f32[256,1024]{1,0:T(8,128)S(1)}) custom-call(f32[2,2,16,128,128]{4,3,2,1,0:T(8,128)S(1)} %get-tuple-element.12.field, f32[2,2,2,1,2048]{4,3,2,1,0:T(1,128)S(1)} %get-tuple-element.13.halo, ...), custom_call_target="tpu_custom_call" | custom-call | bytes 45000000 | tf_op jit(solution)/shard_map/forward/pallas_call | solution.py:856
  46.8 6.4 %inverse.1 = (f32[2,2,128,2048]{3,2,1,0:T(8,128)}, f32[2,128,2048]{2,1,0:T(8,128)}) custom-call(f32[2,2,16,128,128]{4,3,2,1,0:T(8,128)S(1)} %get-tuple-element.12.field, f32[2,128,1024]{2,1,0:T(8,128)S(1)} %get-tuple-element.18.value, f32[8,4,8,128]{3,2,1,0:T(8,128)S(1)} %get-tuple-element.19.carries, f32[2,4,2,4,128]{4,3,2,1,0:T(4,128)S(1)} %get-tuple-element.20.incoming, ...), custom_call_target="tpu_custom_call" | custom-call | bytes 18000000 | tf_op jit(solution)/shard_map/inverse/pallas_call | solution.py:894
Async XLA Ops:
  1.3 21.9 %copy-start = (f32[36,2048]{1,0:T(8,128)S(1)}, f32[36,2048]{1,0:T(8,128)}, u32[]{:S(2)}) copy-start(f32[36,2048]{1,0:T(8,128)} %constant.14.clone.decays) | copy-start | bytes 884740
  1.3 21.9 %copy-start.1 = (f32[2,4,5,2,128]{4,3,2,1,0:T(2,128)S(1)}, f32[2,4,5,2,128]{4,3,2,1,0:T(2,128)}, u32[]{:S(2)}) copy-start(f32[2,4,5,2,128]{4,3,2,1,0:T(2,128)} %constant.10.clone.joins) | copy-start | bytes 122884

commit v5 on v4

--- a/solution.py
+++ b/solution.py
@@ -79,7 +79,10 @@
     segments = np.exp(-groups * np.arange(GROUP)[:, None] * rate)
     steps = np.exp(-(np.arange(groups)[:, None] + 1) * rate)
     jumps = np.exp(-groups * np.array([[1], [2], [4]]) * rate)
-    decays = np.concatenate([segments, segments[::-1], gain[None], jumps, steps])
+    spare = np.zeros((GROUP - 4,) + gain.shape)
+    decays = np.concatenate(
+        [segments, segments[::-1], gain[None], jumps, spare, steps, steps[::-1]]
+    )
     spans = strip_rows * np.array([[1], [plane], [grid_side // strip_rows]])
     closing = 1.0 / (1.0 - np.exp(-2.0 * grid_side * rate))
     joins = np.concatenate([np.exp(-spans * rate), closing[None], gain[None]])
@@ -619,11 +622,10 @@
         result, carry_ref = ((out, carries), (solved, carried))[part]
 
         def run(chunk, _):
-            where = pl.ds(pl.multiple_of(chunk * LANES, LANES), LANES)
             table = pl.ds(pl.multiple_of(part * half + chunk * LANES, LANES), LANES)
             owner, place = chunk // share, lax.rem(chunk, share)
             gain = decays[2 * GROUP : 2 * GROUP + 1, table]
-            step = decays[2 * GROUP + 4 : 2 * GROUP + 5, table]
+            step = decays[3 * GROUP : 3 * GROUP + 1, table]
             for angle in range(angles):
                 values = [
                     coefs[part, chunk, pl.ds(angle * strip + group, GROUP, stride=groups)]
@@ -640,7 +642,8 @@
                         later = step * rise
                         total = total + later
                         rise = values[group] + later
-                    result[angle, group * GROUP : (group + 1) * GROUP, where] = gain * total
+                    first = angle * strip + group * GROUP
+                    result[chunk, first : first + GROUP] = gain * total
                 for index, by in enumerate((1, 2, 4)):
                     jump = decays[2 * GROUP + 1 + index : 2 * GROUP + 2 + index, table]
                     fall = fall + jnp.where(segment >= by, pltpu.roll(fall, by, 0), 0.0) * jump
@@ -690,8 +693,11 @@
 
 
 def enter(part, value, carries, incoming, decays, high, low):
-    angles, strip, half = value.shape
+    angles = incoming.shape[3] // 2
+    strip = value.shape[1] // angles
+    half = value.shape[0] * LANES
     groups = strip // GROUP
+    length = min(groups, GROUP)
     share = incoming.shape[2]
 
     def run(chunk, _):
@@ -708,19 +714,23 @@
                 + decays[GROUP : 2 * GROUP, table]
                 * incoming[part, owner, place, angles + angle : angles + angle + 1]
             )
-            for pair in range(0, groups, 2):
+            for pair in range(0, strip, 2 * GROUP):
                 rows = []
-                for group in (pair, pair + 1):
-                    ahead = 2 * GROUP + 4 + group
-                    behind = 2 * GROUP + 4 + groups - 1 - group
+                for row in range(pair, pair + 2 * GROUP, length):
+                    owner_row, group = row // groups, row % groups
+                    ahead = 3 * GROUP + group
+                    behind = ahead + groups
                     rows.append(
-                        value[angle, group * GROUP : (group + 1) * GROUP, where]
-                        + decays[ahead : ahead + 1, table] * fall
-                        + decays[behind : behind + 1, table] * rise
+                        value[
+                            chunk,
+                            pl.ds(angle * strip + group * GROUP + owner_row, length, stride=GROUP),
+                        ]
+                        + decays[ahead : ahead + length, table] * fall[owner_row : owner_row + 1]
+                        + decays[behind : behind + length, table] * rise[owner_row : owner_row + 1]
                     )
                 item = jnp.concatenate(rows, 0)
                 rounded = item.astype(bf16)
-                start = angle * strip + pair * GROUP
+                start = angle * strip + pair
                 high[start : start + 2 * GROUP, where] = rounded
                 low[start : start + 2 * GROUP, where] = (item - rounded.astype(f32)).astype(bf16)
         return 0
@@ -741,9 +751,8 @@
     field, value, carries, incoming, evens, odd_hi, odd_lo, decays,
     updated, out, xh, xl, parted, sems, field_sems,
 ):
-    angles, strip, half = value.shape
-    width = 2 * half
-    groups = strip // GROUP
+    angles, strip, width = out.shape
+    half = width // 2
     blocks = width // LANES
     copies = []
     for block in range(blocks):
@@ -755,28 +764,23 @@
         copy.start()
         copies.append(copy)
     enter(1, value, carries, incoming, decays, xh, xl)
-    for first in range(0, half, TILE):
-        where = slice(first, first + TILE)
-        even = evens[:, where]
-        odd = restored(xh, xl, odd_hi, odd_lo, where)
+    tiles = [slice(first, first + TILE) for first in range(0, half, TILE)]
+    later = restored(xh, xl, odd_hi, odd_lo, tiles[0])
+    for index, where in enumerate(tiles):
+        first, odd, even = where.start, later, evens[:, where]
+        if index + 1 < len(tiles):
+            later = restored(xh, xl, odd_hi, odd_lo, tiles[index + 1])
         near = even + odd
         far = mirror(even - odd)
         for item, start in ((near, first), (far, width - first - TILE)):
-            for column in range(0, TILE, LANES):
-                block = (start + column) // LANES
-                for angle in range(angles):
-                    for group in range(groups):
-                        row = angle * strip + group * GROUP
-                        parted[angle, block, pl.ds(group, GROUP, stride=groups)] = item[
-                            row : row + GROUP, column : column + LANES
-                        ]
-                copy = pltpu.make_async_copy(
-                    parted.at[:, block],
-                    out.at[:, :, block * LANES : (block + 1) * LANES],
-                    sems.at[block],
-                )
-                copy.start()
-                copies.append(copy)
+            where = slice(start, start + TILE)
+            for angle in range(angles):
+                parted[angle, :, where] = item[angle * strip : (angle + 1) * strip]
+            copy = pltpu.make_async_copy(
+                parted.at[:, :, where], out.at[:, :, where], sems.at[start // TILE]
+            )
+            copy.start()
+            copies.append(copy)
     for copy in copies:
         copy.wait()
 
@@ -856,7 +860,7 @@
     solved, carried, incoming, evens = pl.pallas_call(
         forward_kernel,
         out_shape=[
-            shape((angles, strip, half), f32),
+            shape((blocks // 2, rows, LANES), f32),
             shape((blocks // 2, 2 * angles, GROUP, LANES), f32),
             shape((2, plane) + lines, f32),
             shape((rows, half), f32),
@@ -873,7 +877,7 @@
             pltpu.VMEM((2, strip // GROUP, GROUP, LANES), f32),
             pltpu.VMEM((2, strip // GROUP, GROUP, LANES), f32),
             pltpu.VMEM((strip // GROUP, GROUP, LANES), f32),
-            pltpu.VMEM((angles, strip, half), f32),
+            pltpu.VMEM((blocks // 2, rows, LANES), f32),
             pltpu.VMEM((blocks // 2, 2 * angles, GROUP, LANES), f32),
             pltpu.VMEM((2, plane) + lines, f32),
             pltpu.VMEM((2, plane) + lines, f32),
@@ -899,8 +903,8 @@
         scratch_shapes=[
             pltpu.VMEM((rows, half), bf16),
             pltpu.VMEM((rows, half), bf16),
-            pltpu.VMEM((angles, blocks, strip, LANES), f32),
-            pltpu.SemaphoreType.DMA((blocks,)),
+            pltpu.VMEM((angles, strip, width), f32),
+            pltpu.SemaphoreType.DMA((width // TILE,)),
             pltpu.SemaphoreType.DMA((blocks,)),
         ],
         compiler_params=params(),

time: 53.6 us -> 51 us (0.951)
  Pallas kernels: 51.9 us -> 49.3 us
    pallas_call x1, Pallas kernels: 6.44 us -> 3.87 us  [body(): pl.pallas_call(inverse_kernel, out_shape=[shape(object_field.shape, f32),...]
where the time goes in v5:
time: 51 us; the launch traced here: 50.8 us
  Pallas kernels  49.3 us (97%)
  between operations  1.49 us (3%)
    pallas_call x1, Pallas kernels, body(): pl.pallas_call(forward_kernel, out_shape=[shape((blocks // 2, rows, LANES...  23.6 us
    pallas_call x1, Pallas kernels, body(): pl.pallas_call(update_kernel, out_shape=[shape((angles, 2, blocks, strip,...  21.9 us
    pallas_call x1, Pallas kernels, body(): pl.pallas_call(inverse_kernel, out_shape=[shape(object_field.shape, f32),...  3.87 us

profile of v5, /device:TPU:0, one launch (start us, length us, event | category | flops | bytes accessed | tf_op | source)
XLA Modules:
  0.0 50.8 jit_solution(1072922269318457493)
XLA Ops:
  1.3 0.0 copy-start
  1.3 0.0 copy-start.1
  1.3 21.9 %update.1 = (f32[2,2,16,128,128]{4,3,2,1,0:T(8,128)S(1)}, f32[2,2,2,1,2048]{4,3,2,1,0:T(1,128)S(1)}, bf16[1024,1024]{1,0:T(8,128)(2,1)S(1)}, bf16[1024,1024]{1,0...) custom-call(s32[1]{0:T(128)S(6)} %copy.12.frame_count, s32[2,3]{1,0:T(2,128)} %frame_table.1, ...), custom_call_target="tpu_custom_call" | custom-call | bytes 60000000 | tf_op jit(solution)/shard_map/update/pallas_call | solution.py:807
  23.2 0.0 copy-done
  23.2 0.0 copy-done.1
  23.2 23.6 %forward.1 = (f32[8,256,128]{2,1,0:T(8,128)S(1)}, f32[8,4,8,128]{3,2,1,0:T(8,128)S(1)}, f32[2,4,2,4,128]{4,3,2,1,0:T(4,128)S(1)}, f32[256,1024]{1,0:T(8,128)S(1)}) custom-call(f32[2,2,16,128,128]{4,3,2,1,0:T(8,128)S(1)} %get-tuple-element.12.field, f32[2,2,2,1,2048]{4,3,2,1,0:T(1,128)S(1)} %get-tuple-element.13.halo, ...), custom_call_target="tpu_custom_call" | custom-call | bytes 45000000 | tf_op jit(solution)/shard_map/forward/pallas_call | solution.py:860
  46.8 3.9 %inverse.1 = (f32[2,2,128,2048]{3,2,1,0:T(8,128)}, f32[2,128,2048]{2,1,0:T(8,128)}) custom-call(f32[2,2,16,128,128]{4,3,2,1,0:T(8,128)S(1)} %get-tuple-element.12.field, f32[8,256,128]{2,1,0:T(8,128)S(1)} %get-tuple-element.18.value, f32[8,4,8,128]{3,2,1,0:T(8,128)S(1)} %get-tuple-element.19.carries, f32[2,4,2,4,128]{4,3,2,1,0:T(4,128)S(1)} %get-tuple-element.20.incoming, ...), custom_call_target="tpu_custom_call" | custom-call | bytes 18000000 | tf_op jit(solution)/shard_map/inverse/pallas_call | solution.py:898
Async XLA Ops:
  1.3 21.9 %copy-start = (f32[56,2048]{1,0:T(8,128)S(1)}, f32[56,2048]{1,0:T(8,128)}, u32[]{:S(2)}) copy-start(f32[56,2048]{1,0:T(8,128)} %constant.14.clone.decays) | copy-start | bytes 1376260
  1.3 21.9 %copy-start.1 = (f32[2,4,5,2,128]{4,3,2,1,0:T(2,128)S(1)}, f32[2,4,5,2,128]{4,3,2,1,0:T(2,128)}, u32[]{:S(2)}) copy-start(f32[2,4,5,2,128]{4,3,2,1,0:T(2,128)} %constant.10.clone.joins) | copy-start | bytes 122884

commit v6 on v5

--- a/solution.py
+++ b/solution.py
@@ -110,10 +110,19 @@
     return jnp.minimum(column // LANES, (width - span) // LANES) * LANES
 
 
+def power_of(re, im):
+    return re * re + im * im + 0.5 * soften_term
+
+
+def half_bond(first, second):
+    cross = first[0] * second[1] - first[1] * second[0]
+    return cross / (first[2] + second[2])
+
+
 def update_kernel(
     frame_count, frame_table, field, probe_in, measured, cos_in, sin_in, factors_in,
-    held, halo, even_hi, even_lo, odd_hi, odd_lo,
-    tables, counts, probe, cos_ref, sin_ref, factors, moved, cuts, arrived, away, landed,
+    held, source, even_hi, even_lo, odd_hi, odd_lo,
+    halo, power, drops, shifts, bonds, partial, afters, tables, counts, probe, cos_ref, sin_ref, factors, moved, cuts, arrived, away, landed,
     own, placed, window, edges,
     load_sems, tell_sems, count_sems, moved_sems, fetch_sems, give_sems, edge_sems,
 ):
@@ -370,7 +379,99 @@
                 edges[1, angle, part, :, where] = held[angle, part, block, strip - 1 :]
     start(borders)
     add(late, [slice(GROUP, strip - GROUP)])
+
+    groups = strip // GROUP
+    lane = lax.broadcasted_iota(jnp.int32, (GROUP, LANES), 1)
+    segment = lax.broadcasted_iota(jnp.int32, (GROUP, LANES), 0)
+    drops[:GROUP] = jnp.zeros((GROUP, LANES), f32)
+    for angle in range(angles):
+
+        def rows_of(group):
+            return slice(group * GROUP, (group + 1) * GROUP)
+
+        def prepare(block, slot):
+            for group in range(groups):
+                pair = [held[angle, part, block, rows_of(group)] for part in range(2)]
+                power[slot, rows_of(group)] = power_of(*pair)
+                for part, value in enumerate(pair):
+                    shifts[slot, part, group] = pltpu.roll(value, 1, 1)
+
+        def combine(block, slot):
+            for group in range(groups):
+                here = [held[angle, part, block, rows_of(group)] for part in range(2)]
+                here.append(power[slot, rows_of(group)])
+                if group == groups - 1:
+                    below = [
+                        jnp.where(segment == GROUP - 1, 0.0, pltpu.roll(value, GROUP - 1, 0))
+                        for value in here[:2]
+                    ]
+                    below.append(power_of(*below))
+                else:
+                    lower = slice(group * GROUP + 1, (group + 1) * GROUP + 1)
+                    below = [held[angle, part, block, lower] for part in range(2)]
+                    below.append(power[slot, lower])
+                down = half_bond(here, below)
+                first = (group + 1) * GROUP
+                drops[first : first + GROUP] = down
+                up = drops[first - 1 : first - 1 + GROUP]
+                left = [
+                    jnp.where(lane == 0, shifts[1 - slot, part, group], shifts[slot, part, group])
+                    for part in range(2)
+                ]
+                bond = half_bond(left + [power_of(*left)], here)
+                bonds[slot, group] = bond
+                partial[slot, group] = up - down + bond
+
+        def finish(block, slot):
+            behind = pl.ds(pl.multiple_of(jnp.maximum(block - 1, 0) * LANES, LANES), LANES)
+            for group in range(groups):
+                after = pltpu.roll(bonds[slot, group], LANES - 1, 1)
+                first = angle * strip + group * GROUP
+                source[first : first + GROUP, behind] = partial[1 - slot, group] - jnp.where(
+                    lane == LANES - 1, after, afters[group]
+                )
+                afters[group] = after
+
+        def step(pair, _):
+            block = 2 * pair
+            finish(block - 1, 1)
+            combine(block, 0)
+            prepare(block + 1, 1)
+            finish(block, 0)
+            combine(block + 1, 1)
+            prepare(jnp.minimum(block + 2, blocks - 1), 0)
+            return 0
+
+        for group in range(groups):
+            for part in range(2):
+                shifts[1, part, group] = jnp.zeros((GROUP, LANES), f32)
+        prepare(0, 0)
+        lax.fori_loop(0, blocks // 2, step, 0)
+        finish(blocks - 1, 1)
+        for group in range(groups):
+            first = angle * strip + group * GROUP
+            source[first : first + GROUP, width - LANES :] = partial[1, group] - jnp.where(
+                lane == LANES - 1, 0.0, afters[group]
+            )
+
     arrive(borders)
+
+    def line(values):
+        return values + [power_of(*values)]
+
+    for angle in range(angles):
+        for border, row in ((0, 0), (1, strip - 1)):
+            inner = line(
+                [
+                    jnp.concatenate(
+                        [held[angle, part, block, row : row + 1] for block in range(blocks)], 1
+                    )
+                    for part in range(2)
+                ]
+            )
+            outer = line([halo[border, angle, part] for part in range(2)])
+            place = slice(angle * strip + row, angle * strip + row + 1)
+            source[place] = source[place] + half_bond(outer, inner)
     for copy, sends in started:
         pl.when(sends)(copy.wait_send)
 
@@ -393,24 +494,15 @@
     low[:, columns] = (value - rounded.astype(f32)).astype(bf16)
 
 
-def power_of(re, im):
-    return re * re + im * im + 0.5 * soften_term
-
-
-def half_bond(first, second):
-    cross = first[0] * second[1] - first[1] * second[0]
-    return cross / (first[2] + second[2])
-
-
 def forward_kernel(
-    field, halo, even_hi, even_lo, odd_hi, odd_lo, decays, joins,
+    source, even_hi, even_lo, odd_hi, odd_lo, decays, joins,
     solved, carried, incoming, evens,
-    source, xeh, xel, xoh, xol, coefs, power, drops, shifts, bonds, partial, afters,
+    xeh, xel, xoh, xol, coefs,
     out, carries, ends, heard, sums, totals, told,
     up_sems, in_sems, over_sems, across_sems, down_sems, back_sems,
 ):
-    angles, _, blocks, strip, _ = field.shape
-    width = blocks * LANES
+    angles, width = ends.shape[3] // 2, source.shape[1]
+    strip, blocks = source.shape[0] // angles, width // LANES
     groups = strip // GROUP
     plane, share = ends.shape[1], ends.shape[2]
     planes = totals.shape[1]
@@ -504,91 +596,7 @@
         for other in beside:
             down(part, other, other).wait_recv()
 
-    lane = lax.broadcasted_iota(jnp.int32, (GROUP, LANES), 1)
     segment = lax.broadcasted_iota(jnp.int32, (GROUP, LANES), 0)
-
-    for angle in range(angles):
-
-        def rows_of(group):
-            return slice(group * GROUP, (group + 1) * GROUP)
-
-        def prepare(block, slot):
-            for group in range(groups):
-                pair = [field[angle, part, block, rows_of(group)] for part in range(2)]
-                power[slot, rows_of(group)] = power_of(*pair)
-                for part, value in enumerate(pair):
-                    shifts[slot, part, group] = pltpu.roll(value, 1, 1)
-
-        def combine(block, slot):
-            where = pl.ds(pl.multiple_of(block * LANES, LANES), LANES)
-
-            def beyond(upper):
-                edge, by, border = (0, 1, 0) if upper else (GROUP - 1, GROUP - 1, 1)
-                pair = [
-                    jnp.where(
-                        segment == edge,
-                        halo[border, angle, part, :, where],
-                        pltpu.roll(field[angle, part, block, rows_of(0 if upper else groups - 1)], by, 0),
-                    )
-                    for part in range(2)
-                ]
-                return pair + [power_of(*pair)]
-
-            for group in range(groups):
-                here = [field[angle, part, block, rows_of(group)] for part in range(2)]
-                here.append(power[slot, rows_of(group)])
-                if group == 0:
-                    drops[GROUP - 1 : 2 * GROUP - 1] = half_bond(beyond(True), here)
-                if group == groups - 1:
-                    below = beyond(False)
-                else:
-                    lower = slice(group * GROUP + 1, (group + 1) * GROUP + 1)
-                    below = [field[angle, part, block, lower] for part in range(2)]
-                    below.append(power[slot, lower])
-                down = half_bond(here, below)
-                first = (group + 1) * GROUP
-                drops[first : first + GROUP] = down
-                up = drops[first - 1 : first - 1 + GROUP]
-                left = [
-                    jnp.where(lane == 0, shifts[1 - slot, part, group], shifts[slot, part, group])
-                    for part in range(2)
-                ]
-                bond = half_bond(left + [power_of(*left)], here)
-                bonds[slot, group] = bond
-                partial[slot, group] = up - down + bond
-
-        def finish(block, slot):
-            behind = pl.ds(pl.multiple_of(jnp.maximum(block - 1, 0) * LANES, LANES), LANES)
-            for group in range(groups):
-                after = pltpu.roll(bonds[slot, group], LANES - 1, 1)
-                first = angle * strip + group * GROUP
-                source[first : first + GROUP, behind] = partial[1 - slot, group] - jnp.where(
-                    lane == LANES - 1, after, afters[group]
-                )
-                afters[group] = after
-
-        def step(pair, _):
-            block = 2 * pair
-            finish(block - 1, 1)
-            combine(block, 0)
-            prepare(block + 1, 1)
-            finish(block, 0)
-            combine(block + 1, 1)
-            prepare(jnp.minimum(block + 2, blocks - 1), 0)
-            return 0
-
-        for group in range(groups):
-            for part in range(2):
-                shifts[1, part, group] = jnp.zeros((GROUP, LANES), f32)
-        prepare(0, 0)
-        lax.fori_loop(0, blocks // 2, step, 0)
-        finish(blocks - 1, 1)
-        for group in range(groups):
-            first = angle * strip + group * GROUP
-            source[first : first + GROUP, width - LANES :] = partial[1, group] - jnp.where(
-                lane == LANES - 1, 0.0, afters[group]
-            )
-
     half = width // 2
 
     def tile(index):
@@ -804,16 +812,23 @@
 
     factors = cosine_factors(width)
     table = (reach + 1, cap, 2, strip, side)
-    held, halo, *half_tables = pl.pallas_call(
+    held, source, *half_tables = pl.pallas_call(
         update_kernel,
         out_shape=[
             shape((angles, 2, blocks, strip, LANES), f32),
-            shape((2, angles, 2, 1, width), f32),
+            shape((rows, width), f32),
         ]
         + [shape((half, half), bf16)] * 4,
         in_specs=[smem] + [hbm] * 7,
         out_specs=[vmem] * 6,
         scratch_shapes=[
+            pltpu.VMEM((2, angles, 2, 1, width), f32),
+            pltpu.VMEM((2, strip, LANES), f32),
+            pltpu.VMEM((strip + GROUP, LANES), f32),
+            pltpu.VMEM((2, 2, strip // GROUP, GROUP, LANES), f32),
+            pltpu.VMEM((2, strip // GROUP, GROUP, LANES), f32),
+            pltpu.VMEM((2, strip // GROUP, GROUP, LANES), f32),
+            pltpu.VMEM((strip // GROUP, GROUP, LANES), f32),
             pltpu.SMEM((reach + 1, cap, 3), jnp.int32),
             pltpu.SMEM((1,), jnp.int32),
             pltpu.VMEM(probe.shape, f32),
@@ -865,18 +880,11 @@
             shape((2, plane) + lines, f32),
             shape((rows, half), f32),
         ],
-        in_specs=[vmem] * 8,
+        in_specs=[vmem] * 7,
         out_specs=[vmem] * 4,
-        scratch_shapes=[pltpu.VMEM((rows, width), f32)]
-        + [pltpu.VMEM((rows, half), bf16)] * 4
+        scratch_shapes=[pltpu.VMEM((rows, half), bf16)] * 4
         + [
             pltpu.VMEM((2, blocks // 2, rows, LANES), f32),
-            pltpu.VMEM((2, strip, LANES), f32),
-            pltpu.VMEM((strip + GROUP, LANES), f32),
-            pltpu.VMEM((2, 2, strip // GROUP, GROUP, LANES), f32),
-            pltpu.VMEM((2, strip // GROUP, GROUP, LANES), f32),
-            pltpu.VMEM((2, strip // GROUP, GROUP, LANES), f32),
-            pltpu.VMEM((strip // GROUP, GROUP, LANES), f32),
             pltpu.VMEM((blocks // 2, rows, LANES), f32),
             pltpu.VMEM((blocks // 2, 2 * angles, GROUP, LANES), f32),
             pltpu.VMEM((2, plane) + lines, f32),
@@ -894,7 +902,7 @@
         compiler_params=params(collective_id=1, has_side_effects=True),
         cost_estimate=cost(15),
         name="forward",
-    )(held, halo, *half_tables, decays, joins)
+    )(source, *half_tables, decays, joins)
     updated, phase_map = pl.pallas_call(
         inverse_kernel,
         out_shape=[shape(object_field.shape, f32), shape((angles, strip, width), f32)],

time: 51 us -> 50.2 us (0.984)
  Pallas kernels: 49.3 us -> 48.5 us
    pallas_call x1, Pallas kernels: 23.6 us -> 22.7 us  [body(): pl.pallas_call(forward_kernel, out_shape=[shape((blocks // 2, rows, LANES...]
where the time goes in v6:
time: 50.2 us; the launch traced here: 50 us
  Pallas kernels  48.5 us (97%)
  between operations  1.49 us (3%)
    pallas_call x1, Pallas kernels, body(): pl.pallas_call(forward_kernel, out_shape=[shape((blocks // 2, rows, LANES...  22.7 us
    pallas_call x1, Pallas kernels, body(): pl.pallas_call(update_kernel, out_shape=[shape((angles, 2, blocks, strip,...  22 us
    pallas_call x1, Pallas kernels, body(): pl.pallas_call(inverse_kernel, out_shape=[shape(object_field.shape, f32),...  3.88 us

profile of v6, /device:TPU:0, one launch (start us, length us, event | category | flops | bytes accessed | tf_op | source)
XLA Modules:
  0.0 50.0 jit_solution(13296429362603844202)
XLA Ops:
  1.3 0.0 copy-start
  1.3 0.0 copy-start.1
  1.3 22.0 %update.1 = (f32[2,2,16,128,128]{4,3,2,1,0:T(8,128)S(1)}, f32[256,2048]{1,0:T(8,128)S(1)}, bf16[1024,1024]{1,0:T(8,128)(2,1)S(1)}, bf16[1024,1024]{1,0:T(8,128)(...) custom-call(s32[1]{0:T(128)S(6)} %copy.12.frame_count, s32[2,3]{1,0:T(2,128)} %frame_table.1, ...), custom_call_target="tpu_custom_call" | custom-call | bytes 60000000 | tf_op jit(solution)/shard_map/update/pallas_call | solution.py:815
  23.3 0.0 copy-done
  23.3 0.0 copy-done.1
  23.3 22.7 %forward.1 = (f32[8,256,128]{2,1,0:T(8,128)S(1)}, f32[8,4,8,128]{3,2,1,0:T(8,128)S(1)}, f32[2,4,2,4,128]{4,3,2,1,0:T(4,128)S(1)}, f32[256,1024]{1,0:T(8,128)S(1)}) custom-call(f32[256,2048]{1,0:T(8,128)S(1)} %get-tuple-element.13.source, bf16[1024,1024]{1,0:T(8,128)(2,1)S(1)} %get-tuple-element.14.even_hi, bf16[1024,1024]{1,0:T(8,128)(2,1)S(1)} %get-tuple-element.15.even_lo, ...), custom_call_target="tpu_custom_call" | custom-call | bytes 45000000 | tf_op jit(solution)/shard_map/forward/pallas_call | solution.py:875
  46.0 3.9 %inverse.1 = (f32[2,2,128,2048]{3,2,1,0:T(8,128)}, f32[2,128,2048]{2,1,0:T(8,128)}) custom-call(f32[2,2,16,128,128]{4,3,2,1,0:T(8,128)S(1)} %get-tuple-element.12.field, f32[8,256,128]{2,1,0:T(8,128)S(1)} %get-tuple-element.18.value, f32[8,4,8,128]{3,2,1,0:T(8,128)S(1)} %get-tuple-element.19.carries, f32[2,4,2,4,128]{4,3,2,1,0:T(4,128)S(1)} %get-tuple-element.20.incoming, ...), custom_call_target="tpu_custom_call" | custom-call | bytes 18000000 | tf_op jit(solution)/shard_map/inverse/pallas_call | solution.py:906
Async XLA Ops:
  1.3 22.0 %copy-start = (f32[56,2048]{1,0:T(8,128)S(1)}, f32[56,2048]{1,0:T(8,128)}, u32[]{:S(2)}) copy-start(f32[56,2048]{1,0:T(8,128)} %constant.14.clone.decays) | copy-start | bytes 1376260
  1.3 22.0 %copy-start.1 = (f32[2,4,5,2,128]{4,3,2,1,0:T(2,128)S(1)}, f32[2,4,5,2,128]{4,3,2,1,0:T(2,128)}, u32[]{:S(2)}) copy-start(f32[2,4,5,2,128]{4,3,2,1,0:T(2,128)} %constant.10.clone.joins) | copy-start | bytes 122884

commit v7 on v6

--- a/solution.py
+++ b/solution.py
@@ -46,12 +46,17 @@
     )
 
 
+def frequencies(grid_side):
+    quarter = np.arange(grid_side // 4)
+    even = np.concatenate([4 * quarter, 4 * quarter + 2])
+    return even, 2 * np.arange(grid_side // 2) + 1
+
+
 def cosine_factors(grid_side):
     half = grid_side // 2
     step = 32
     out = []
-    for odd in (0, 1):
-        freqs = 2 * np.arange(half) + odd
+    for freqs in frequencies(grid_side):
         scale = np.where(freqs == 0, math.sqrt(1.0 / grid_side), math.sqrt(2.0 / grid_side))
         coarse = (2 * step * np.arange(half // step)[:, None] * freqs[None, :]) % (4 * grid_side)
         fine = ((2 * np.arange(step)[:, None] + 1) * freqs[None, :]) % (4 * grid_side)
@@ -71,7 +76,7 @@
 
 def decay_tables(grid_side, strip_rows, plane):
     half = grid_side // 2
-    freqs = np.concatenate([2 * np.arange(half), 2 * np.arange(half) + 1]).astype(np.float64)
+    freqs = np.concatenate(frequencies(grid_side)).astype(np.float64)
     shift = screen_term + 2.0 - 2.0 * np.cos(freqs * math.pi / grid_side)
     rate = 2.0 * np.arcsinh(np.sqrt(shift) / 2.0)
     gain = 2.0 / (2.0 * np.sinh(rate))
@@ -305,8 +310,7 @@
         half_re, half_im = left(wave_re, wave_im, 1)
         spec_re, spec_im = right(half_re.astype(bf16), half_im.astype(bf16), 1)
         amplitude = jnp.sqrt(spec_re * spec_re + spec_im * spec_im)
-        if s == 0:
-            arrive(moves)
+        arrive(moves[s : s + 1])
         factor = moved[s].astype(f32) / jnp.maximum(amplitude, magnitude_floor) - 1.0
         back_re, back_im = left(
             (spec_re * factor).astype(bf16), (spec_im * factor).astype(bf16), -1
@@ -602,25 +606,31 @@
     def tile(index):
         return slice(index * TILE, (index + 1) * TILE)
 
-    def fold(index):
-        where = tile(index)
-        near = source[:, where]
+    tiles = half // TILE
+    sums_even = []
+    for index in range(tiles):
+        near = source[:, tile(index)]
         far = mirror(source[:, tile(width // TILE - 1 - index)])
-        split_store(near + far, xeh, xel, where)
-        split_store(near - far, xoh, xol, where)
-
-    for index in range(half // TILE):
-        fold(index)
+        sums_even.append(near + far)
+        split_store(near - far, xoh, xol, tile(index))
+    for index in range(tiles // 2):
+        near, far = sums_even[index], mirror(sums_even[tiles - 1 - index])
+        split_store(near + far, xeh, xel, tile(index))
+        split_store(near - far, xeh, xel, tile(index + tiles // 2))
+
     def transform(part, index):
         high, low, table_hi, table_lo = (
             (xeh, xel, even_hi, even_lo),
             (xoh, xol, odd_hi, odd_lo),
         )[part]
         where = tile(index)
+        depth = half if part else half // 2
+        start = 0 if part or index < tiles // 2 else depth
+        inner, outer = slice(start, start + depth), slice(0, depth)
         value = (
-            jnp.dot(high[...], table_hi[:, where], preferred_element_type=f32)
-            + jnp.dot(low[...], table_hi[:, where], preferred_element_type=f32)
-            + jnp.dot(high[...], table_lo[:, where], preferred_element_type=f32)
+            jnp.dot(high[:, inner], table_hi[outer, where], preferred_element_type=f32)
+            + jnp.dot(low[:, inner], table_hi[outer, where], preferred_element_type=f32)
+            + jnp.dot(high[:, inner], table_lo[outer, where], preferred_element_type=f32)
         )
         for column in range(TILE // LANES):
             block = index * TILE // LANES + column
@@ -672,7 +682,6 @@
 
         lax.fori_loop(0, blocks // 2, run, 0, unroll=2)
 
-    tiles = half // TILE
     for index in range(tiles):
         transform(0, index)
     scan(0)
@@ -687,10 +696,16 @@
     answer(0)
     learn(0)
     enter(0, out, carries, incoming, decays, xeh, xel)
-    for index in range(tiles):
-        if index == 1 or tiles == 1:
+    for index in range(tiles // 2):
+        where = tile(index)
+        whole, crossed = [
+            restored(xeh, xel, even_hi, even_lo, where, slice(first, first + half // 2))
+            for first in (0, half // 2)
+        ]
+        if index == 0:
             answer(1)
-        evens[:, tile(index)] = restored(xeh, xel, even_hi, even_lo, tile(index))
+        evens[:, where] = whole + crossed
+        evens[:, tile(tiles - 1 - index)] = mirror(whole - crossed)
     learn(1)
     for part in range(2):
         for other in beside:
@@ -746,12 +761,12 @@
     lax.fori_loop(0, half // LANES, run, 0)
 
 
-def restored(high, low, table_hi, table_lo, where):
+def restored(high, low, table_hi, table_lo, where, depth=slice(None)):
     last = (((1,), (1,)), ((), ()))
     return (
-        lax.dot_general(high[...], table_hi[where], last, preferred_element_type=f32)
-        + lax.dot_general(low[...], table_hi[where], last, preferred_element_type=f32)
-        + lax.dot_general(high[...], table_lo[where], last, preferred_element_type=f32)
+        lax.dot_general(high[:, depth], table_hi[where, depth], last, preferred_element_type=f32)
+        + lax.dot_general(low[:, depth], table_hi[where, depth], last, preferred_element_type=f32)
+        + lax.dot_general(high[:, depth], table_lo[where, depth], last, preferred_element_type=f32)
     )
 
 

time: 50.2 us -> 49.2 us (0.980)
  Pallas kernels: 48.5 us -> 47.6 us
    pallas_call x1, Pallas kernels: 22.7 us -> 21.7 us  [body(): pl.pallas_call(forward_kernel, out_shape=[shape((blocks // 2, rows, LANES...]
where the time goes in v7:
time: 49.2 us; the launch traced here: 49.1 us
  Pallas kernels  47.6 us (97%)
  between operations  1.49 us (3%)
    pallas_call x1, Pallas kernels, body(): pl.pallas_call(update_kernel, out_shape=[shape((angles, 2, blocks, strip,...  21.9 us
    pallas_call x1, Pallas kernels, body(): pl.pallas_call(forward_kernel, out_shape=[shape((blocks // 2, rows, LANES...  21.7 us
    pallas_call x1, Pallas kernels, body(): pl.pallas_call(inverse_kernel, out_shape=[shape(object_field.shape, f32),...  3.88 us

profile of v7, /device:TPU:0, one launch (start us, length us, event | category | flops | bytes accessed | tf_op | source)
XLA Modules:
  0.0 49.1 jit_solution(7934157609476017743)
XLA Ops:
  1.3 0.0 copy-start
  1.3 0.0 copy-start.1
  1.3 21.9 %update.1 = (f32[2,2,16,128,128]{4,3,2,1,0:T(8,128)S(1)}, f32[256,2048]{1,0:T(8,128)S(1)}, bf16[1024,1024]{1,0:T(8,128)(2,1)S(1)}, bf16[1024,1024]{1,0:T(8,128)(...) custom-call(s32[1]{0:T(128)S(6)} %copy.12.frame_count, s32[2,3]{1,0:T(2,128)} %frame_table.1, ...), custom_call_target="tpu_custom_call" | custom-call | bytes 60000000 | tf_op jit(solution)/shard_map/update/pallas_call | solution.py:830
  23.3 0.0 copy-done
  23.3 0.0 copy-done.1
  23.3 21.7 %forward.1 = (f32[8,256,128]{2,1,0:T(8,128)S(1)}, f32[8,4,8,128]{3,2,1,0:T(8,128)S(1)}, f32[2,4,2,4,128]{4,3,2,1,0:T(4,128)S(1)}, f32[256,1024]{1,0:T(8,128)S(1)}) custom-call(f32[256,2048]{1,0:T(8,128)S(1)} %get-tuple-element.13.source, bf16[1024,1024]{1,0:T(8,128)(2,1)S(1)} %get-tuple-element.14.even_hi, bf16[1024,1024]{1,0:T(8,128)(2,1)S(1)} %get-tuple-element.15.even_lo, ...), custom_call_target="tpu_custom_call" | custom-call | bytes 45000000 | tf_op jit(solution)/shard_map/forward/pallas_call | solution.py:890
  45.0 3.9 %inverse.1 = (f32[2,2,128,2048]{3,2,1,0:T(8,128)}, f32[2,128,2048]{2,1,0:T(8,128)}) custom-call(f32[2,2,16,128,128]{4,3,2,1,0:T(8,128)S(1)} %get-tuple-element.12.field, f32[8,256,128]{2,1,0:T(8,128)S(1)} %get-tuple-element.18.value, f32[8,4,8,128]{3,2,1,0:T(8,128)S(1)} %get-tuple-element.19.carries, f32[2,4,2,4,128]{4,3,2,1,0:T(4,128)S(1)} %get-tuple-element.20.incoming, ...), custom_call_target="tpu_custom_call" | custom-call | bytes 18000000 | tf_op jit(solution)/shard_map/inverse/pallas_call | solution.py:921
Async XLA Ops:
  1.3 22.0 %copy-start = (f32[56,2048]{1,0:T(8,128)S(1)}, f32[56,2048]{1,0:T(8,128)}, u32[]{:S(2)}) copy-start(f32[56,2048]{1,0:T(8,128)} %constant.14.clone.decays) | copy-start | bytes 1376260
  1.3 22.0 %copy-start.1 = (f32[2,4,5,2,128]{4,3,2,1,0:T(2,128)S(1)}, f32[2,4,5,2,128]{4,3,2,1,0:T(2,128)}, u32[]{:S(2)}) copy-start(f32[2,4,5,2,128]{4,3,2,1,0:T(2,128)} %constant.10.clone.joins) | copy-start | bytes 122884

commit v8 on v7

--- a/solution.py
+++ b/solution.py
@@ -127,7 +127,7 @@
 def update_kernel(
     frame_count, frame_table, field, probe_in, measured, cos_in, sin_in, factors_in,
     held, source, even_hi, even_lo, odd_hi, odd_lo,
-    halo, power, drops, shifts, bonds, partial, afters, tables, counts, probe, cos_ref, sin_ref, factors, moved, cuts, arrived, away, landed,
+    staged, halo, power, drops, shifts, bonds, partial, afters, tables, counts, probe, cos_ref, sin_ref, factors, moved, cuts, arrived, away, landed,
     own, placed, window, edges,
     load_sems, tell_sems, count_sems, moved_sems, fetch_sems, give_sems, edge_sems,
 ):
@@ -155,12 +155,13 @@
         load(2, probe_in, probe),
         load(3, cos_in, cos_ref),
         load(4, sin_in, sin_ref),
+        load(5, measured, staged),
     ]
     strips = [
-        load(5 + block, field.at[:, :, :, block * LANES : (block + 1) * LANES], held.at[:, :, block])
+        load(6 + block, field.at[:, :, :, block * LANES : (block + 1) * LANES], held.at[:, :, block])
         for block in range(blocks)
     ]
-    for item in loads[:2] + strips + loads[2:5]:
+    for item in [loads[0], loads[5]] + strips + loads[1:5]:
         item.start()
 
     def send(source, target, sems, index, by):
@@ -192,7 +193,7 @@
     ]
     tells.append(send(frame_count, counts, count_sems, 0, middle))
     moves = [
-        send(measured.at[s], moved.at[s], moved_sems, s, middle) for s in range(cap)
+        send(staged.at[s], moved.at[s], moved_sems, s, middle) for s in range(cap)
     ]
     fetches = [
         [send(cuts.at[j, s], arrived.at[j, s], fetch_sems, s * (reach + 1) + j, middle - j) for j in others]
@@ -237,6 +238,7 @@
 
     loads[0].wait()
     start(tells)
+    loads[5].wait()
     start(moves)
     blank(tells, wipe_table)
     blank(moves, lambda s: wipe(moved, s))
@@ -695,6 +697,7 @@
     spread(1)
     answer(0)
     learn(0)
+    answer(1)
     enter(0, out, carries, incoming, decays, xeh, xel)
     for index in range(tiles // 2):
         where = tile(index)
@@ -702,8 +705,6 @@
             restored(xeh, xel, even_hi, even_lo, where, slice(first, first + half // 2))
             for first in (0, half // 2)
         ]
-        if index == 0:
-            answer(1)
         evens[:, where] = whole + crossed
         evens[:, tile(tiles - 1 - index)] = mirror(whole - crossed)
     learn(1)
@@ -837,6 +838,7 @@
         in_specs=[smem] + [hbm] * 7,
         out_specs=[vmem] * 6,
         scratch_shapes=[
+            pltpu.VMEM(measured.shape, bf16),
             pltpu.VMEM((2, angles, 2, 1, width), f32),
             pltpu.VMEM((2, strip, LANES), f32),
             pltpu.VMEM((strip + GROUP, LANES), f32),
@@ -859,7 +861,7 @@
             pltpu.VMEM((reach + 1, cap, 2, side // LANES + 2, strip, LANES), f32),
             pltpu.VMEM(((reach + 1) * strip, side), f32),
             pltpu.VMEM((2, angles, 2, 1, width), f32),
-            pltpu.SemaphoreType.DMA((5 + blocks,)),
+            pltpu.SemaphoreType.DMA((6 + blocks,)),
             pltpu.SemaphoreType.DMA((2, reach + 1)),
             pltpu.SemaphoreType.DMA((2, 1)),
             pltpu.SemaphoreType.DMA((2, cap)),

time: 49.2 us -> 48.3 us (0.982)
  Pallas kernels: 47.6 us -> 46.7 us
    pallas_call x1, Pallas kernels: 21.7 us -> 21 us  [body(): pl.pallas_call(forward_kernel, out_shape=[shape((blocks // 2, rows, LANES...]
where the time goes in v8:
time: 48.3 us; the launch traced here: 48.2 us
  Pallas kernels  46.7 us (97%)
  between operations  1.49 us (3%)
    pallas_call x1, Pallas kernels, body(): pl.pallas_call(update_kernel, out_shape=[shape((angles, 2, blocks, strip,...  21.8 us
    pallas_call x1, Pallas kernels, body(): pl.pallas_call(forward_kernel, out_shape=[shape((blocks // 2, rows, LANES...  21 us
    pallas_call x1, Pallas kernels, body(): pl.pallas_call(inverse_kernel, out_shape=[shape(object_field.shape, f32),...  3.88 us

profile of v8, /device:TPU:0, one launch (start us, length us, event | category | flops | bytes accessed | tf_op | source)
XLA Modules:
  0.0 48.2 jit_solution(9235746722098167129)
XLA Ops:
  1.3 0.0 copy-start
  1.3 0.0 copy-start.1
  1.3 21.8 %update.1 = (f32[2,2,16,128,128]{4,3,2,1,0:T(8,128)S(1)}, f32[256,2048]{1,0:T(8,128)S(1)}, bf16[1024,1024]{1,0:T(8,128)(2,1)S(1)}, bf16[1024,1024]{1,0:T(8,128)(...) custom-call(s32[1]{0:T(128)S(6)} %copy.12.frame_count, s32[2,3]{1,0:T(2,128)} %frame_table.1, ...), custom_call_target="tpu_custom_call" | custom-call | bytes 60000000 | tf_op jit(solution)/shard_map/update/pallas_call | solution.py:831
  23.1 0.0 copy-done
  23.1 0.0 copy-done.1
  23.1 21.0 %forward.1 = (f32[8,256,128]{2,1,0:T(8,128)S(1)}, f32[8,4,8,128]{3,2,1,0:T(8,128)S(1)}, f32[2,4,2,4,128]{4,3,2,1,0:T(4,128)S(1)}, f32[256,1024]{1,0:T(8,128)S(1)}) custom-call(f32[256,2048]{1,0:T(8,128)S(1)} %get-tuple-element.13.source, bf16[1024,1024]{1,0:T(8,128)(2,1)S(1)} %get-tuple-element.14.even_hi, bf16[1024,1024]{1,0:T(8,128)(2,1)S(1)} %get-tuple-element.15.even_lo, ...), custom_call_target="tpu_custom_call" | custom-call | bytes 45000000 | tf_op jit(solution)/shard_map/forward/pallas_call | solution.py:892
  44.1 3.9 %inverse.1 = (f32[2,2,128,2048]{3,2,1,0:T(8,128)}, f32[2,128,2048]{2,1,0:T(8,128)}) custom-call(f32[2,2,16,128,128]{4,3,2,1,0:T(8,128)S(1)} %get-tuple-element.12.field, f32[8,256,128]{2,1,0:T(8,128)S(1)} %get-tuple-element.18.value, f32[8,4,8,128]{3,2,1,0:T(8,128)S(1)} %get-tuple-element.19.carries, f32[2,4,2,4,128]{4,3,2,1,0:T(4,128)S(1)} %get-tuple-element.20.incoming, ...), custom_call_target="tpu_custom_call" | custom-call | bytes 18000000 | tf_op jit(solution)/shard_map/inverse/pallas_call | solution.py:923
Async XLA Ops:
  1.3 21.8 %copy-start = (f32[56,2048]{1,0:T(8,128)S(1)}, f32[56,2048]{1,0:T(8,128)}, u32[]{:S(2)}) copy-start(f32[56,2048]{1,0:T(8,128)} %constant.14.clone.decays) | copy-start | bytes 1376260
  1.3 21.8 %copy-start.1 = (f32[2,4,5,2,128]{4,3,2,1,0:T(2,128)S(1)}, f32[2,4,5,2,128]{4,3,2,1,0:T(2,128)}, u32[]{:S(2)}) copy-start(f32[2,4,5,2,128]{4,3,2,1,0:T(2,128)} %constant.10.clone.joins) | copy-start | bytes 122884

commit v9 on v8

--- a/solution.py
+++ b/solution.py
@@ -502,7 +502,7 @@
 
 def forward_kernel(
     source, even_hi, even_lo, odd_hi, odd_lo, decays, joins,
-    solved, carried, incoming, evens,
+    solved, carried, incoming, odds,
     xeh, xel, xoh, xol, coefs,
     out, carries, ends, heard, sums, totals, told,
     up_sems, in_sems, over_sems, across_sems, down_sems, back_sems,
@@ -639,7 +639,7 @@
             coefs[part, block] = value[:, column * LANES : (column + 1) * LANES]
 
     def scan(part):
-        result, carry_ref = ((out, carries), (solved, carried))[part]
+        result, carry_ref = ((solved, carried), (out, carries))[part]
 
         def run(chunk, _):
             table = pl.ds(pl.multiple_of(part * half + chunk * LANES, LANES), LANES)
@@ -685,29 +685,23 @@
         lax.fori_loop(0, blocks // 2, run, 0, unroll=2)
 
     for index in range(tiles):
+        transform(1, index)
+    scan(1)
+    pl.semaphore_wait(barrier, plane + planes - 2)
+    gather(1)
+    for index in range(tiles):
         transform(0, index)
+    spread(1)
     scan(0)
-    pl.semaphore_wait(barrier, plane + planes - 2)
     gather(0)
+    spread(0)
+    answer(1)
+    answer(0)
+    learn(1)
+    enter(1, out, carries, incoming, decays, xoh, xol)
     for index in range(tiles):
-        transform(1, index)
-    spread(0)
-    scan(1)
-    gather(1)
-    spread(1)
-    answer(0)
+        odds[:, tile(index)] = restored(xoh, xol, odd_hi, odd_lo, tile(index))
     learn(0)
-    answer(1)
-    enter(0, out, carries, incoming, decays, xeh, xel)
-    for index in range(tiles // 2):
-        where = tile(index)
-        whole, crossed = [
-            restored(xeh, xel, even_hi, even_lo, where, slice(first, first + half // 2))
-            for first in (0, half // 2)
-        ]
-        evens[:, where] = whole + crossed
-        evens[:, tile(tiles - 1 - index)] = mirror(whole - crossed)
-    learn(1)
     for part in range(2):
         for other in beside:
             up(part, other, seat).wait_send()
@@ -772,7 +766,7 @@
 
 
 def inverse_kernel(
-    field, value, carries, incoming, evens, odd_hi, odd_lo, decays,
+    field, value, carries, incoming, odds, even_hi, even_lo, decays,
     updated, out, xh, xl, parted, sems, field_sems,
 ):
     angles, strip, width = out.shape
@@ -787,24 +781,36 @@
         )
         copy.start()
         copies.append(copy)
-    enter(1, value, carries, incoming, decays, xh, xl)
+    enter(0, value, carries, incoming, decays, xh, xl)
     tiles = [slice(first, first + TILE) for first in range(0, half, TILE)]
-    later = restored(xh, xl, odd_hi, odd_lo, tiles[0])
-    for index, where in enumerate(tiles):
-        first, odd, even = where.start, later, evens[:, where]
-        if index + 1 < len(tiles):
-            later = restored(xh, xl, odd_hi, odd_lo, tiles[index + 1])
-        near = even + odd
-        far = mirror(even - odd)
-        for item, start in ((near, first), (far, width - first - TILE)):
-            where = slice(start, start + TILE)
-            for angle in range(angles):
-                parted[angle, :, where] = item[angle * strip : (angle + 1) * strip]
-            copy = pltpu.make_async_copy(
-                parted.at[:, :, where], out.at[:, :, where], sems.at[start // TILE]
-            )
-            copy.start()
-            copies.append(copy)
+
+    def pair(index):
+        return [
+            restored(xh, xl, even_hi, even_lo, tiles[index], slice(first, first + half // 2))
+            for first in (0, half // 2)
+        ]
+
+    later = pair(0)
+    for index in range(len(tiles) // 2):
+        whole, crossed = later
+        if index + 1 < len(tiles) // 2:
+            later = pair(index + 1)
+        for place, even in (
+            (index, whole + crossed),
+            (len(tiles) - 1 - index, mirror(whole - crossed)),
+        ):
+            first, odd = tiles[place].start, odds[:, tiles[place]]
+            near = even + odd
+            far = mirror(even - odd)
+            for item, start in ((near, first), (far, width - first - TILE)):
+                where = slice(start, start + TILE)
+                for angle in range(angles):
+                    parted[angle, :, where] = item[angle * strip : (angle + 1) * strip]
+                copy = pltpu.make_async_copy(
+                    parted.at[:, :, where], out.at[:, :, where], sems.at[start // TILE]
+                )
+                copy.start()
+                copies.append(copy)
     for copy in copies:
         copy.wait()
 
@@ -889,7 +895,7 @@
 
     planes = strips // plane
     lines = (share, 2 * angles, LANES)
-    solved, carried, incoming, evens = pl.pallas_call(
+    solved, carried, incoming, odds = pl.pallas_call(
         forward_kernel,
         out_shape=[
             shape((blocks // 2, rows, LANES), f32),
@@ -935,7 +941,7 @@
         compiler_params=params(),
         cost_estimate=cost(6),
         name="inverse",
-    )(held, solved, carried, incoming, evens, *half_tables[2:], decays)
+    )(held, solved, carried, incoming, odds, *half_tables[:2], decays)
     return (updated, phase_map)
 
 

time: 48.3 us -> 48.4 us (level)
    pallas_call x1, Pallas kernels: 21 us -> 21.8 us  [body(): pl.pallas_call(forward_kernel, out_shape=[shape((blocks // 2, rows, LANES...]
    pallas_call x1, Pallas kernels: 3.88 us -> 3.17 us  [body(): pl.pallas_call(inverse_kernel, out_shape=[shape(object_field.shape, f32),...]
where the time goes in v9:
time: 48.4 us; the launch traced here: 48.2 us
  Pallas kernels  46.7 us (96%)
  between operations  1.49 us (3%)
    pallas_call x1, Pallas kernels, body(): pl.pallas_call(forward_kernel, out_shape=[shape((blocks // 2, rows, LANES...  21.8 us
    pallas_call x1, Pallas kernels, body(): pl.pallas_call(update_kernel, out_shape=[shape((angles, 2, blocks, strip,...  21.8 us
    pallas_call x1, Pallas kernels, body(): pl.pallas_call(inverse_kernel, out_shape=[shape(object_field.shape, f32),...  3.17 us

profile of v9, /device:TPU:0, one launch (start us, length us, event | category | flops | bytes accessed | tf_op | source)
XLA Modules:
  0.0 48.2 jit_solution(10503676760910936691)
XLA Ops:
  1.3 0.0 copy-start
  1.3 0.0 copy-start.1
  1.3 21.8 %update.1 = (f32[2,2,16,128,128]{4,3,2,1,0:T(8,128)S(1)}, f32[256,2048]{1,0:T(8,128)S(1)}, bf16[1024,1024]{1,0:T(8,128)(2,1)S(1)}, bf16[1024,1024]{1,0:T(8,128)(...) custom-call(s32[1]{0:T(128)S(6)} %copy.12.frame_count, s32[2,3]{1,0:T(2,128)} %frame_table.1, ...), custom_call_target="tpu_custom_call" | custom-call | bytes 60000000 | tf_op jit(solution)/shard_map/update/pallas_call | solution.py:837
  23.1 0.0 copy-done
  23.1 0.0 copy-done.1
  23.1 21.8 %forward.1 = (f32[8,256,128]{2,1,0:T(8,128)S(1)}, f32[8,4,8,128]{3,2,1,0:T(8,128)S(1)}, f32[2,4,2,4,128]{4,3,2,1,0:T(4,128)S(1)}, f32[256,1024]{1,0:T(8,128)S(1)}) custom-call(f32[256,2048]{1,0:T(8,128)S(1)} %get-tuple-element.13.source, bf16[1024,1024]{1,0:T(8,128)(2,1)S(1)} %get-tuple-element.14.even_hi, bf16[1024,1024]{1,0:T(8,128)(2,1)S(1)} %get-tuple-element.15.even_lo, ...), custom_call_target="tpu_custom_call" | custom-call | bytes 45000000 | tf_op jit(solution)/shard_map/forward/pallas_call | solution.py:898
  44.9 3.2 %inverse.1 = (f32[2,2,128,2048]{3,2,1,0:T(8,128)}, f32[2,128,2048]{2,1,0:T(8,128)}) custom-call(f32[2,2,16,128,128]{4,3,2,1,0:T(8,128)S(1)} %get-tuple-element.12.field, f32[8,256,128]{2,1,0:T(8,128)S(1)} %get-tuple-element.18.value, f32[8,4,8,128]{3,2,1,0:T(8,128)S(1)} %get-tuple-element.19.carries, f32[2,4,2,4,128]{4,3,2,1,0:T(4,128)S(1)} %get-tuple-element.20.incoming, ...), custom_call_target="tpu_custom_call" | custom-call | bytes 18000000 | tf_op jit(solution)/shard_map/inverse/pallas_call | solution.py:929
Async XLA Ops:
  1.3 21.8 %copy-start = (f32[56,2048]{1,0:T(8,128)S(1)}, f32[56,2048]{1,0:T(8,128)}, u32[]{:S(2)}) copy-start(f32[56,2048]{1,0:T(8,128)} %constant.14.clone.decays) | copy-start | bytes 1376260
  1.3 21.8 %copy-start.1 = (f32[2,4,5,2,128]{4,3,2,1,0:T(2,128)S(1)}, f32[2,4,5,2,128]{4,3,2,1,0:T(2,128)}, u32[]{:S(2)}) copy-start(f32[2,4,5,2,128]{4,3,2,1,0:T(2,128)} %constant.10.clone.joins) | copy-start | bytes 122884

commit v10 on v9

--- a/solution.py
+++ b/solution.py
@@ -696,9 +696,9 @@
     gather(0)
     spread(0)
     answer(1)
-    answer(0)
     learn(1)
     enter(1, out, carries, incoming, decays, xoh, xol)
+    answer(0)
     for index in range(tiles):
         odds[:, tile(index)] = restored(xoh, xol, odd_hi, odd_lo, tile(index))
     learn(0)

time: 48.4 us -> 48.4 us (level)
  no operation moved by 1% of the time
where the time goes in v10:
time: 48.4 us; the launch traced here: 48.3 us
  Pallas kernels  46.8 us (97%)
  between operations  1.49 us (3%)
    pallas_call x1, Pallas kernels, body(): pl.pallas_call(forward_kernel, out_shape=[shape((blocks // 2, rows, LANES...  21.8 us
    pallas_call x1, Pallas kernels, body(): pl.pallas_call(update_kernel, out_shape=[shape((angles, 2, blocks, strip,...  21.8 us
    pallas_call x1, Pallas kernels, body(): pl.pallas_call(inverse_kernel, out_shape=[shape(object_field.shape, f32),...  3.17 us

profile of v10, /device:TPU:0, one launch (start us, length us, event | category | flops | bytes accessed | tf_op | source)
XLA Modules:
  0.0 48.3 jit_solution(12125131467064000860)
XLA Ops:
  1.3 0.0 copy-start
  1.3 0.0 copy-start.1
  1.3 21.8 %update.1 = (f32[2,2,16,128,128]{4,3,2,1,0:T(8,128)S(1)}, f32[256,2048]{1,0:T(8,128)S(1)}, bf16[1024,1024]{1,0:T(8,128)(2,1)S(1)}, bf16[1024,1024]{1,0:T(8,128)(...) custom-call(s32[1]{0:T(128)S(6)} %copy.12.frame_count, s32[2,3]{1,0:T(2,128)} %frame_table.1, ...), custom_call_target="tpu_custom_call" | custom-call | bytes 60000000 | tf_op jit(solution)/shard_map/update/pallas_call | solution.py:837
  23.1 0.0 copy-done
  23.1 0.0 copy-done.1
  23.1 21.8 %forward.1 = (f32[8,256,128]{2,1,0:T(8,128)S(1)}, f32[8,4,8,128]{3,2,1,0:T(8,128)S(1)}, f32[2,4,2,4,128]{4,3,2,1,0:T(4,128)S(1)}, f32[256,1024]{1,0:T(8,128)S(1)}) custom-call(f32[256,2048]{1,0:T(8,128)S(1)} %get-tuple-element.13.source, bf16[1024,1024]{1,0:T(8,128)(2,1)S(1)} %get-tuple-element.14.even_hi, bf16[1024,1024]{1,0:T(8,128)(2,1)S(1)} %get-tuple-element.15.even_lo, ...), custom_call_target="tpu_custom_call" | custom-call | bytes 45000000 | tf_op jit(solution)/shard_map/forward/pallas_call | solution.py:898
  44.9 3.2 %inverse.1 = (f32[2,2,128,2048]{3,2,1,0:T(8,128)}, f32[2,128,2048]{2,1,0:T(8,128)}) custom-call(f32[2,2,16,128,128]{4,3,2,1,0:T(8,128)S(1)} %get-tuple-element.12.field, f32[8,256,128]{2,1,0:T(8,128)S(1)} %get-tuple-element.18.value, f32[8,4,8,128]{3,2,1,0:T(8,128)S(1)} %get-tuple-element.19.carries, f32[2,4,2,4,128]{4,3,2,1,0:T(4,128)S(1)} %get-tuple-element.20.incoming, ...), custom_call_target="tpu_custom_call" | custom-call | bytes 18000000 | tf_op jit(solution)/shard_map/inverse/pallas_call | solution.py:929
Async XLA Ops:
  1.3 21.8 %copy-start = (f32[56,2048]{1,0:T(8,128)S(1)}, f32[56,2048]{1,0:T(8,128)}, u32[]{:S(2)}) copy-start(f32[56,2048]{1,0:T(8,128)} %constant.14.clone.decays) | copy-start | bytes 1376260
  1.3 21.8 %copy-start.1 = (f32[2,4,5,2,128]{4,3,2,1,0:T(2,128)S(1)}, f32[2,4,5,2,128]{4,3,2,1,0:T(2,128)}, u32[]{:S(2)}) copy-start(f32[2,4,5,2,128]{4,3,2,1,0:T(2,128)} %constant.10.clone.joins) | copy-start | bytes 122884

commit v11 on v8

--- a/solution.py
+++ b/solution.py
@@ -696,8 +696,8 @@
     gather(1)
     spread(1)
     answer(0)
+    answer(1)
     learn(0)
-    answer(1)
     enter(0, out, carries, incoming, decays, xeh, xel)
     for index in range(tiles // 2):
         where = tile(index)

time: 48.3 us -> 48.3 us (level)
  no operation moved by 1% of the time
where the time goes in v11:
time: 48.3 us; the launch traced here: 48.2 us
  Pallas kernels  46.7 us (97%)
  between operations  1.49 us (3%)
    pallas_call x1, Pallas kernels, body(): pl.pallas_call(update_kernel, out_shape=[shape((angles, 2, blocks, strip,...  21.8 us
    pallas_call x1, Pallas kernels, body(): pl.pallas_call(forward_kernel, out_shape=[shape((blocks // 2, rows, LANES...  21 us
    pallas_call x1, Pallas kernels, body(): pl.pallas_call(inverse_kernel, out_shape=[shape(object_field.shape, f32),...  3.88 us

profile of v11, /device:TPU:0, one launch (start us, length us, event | category | flops | bytes accessed | tf_op | source)
XLA Modules:
  0.0 48.2 jit_solution(12679590719720071021)
XLA Ops:
  1.3 0.0 copy-start
  1.3 0.0 copy-start.1
  1.3 21.8 %update.1 = (f32[2,2,16,128,128]{4,3,2,1,0:T(8,128)S(1)}, f32[256,2048]{1,0:T(8,128)S(1)}, bf16[1024,1024]{1,0:T(8,128)(2,1)S(1)}, bf16[1024,1024]{1,0:T(8,128)(...) custom-call(s32[1]{0:T(128)S(6)} %copy.12.frame_count, s32[2,3]{1,0:T(2,128)} %frame_table.1, ...), custom_call_target="tpu_custom_call" | custom-call | bytes 60000000 | tf_op jit(solution)/shard_map/update/pallas_call | solution.py:831
  23.1 0.0 copy-done
  23.1 0.0 copy-done.1
  23.1 21.0 %forward.1 = (f32[8,256,128]{2,1,0:T(8,128)S(1)}, f32[8,4,8,128]{3,2,1,0:T(8,128)S(1)}, f32[2,4,2,4,128]{4,3,2,1,0:T(4,128)S(1)}, f32[256,1024]{1,0:T(8,128)S(1)}) custom-call(f32[256,2048]{1,0:T(8,128)S(1)} %get-tuple-element.13.source, bf16[1024,1024]{1,0:T(8,128)(2,1)S(1)} %get-tuple-element.14.even_hi, bf16[1024,1024]{1,0:T(8,128)(2,1)S(1)} %get-tuple-element.15.even_lo, ...), custom_call_target="tpu_custom_call" | custom-call | bytes 45000000 | tf_op jit(solution)/shard_map/forward/pallas_call | solution.py:892
  44.1 3.9 %inverse.1 = (f32[2,2,128,2048]{3,2,1,0:T(8,128)}, f32[2,128,2048]{2,1,0:T(8,128)}) custom-call(f32[2,2,16,128,128]{4,3,2,1,0:T(8,128)S(1)} %get-tuple-element.12.field, f32[8,256,128]{2,1,0:T(8,128)S(1)} %get-tuple-element.18.value, f32[8,4,8,128]{3,2,1,0:T(8,128)S(1)} %get-tuple-element.19.carries, f32[2,4,2,4,128]{4,3,2,1,0:T(4,128)S(1)} %get-tuple-element.20.incoming, ...), custom_call_target="tpu_custom_call" | custom-call | bytes 18000000 | tf_op jit(solution)/shard_map/inverse/pallas_call | solution.py:923
Async XLA Ops:
  1.3 21.8 %copy-start = (f32[56,2048]{1,0:T(8,128)S(1)}, f32[56,2048]{1,0:T(8,128)}, u32[]{:S(2)}) copy-start(f32[56,2048]{1,0:T(8,128)} %constant.14.clone.decays) | copy-start | bytes 1376260
  1.3 21.8 %copy-start.1 = (f32[2,4,5,2,128]{4,3,2,1,0:T(2,128)S(1)}, f32[2,4,5,2,128]{4,3,2,1,0:T(2,128)}, u32[]{:S(2)}) copy-start(f32[2,4,5,2,128]{4,3,2,1,0:T(2,128)} %constant.10.clone.joins) | copy-start | bytes 122884
